TPU v7x, 512 devices: a whole 4x8x8 slice. The times are simulated.
512 devices in a mesh: comp: 2 (over z_lo), lat: 16 (over y, core), lon: 16 (over x, z_hi).
Axes of the slice: x: 4, y: 8, z: 8 (z_hi: 4, z_lo: 2; z = z_hi * 2 + z_lo), core: 2. Of those that a mesh axis runs over, the one named last changes fastest.
Arguments:
- state: float32 [2, 12, 256, 2048], P('comp', None, 'lat', 'lon'), may hold values from -6 to 6
- prev_surface: float32 [2, 256, 2048], P(None, 'lat', 'lon'), may hold values from -6 to 6
- mixing: float32 [2, 11, 256, 2048], P('comp', None, 'lat', 'lon'), may hold values from 0.1 to 3
- velocity: float32 [2, 2, 256, 2048], P('comp', None, 'lat', 'lon'), may hold values from -0.3 to 0.3
- coupling: float32 [2, 256, 2048], P('comp', 'lat', 'lon'), may hold values from 0.1 to 1
- sea_mask: int32 [2, 256, 2048], P('comp', 'lat', 'lon'), may hold values 0 or 1
- interp_index: int32 [2, 4, 256, 2048], P('comp', None, 'lat', 'lon'), may hold values from 0 to 2047
- interp_weight: float32 [2, 4, 256, 2048], P('comp', None, 'lat', 'lon'), may hold values from 0.05 to 0.45
Outputs:
- new_state: float32 [2, 12, 256, 2048], P('comp', None, 'lat', 'lon')
- surface_series: float32 [2, 2, 256, 2048], P('comp', None, 'lat', 'lon')
Inputs may be any that keep to these rules, and one draw needn't show every extreme that they name: `interp_index`: A tile index, r * 128 + c, of a cell in the same latitude-longitude tile.
All inputs are finite; a program needn't handle non-finite values. No bound on the sum of `sea_mask` on one device may be relied on, other than what follows from the above.
Results may differ from a plain program's by a relative error of at most 0.0001.
Values sent between devices are 32-bit elements; how exact they have to be, the bound alone decides.
No kernel may reach another device: no remote copies, remote signals or barrier semaphores. Data moves between devices by JAX's collectives and lax.ppermute only.
A program may use at most 64 MiB of HBM per device.

v0:
```python
import jax
import jax.numpy as jnp
from jax import lax
from jax.sharding import PartitionSpec as P

NSTEP = 2


smoothing = 0.15


def extended(shard, sides, width, wrap):
    for axis, dim in sides:
        size, length = (lax.axis_size(axis), shard.shape[dim])
        up = [(i, (i + 1) % size) for i in range(size if wrap else size - 1)]
        down = [(j, i) for i, j in up]
        last = lax.slice_in_dim(shard, length - width, length, axis=dim)
        initial = lax.slice_in_dim(shard, 0, width, axis=dim)
        before = lax.ppermute(last, axis, up)
        after = lax.ppermute(initial, axis, down)
        shard = jnp.concatenate([before, shard, after], axis=dim)
    return shard


def passed_along(value, axis, steps):
    count = lax.axis_size(axis)
    initial, last = (max(0, -steps), min(count, count - steps))
    return lax.ppermute(value, axis, [(source, source + steps) for source in range(initial, last)])


def stencil(field, lat_padded, lon_padded, east_speed, north_speed):
    lat_slope = (
        lat_padded[:, 0:-4]
        - 8.0 * lat_padded[:, 1:-3]
        + 8.0 * lat_padded[:, 3:-1]
        - lat_padded[:, 4:]
    ) / 12.0
    lon_slope = (
        lon_padded[:, :, 0:-4]
        - 8.0 * lon_padded[:, :, 1:-3]
        + 8.0 * lon_padded[:, :, 3:-1]
        - lon_padded[:, :, 4:]
    ) / 12.0
    lat_curve = lat_padded[:, 1:-3] + lat_padded[:, 3:-1] - 2.0 * field
    lon_curve = lon_padded[:, :, 1:-3] + lon_padded[:, :, 3:-1] - 2.0 * field
    return (
        field
        + smoothing * (lat_curve + lon_curve)
        - east_speed * lon_slope
        - north_speed * lat_slope
    )


def column_solve(rhs, mixing):
    levels = rhs.shape[0]
    nothing = jnp.zeros_like(rhs[0])
    ratios = []
    values = []
    for level in range(levels):
        lower = mixing[level - 1] if level > 0 else nothing
        upper = mixing[level] if level < levels - 1 else nothing
        pivot = 1.0 + lower + upper
        source = rhs[level]
        if level > 0:
            pivot = pivot + lower * ratios[-1]
            source = source + lower * values[-1]
        ratios.append(-upper / pivot)
        values.append(source / pivot)
    result = [values[-1]]
    for level in range(levels - 2, -1, -1):
        result.insert(0, values[level] - ratios[level] * result[0])
    return jnp.stack(result)


def regrid_local(source, index, weight):
    flat = source.reshape(-1)
    picked = jnp.take(flat, index.reshape(index.shape[0], -1), axis=0).reshape(index.shape)
    return jnp.sum(weight * picked, axis=0)


def padded_rims(field):
    lat_padded = extended(field, (("lat", 1),), 2, False)
    lon_padded = extended(field, (("lon", 2),), 2, True)
    return (lat_padded, lon_padded)


def per_device(
    state, prev_surface, mixing, velocity, coupling, sea_mask, interp_index, interp_weight
):
    is_atmosphere = lax.axis_index("comp") == 0
    field = state[0]
    column_mixing = mixing[0]
    east_speed = velocity[0, 0]
    north_speed = velocity[0, 1]
    exchange_rate = coupling[0] * sea_mask[0].astype(jnp.float32)
    index = interp_index[0]
    weight = interp_weight[0]

    def model_step(current, partner):
        lat_padded, lon_padded = padded_rims(current)
        moved = stencil(current, lat_padded, lon_padded, east_speed, north_speed)
        forcing = jnp.where(
            is_atmosphere, exchange_rate * (partner - current[0]), exchange_rate * partner
        )
        moved = moved.at[0].add(forcing)
        solved = column_solve(moved, column_mixing)
        return (solved, jnp.where(is_atmosphere, forcing, solved[0]))

    first_series = []
    for step_index in range(NSTEP):
        partner = regrid_local(prev_surface[step_index], index, weight)
        advanced, surface_now = model_step(field, partner)
        field = jnp.where(is_atmosphere, advanced, field)
        first_series.append(surface_now)
    sent = jnp.stack(first_series)
    received = passed_along(sent, "comp", 1)
    second_series = []
    for step_index in range(NSTEP):
        partner = regrid_local(received[step_index], index, weight)
        advanced, surface_now = model_step(field, partner)
        field = jnp.where(is_atmosphere, field, advanced)
        second_series.append(surface_now)
    series = jnp.where(is_atmosphere, sent, jnp.stack(second_series))
    return (field[None], series[None])


def solution(mesh):
    in_specs = (
        P("comp", None, "lat", "lon"),
        P(None, "lat", "lon"),
        P("comp", None, "lat", "lon"),
        P("comp", None, "lat", "lon"),
        P("comp", "lat", "lon"),
        P("comp", "lat", "lon"),
        P("comp", None, "lat", "lon"),
        P("comp", None, "lat", "lon"),
    )
    out_specs = (P("comp", None, "lat", "lon"), P("comp", None, "lat", "lon"))
    return jax.shard_map(
        per_device, mesh=mesh, in_specs=in_specs, out_specs=out_specs, check_vma=False
    )
```

profile of v0, /device:TPU:96, one launch (start us, length us, event | category | flops | bytes accessed | tf_op | source)
XLA Modules:
  0.0 272.5 jit_solution(2130217671073013175)
XLA Ops:
  0.6 0.8 fusion.211
  1.5 1.9 collective-permute-start
  3.4 4.9 %collective-permute-start.1 = (f32[12,2,128]{2,1,0:T(2,128)S(1)}, f32[12,2,128]{2,1,0:T(2,128)S(1)}, u32[]{:S(2)}, u32[]{:S(2)}) collective-permute-start(f32[12,2,128]{2,1,0:T(2,128)S(1)} %get-tuple-element.184), channel_id=1, source_target_pairs={{16,0},{32,16},{48,32},{64,48},{80,64},{96,80},{112,96},{128,112},... | collective-permute-start | bytes 36872 | tf_op jit(solution)/shard_map/ppermute | solution.py:20
  8.3 1.1 fusion.210
  9.3 6.1 %collective-permute-start.2 = (f32[12,16,2]{2,1,0:T(8,128)S(1)}, f32[12,16,2]{2,1,0:T(8,128)S(1)}, u32[]{:S(2)}, u32[]{:S(2)}) collective-permute-start(f32[12,16,2]{2,1,0:T(8,128)S(1)} %get-tuple-element.181), channel_id=1, source_target_pairs={{0,1},{1,2},{2,3},{3,4},{4,5},{5,6},{6,7},{7,8},{8,9},{9,10},{10,1... | collective-permute-start | bytes 4616 | tf_op jit(solution)/shard_map/ppermute | solution.py:19
  15.4 8.1 %collective-permute-start.3 = (f32[12,16,2]{2,1,0:T(8,128)S(1)}, f32[12,16,2]{2,1,0:T(8,128)S(1)}, u32[]{:S(2)}, u32[]{:S(2)}) collective-permute-start(f32[12,16,2]{2,1,0:T(8,128)S(1)} %get-tuple-element.182), channel_id=1, source_target_pairs={{1,0},{2,1},{3,2},{4,3},{5,4},{6,5},{7,6},{8,7},{9,8},{10,9},{11,1... | collective-permute-start | bytes 4616 | tf_op jit(solution)/shard_map/ppermute | solution.py:20
  23.6 45.5 %gather_fusion.1 = f32[8192]{0:T(1024)S(1)} fusion(f32[2048]{0:T(1024)S(1)} %get-tuple-element.187, s32[8192]{0:T(1024)S(1)} %broadcast_clamp_fusion), kind=kCustom, calls=%fused_computation.1.clone | custom fusion | bytes 98304 | tf_op jit(solution)/shard_map/jit(_take)/gather | solution.py:77
  69.2 45.5 %gather_fusion = f32[8192]{0:T(1024)S(1)} fusion(f32[2048]{0:T(1024)S(1)} %get-tuple-element.188, s32[8192]{0:T(1024)S(1)} %broadcast_clamp_fusion), kind=kCustom, calls=%fused_computation.clone | custom fusion | bytes 98304 | tf_op jit(solution)/shard_map/jit(_take)/gather | solution.py:77
  114.9 0.8 copy-done
  116.0 0.6 copy-done.1
  117.1 1.9 collective-permute-start.4
  119.1 4.9 %collective-permute-start.5 = (f32[12,2,128]{2,1,0:T(2,128)S(1)}, f32[12,2,128]{2,1,0:T(2,128)S(1)}, u32[]{:S(2)}, u32[]{:S(2)}) collective-permute-start(f32[12,2,128]{2,1,0:T(2,128)S(1)} %get-tuple-element.180), channel_id=1, source_target_pairs={{16,0},{32,16},{48,32},{64,48},{80,64},{96,80},{112,96},{128,112},... | collective-permute-start | bytes 36872 | tf_op jit(solution)/shard_map/ppermute | solution.py:20
  123.9 1.9 collective-permute-start.6
  125.8 8.1 %collective-permute-start.7 = (f32[12,16,2]{2,1,0:T(8,128)S(1)}, f32[12,16,2]{2,1,0:T(8,128)S(1)}, u32[]{:S(2)}, u32[]{:S(2)}) collective-permute-start(f32[12,16,2]{2,1,0:T(8,128)S(1)} %get-tuple-element.178), channel_id=1, source_target_pairs={{1,0},{2,1},{3,2},{4,3},{5,4},{6,5},{7,6},{8,7},{9,8},{10,9},{11,1... | collective-permute-start | bytes 4616 | tf_op jit(solution)/shard_map/ppermute | solution.py:20
  134.0 1.7 collective-permute-done.6
  137.0 1.9 collective-permute-start.8
  138.9 4.9 %collective-permute-start.9 = (f32[12,2,128]{2,1,0:T(2,128)S(1)}, f32[12,2,128]{2,1,0:T(2,128)S(1)}, u32[]{:S(2)}, u32[]{:S(2)}) collective-permute-start(f32[12,2,128]{2,1,0:T(2,128)S(1)} %get-tuple-element.176), channel_id=1, source_target_pairs={{16,0},{32,16},{48,32},{64,48},{80,64},{96,80},{112,96},{128,112},... | collective-permute-start | bytes 36872 | tf_op jit(solution)/shard_map/ppermute | solution.py:20
  143.7 2.7 %collective-permute-start.10 = (f32[12,16,2]{2,1,0:T(8,128)S(1)}, f32[12,16,2]{2,1,0:T(8,128)S(1)}, u32[]{:S(2)}, u32[]{:S(2)}) collective-permute-start(f32[12,16,2]{2,1,0:T(8,128)S(1)} %get-tuple-element.173), channel_id=1, source_target_pairs={{0,1},{1,2},{2,3},{3,4},{4,5},{5,6},{6,7},{7,8},{8,9},{9,10},{10,1... | collective-permute-start | bytes 4616 | tf_op jit(solution)/shard_map/ppermute | solution.py:19
  146.5 7.8 %collective-permute-start.11 = (f32[12,16,2]{2,1,0:T(8,128)S(1)}, f32[12,16,2]{2,1,0:T(8,128)S(1)}, u32[]{:S(2)}, u32[]{:S(2)}) collective-permute-start(f32[12,16,2]{2,1,0:T(8,128)S(1)} %get-tuple-element.174), channel_id=1, source_target_pairs={{1,0},{2,1},{3,2},{4,3},{5,4},{6,5},{7,6},{8,7},{9,8},{10,9},{11,1... | collective-permute-start | bytes 4616 | tf_op jit(solution)/shard_map/ppermute | solution.py:20
  154.3 1.3 collective-permute-start.12
  156.0 0.5 collective-permute-done.11
  156.8 3.2 %collective-permute-done.12 = f32[2,16,128]{2,1,0:T(8,128)S(1)} collective-permute-done((f32[2,16,128]{2,1,0:T(8,128)S(1)}, f32[2,16,128]{2,1,0:T(8,128)S(1)}, u32[]{:S(2)}, u32[]{:S(2)}) %collective-permute-start.12) | collective-permute-done | bytes 16416 | tf_op jit(solution)/shard_map/ppermute | solution.py:28
  160.0 45.5 %gather_fusion.2 = f32[8192]{0:T(1024)S(1)} fusion(f32[2048]{0:T(1024)S(1)} %get-tuple-element.185, s32[8192]{0:T(1024)S(1)} %broadcast_clamp_fusion), kind=kCustom, calls=%fused_computation.2.clone | custom fusion | bytes 98304 | tf_op jit(solution)/shard_map/jit(_take)/gather | solution.py:77
  205.5 45.5 %gather_fusion.3 = f32[8192]{0:T(1024)S(1)} fusion(f32[2048]{0:T(1024)S(1)} %get-tuple-element.186, s32[8192]{0:T(1024)S(1)} %broadcast_clamp_fusion), kind=kCustom, calls=%fused_computation.3.clone | custom fusion | bytes 98304 | tf_op jit(solution)/shard_map/jit(_take)/gather | solution.py:77
  251.5 1.9 collective-permute-start.13
  253.5 4.9 %collective-permute-start.14 = (f32[12,2,128]{2,1,0:T(2,128)S(1)}, f32[12,2,128]{2,1,0:T(2,128)S(1)}, u32[]{:S(2)}, u32[]{:S(2)}) collective-permute-start(f32[12,2,128]{2,1,0:T(2,128)S(1)} %get-tuple-element.172), channel_id=1, source_target_pairs={{16,0},{32,16},{48,32},{64,48},{80,64},{96,80},{112,96},{128,112},... | collective-permute-start | bytes 36872 | tf_op jit(solution)/shard_map/ppermute | solution.py:20
  258.4 1.9 collective-permute-start.15
  260.4 8.1 %collective-permute-start.16 = (f32[12,16,2]{2,1,0:T(8,128)S(1)}, f32[12,16,2]{2,1,0:T(8,128)S(1)}, u32[]{:S(2)}, u32[]{:S(2)}) collective-permute-start(f32[12,16,2]{2,1,0:T(8,128)S(1)} %get-tuple-element.170), channel_id=1, source_target_pairs={{1,0},{2,1},{3,2},{4,3},{5,4},{6,5},{7,6},{8,7},{9,8},{10,9},{11,1... | collective-permute-start | bytes 4616 | tf_op jit(solution)/shard_map/ppermute | solution.py:20
  268.5 1.1 collective-permute-done.15
  269.6 1.1 collective-permute-done.16
  271.2 0.6 maximum_select_fusion
  271.8 0.7 select_select_fusion
  (143 shorter events, 3.3 us)
Async XLA Ops:
  1.5 113.4 %collective-permute-start = (f32[12,2,128]{2,1,0:T(2,128)S(1)}, f32[12,2,128]{2,1,0:T(2,128)S(1)}, u32[]{:S(2)}, u32[]{:S(2)}) collective-permute-start(f32[12,2,128]{2,1,0:T(2,128)S(1)} %get-tuple-element.183), channel_id=1, source_target_pairs={{0,16},{16,32},{32,48},{48,64},{64,80},{80,96},{96,112},{112,128},... | collective-permute-start | bytes 36872 | tf_op jit(solution)/shard_map/ppermute | solution.py:19
  3.4 20.1 %copy-start.4 = (f32[2,16,128]{2,1,0:T(8,128)S(1)}, f32[2,16,128]{2,1,0:T(8,128)}, u32[]{:S(2)}) copy-start(f32[2,16,128]{2,1,0:T(8,128)} %param.19) | copy-start | bytes 49156
  3.4 111.5 %collective-permute-start.1 = (f32[12,2,128]{2,1,0:T(2,128)S(1)}, f32[12,2,128]{2,1,0:T(2,128)S(1)}, u32[]{:S(2)}, u32[]{:S(2)}) collective-permute-start(f32[12,2,128]{2,1,0:T(2,128)S(1)} %get-tuple-element.184), channel_id=1, source_target_pairs={{16,0},{32,16},{48,32},{64,48},{80,64},{96,80},{112,96},{128,112},... | collective-permute-start | bytes 36872 | tf_op jit(solution)/shard_map/ppermute | solution.py:20
  9.3 105.6 %collective-permute-start.2 = (f32[12,16,2]{2,1,0:T(8,128)S(1)}, f32[12,16,2]{2,1,0:T(8,128)S(1)}, u32[]{:S(2)}, u32[]{:S(2)}) collective-permute-start(f32[12,16,2]{2,1,0:T(8,128)S(1)} %get-tuple-element.181), channel_id=1, source_target_pairs={{0,1},{1,2},{2,3},{3,4},{4,5},{5,6},{6,7},{7,8},{8,9},{9,10},{10,1... | collective-permute-start | bytes 4616 | tf_op jit(solution)/shard_map/ppermute | solution.py:19
  15.4 8.1 %copy-start.5 = (f32[1,2,16,128]{3,2,1,0:T(8,128)S(1)}, f32[1,2,16,128]{3,2,1,0:T(8,128)}, u32[]{:S(2)}) copy-start(f32[1,2,16,128]{3,2,1,0:T(8,128)} %param.21) | copy-start | bytes 49156
  15.4 8.1 %copy-start.3 = (s32[1,4,16,128]{3,2,1,0:T(8,128)S(1)}, s32[1,4,16,128]{3,2,1,0:T(8,128)}, u32[]{:S(2)}) copy-start(s32[1,4,16,128]{3,2,1,0:T(8,128)} %param.24) | copy-start | bytes 98308
  15.4 99.4 %collective-permute-start.3 = (f32[12,16,2]{2,1,0:T(8,128)S(1)}, f32[12,16,2]{2,1,0:T(8,128)S(1)}, u32[]{:S(2)}, u32[]{:S(2)}) collective-permute-start(f32[12,16,2]{2,1,0:T(8,128)S(1)} %get-tuple-element.182), channel_id=1, source_target_pairs={{1,0},{2,1},{3,2},{4,3},{5,4},{6,5},{7,6},{8,7},{9,8},{10,9},{11,1... | collective-permute-start | bytes 4616 | tf_op jit(solution)/shard_map/ppermute | solution.py:20
  69.2 45.7 %copy-start.2 = (f32[1,4,16,128]{3,2,1,0:T(8,128)S(1)}, f32[1,4,16,128]{3,2,1,0:T(8,128)}, u32[]{:S(2)}) copy-start(f32[1,4,16,128]{3,2,1,0:T(8,128)} %param.25) | copy-start | bytes 98308
  114.8 0.9 copy-start
  115.7 0.9 copy-start.1
  115.7 0.9 copy-start.6
  115.7 0.9 copy-start.7
  117.1 19.1 %collective-permute-start.4 = (f32[12,2,128]{2,1,0:T(2,128)S(1)}, f32[12,2,128]{2,1,0:T(2,128)S(1)}, u32[]{:S(2)}, u32[]{:S(2)}) collective-permute-start(f32[12,2,128]{2,1,0:T(2,128)S(1)} %get-tuple-element.179), channel_id=1, source_target_pairs={{0,16},{16,32},{32,48},{48,64},{64,80},{80,96},{96,112},{112,128},... | collective-permute-start | bytes 36872 | tf_op jit(solution)/shard_map/ppermute | solution.py:19
  119.1 17.1 %collective-permute-start.5 = (f32[12,2,128]{2,1,0:T(2,128)S(1)}, f32[12,2,128]{2,1,0:T(2,128)S(1)}, u32[]{:S(2)}, u32[]{:S(2)}) collective-permute-start(f32[12,2,128]{2,1,0:T(2,128)S(1)} %get-tuple-element.180), channel_id=1, source_target_pairs={{16,0},{32,16},{48,32},{64,48},{80,64},{96,80},{112,96},{128,112},... | collective-permute-start | bytes 36872 | tf_op jit(solution)/shard_map/ppermute | solution.py:20
  123.9 11.8 %collective-permute-start.6 = (f32[12,16,2]{2,1,0:T(8,128)S(1)}, f32[12,16,2]{2,1,0:T(8,128)S(1)}, u32[]{:S(2)}, u32[]{:S(2)}) collective-permute-start(f32[12,16,2]{2,1,0:T(8,128)S(1)} %get-tuple-element.177), channel_id=1, source_target_pairs={{0,1},{1,2},{2,3},{3,4},{4,5},{5,6},{6,7},{7,8},{8,9},{9,10},{10,1... | collective-permute-start | bytes 4616 | tf_op jit(solution)/shard_map/ppermute | solution.py:19
  125.8 10.3 %collective-permute-start.7 = (f32[12,16,2]{2,1,0:T(8,128)S(1)}, f32[12,16,2]{2,1,0:T(8,128)S(1)}, u32[]{:S(2)}, u32[]{:S(2)}) collective-permute-start(f32[12,16,2]{2,1,0:T(8,128)S(1)} %get-tuple-element.178), channel_id=1, source_target_pairs={{1,0},{2,1},{3,2},{4,3},{5,4},{6,5},{7,6},{8,7},{9,8},{10,9},{11,1... | collective-permute-start | bytes 4616 | tf_op jit(solution)/shard_map/ppermute | solution.py:20
  137.0 19.6 %collective-permute-start.8 = (f32[12,2,128]{2,1,0:T(2,128)S(1)}, f32[12,2,128]{2,1,0:T(2,128)S(1)}, u32[]{:S(2)}, u32[]{:S(2)}) collective-permute-start(f32[12,2,128]{2,1,0:T(2,128)S(1)} %get-tuple-element.175), channel_id=1, source_target_pairs={{0,16},{16,32},{32,48},{48,64},{64,80},{80,96},{96,112},{112,128},... | collective-permute-start | bytes 36872 | tf_op jit(solution)/shard_map/ppermute | solution.py:19
  138.9 17.6 %collective-permute-start.9 = (f32[12,2,128]{2,1,0:T(2,128)S(1)}, f32[12,2,128]{2,1,0:T(2,128)S(1)}, u32[]{:S(2)}, u32[]{:S(2)}) collective-permute-start(f32[12,2,128]{2,1,0:T(2,128)S(1)} %get-tuple-element.176), channel_id=1, source_target_pairs={{16,0},{32,16},{48,32},{64,48},{80,64},{96,80},{112,96},{128,112},... | collective-permute-start | bytes 36872 | tf_op jit(solution)/shard_map/ppermute | solution.py:20
  143.7 12.3 %collective-permute-start.10 = (f32[12,16,2]{2,1,0:T(8,128)S(1)}, f32[12,16,2]{2,1,0:T(8,128)S(1)}, u32[]{:S(2)}, u32[]{:S(2)}) collective-permute-start(f32[12,16,2]{2,1,0:T(8,128)S(1)} %get-tuple-element.173), channel_id=1, source_target_pairs={{0,1},{1,2},{2,3},{3,4},{4,5},{5,6},{6,7},{7,8},{8,9},{9,10},{10,1... | collective-permute-start | bytes 4616 | tf_op jit(solution)/shard_map/ppermute | solution.py:19
  146.5 10.0 %collective-permute-start.11 = (f32[12,16,2]{2,1,0:T(8,128)S(1)}, f32[12,16,2]{2,1,0:T(8,128)S(1)}, u32[]{:S(2)}, u32[]{:S(2)}) collective-permute-start(f32[12,16,2]{2,1,0:T(8,128)S(1)} %get-tuple-element.174), channel_id=1, source_target_pairs={{1,0},{2,1},{3,2},{4,3},{5,4},{6,5},{7,6},{8,7},{9,8},{10,9},{11,1... | collective-permute-start | bytes 4616 | tf_op jit(solution)/shard_map/ppermute | solution.py:20
  154.3 5.6 %collective-permute-start.12 = (f32[2,16,128]{2,1,0:T(8,128)S(1)}, f32[2,16,128]{2,1,0:T(8,128)S(1)}, u32[]{:S(2)}, u32[]{:S(2)}) collective-permute-start(f32[2,16,128]{2,1,0:T(8,128)S(1)} %pad_maximum_fusion.16), channel_id=1, source_target_pairs={{0,256},{1,257},{2,258},{3,259},{4,260},{5,261},{6,262},{7,263},{8... | collective-permute-start | bytes 49160 | tf_op jit(solution)/shard_map/ppermute | solution.py:28
  251.5 19.2 %collective-permute-start.13 = (f32[12,2,128]{2,1,0:T(2,128)S(1)}, f32[12,2,128]{2,1,0:T(2,128)S(1)}, u32[]{:S(2)}, u32[]{:S(2)}) collective-permute-start(f32[12,2,128]{2,1,0:T(2,128)S(1)} %get-tuple-element.171), channel_id=1, source_target_pairs={{0,16},{16,32},{32,48},{48,64},{64,80},{80,96},{96,112},{112,128},... | collective-permute-start | bytes 36872 | tf_op jit(solution)/shard_map/ppermute | solution.py:19
  253.5 17.2 %collective-permute-start.14 = (f32[12,2,128]{2,1,0:T(2,128)S(1)}, f32[12,2,128]{2,1,0:T(2,128)S(1)}, u32[]{:S(2)}, u32[]{:S(2)}) collective-permute-start(f32[12,2,128]{2,1,0:T(2,128)S(1)} %get-tuple-element.172), channel_id=1, source_target_pairs={{16,0},{32,16},{48,32},{64,48},{80,64},{96,80},{112,96},{128,112},... | collective-permute-start | bytes 36872 | tf_op jit(solution)/shard_map/ppermute | solution.py:20
  258.4 11.2 %collective-permute-start.15 = (f32[12,16,2]{2,1,0:T(8,128)S(1)}, f32[12,16,2]{2,1,0:T(8,128)S(1)}, u32[]{:S(2)}, u32[]{:S(2)}) collective-permute-start(f32[12,16,2]{2,1,0:T(8,128)S(1)} %get-tuple-element.169), channel_id=1, source_target_pairs={{0,1},{1,2},{2,3},{3,4},{4,5},{5,6},{6,7},{7,8},{8,9},{9,10},{10,1... | collective-permute-start | bytes 4616 | tf_op jit(solution)/shard_map/ppermute | solution.py:19
  260.4 10.3 %collective-permute-start.16 = (f32[12,16,2]{2,1,0:T(8,128)S(1)}, f32[12,16,2]{2,1,0:T(8,128)S(1)}, u32[]{:S(2)}, u32[]{:S(2)}) collective-permute-start(f32[12,16,2]{2,1,0:T(8,128)S(1)} %get-tuple-element.170), channel_id=1, source_target_pairs={{1,0},{2,1},{3,2},{4,3},{5,4},{6,5},{7,6},{8,7},{9,8},{10,9},{11,1... | collective-permute-start | bytes 4616 | tf_op jit(solution)/shard_map/ppermute | solution.py:20
where the time goes:
time: 273 us
  local copies, waits for them, and re-layouts  186 us (68%)
  starting transfers between devices  73.2 us (27%)
  waiting for transfers between devices  8.46 us (3%)
  other arithmetic  3.01 us (1%)
    gather x8, local copies, waits for them, and re-layouts, regrid_local(): jnp.take(flat, index.reshape(index.shape[0], -1), axis=0)  182 us
    ppermute x8, starting transfers between devices, extended(): after = lax.ppermute(initial, axis, down)  51.6 us
    ppermute x8, starting transfers between devices, extended(): before = lax.ppermute(last, axis, up)  20.4 us
  transfers between devices with their start and end apart: 17, of which 7 were waited for; matrix products, arithmetic and copies ran while one was open for 34% of the time, Pallas kernels for 0%

commit v1 on v0

v1 whole, which is shorter than its diff:
```python
import jax
import jax.numpy as jnp
from jax import lax
from jax.experimental import pallas as pl
from jax.experimental.pallas import tpu as pltpu
from jax.sharding import PartitionSpec as P

INTERPRET = False
NSTEP = 2
LEV = 12
ROWS = 16
COLS = 128
smoothing = 0.15

AT_MIX = 4 * LEV
AT_VEL = AT_MIX + 2 * (LEV - 1)
AT_RATE = AT_VEL + 4
AT_WEIGHT = 80
AT_INDEX = 88
AT_WEST = 96
AT_EAST = 100
AT_FLUX = 104
ROW_MESSAGE = AT_FLUX + ROWS
COL_MESSAGE = 2 * ROWS


def lanes(rows):
    return lax.broadcasted_iota(jnp.int32, (rows, COLS), 1)


def sublanes():
    return lax.broadcasted_iota(jnp.int32, (8, COLS), 0)


def roll(x, shift, axis):
    shift %= x.shape[axis]
    return pltpu.roll(x, shift, axis) if shift else x


def gather_cells(table, index):
    row = lax.shift_right_logical(index, 7)
    column = lax.bitwise_and(index, COLS - 1)
    total = jnp.zeros(index.shape, jnp.float32)
    for r in range(ROWS):
        source = jnp.broadcast_to(table[r : r + 1], index.shape)
        picked = jnp.take_along_axis(source, column, axis=1, mode="promise_in_bounds")
        total = jnp.where(row == r, picked, total)
    return total


def regrid_tile(table, index_ref, weight_ref):
    index = index_ref[...].reshape(4 * ROWS, COLS)
    picked = gather_cells(table, index).reshape(4, ROWS, COLS)
    return jnp.sum(picked * weight_ref[...], axis=0)


def pack_columns_kernel(
    state, prev, mix, vel, couple, mask, index, weight, msg0, msg1, flux_out
):
    is_atmosphere = lax.axis_index("comp") == 0
    odd = lax.rem(lax.axis_index("lon"), 2) == 1
    lane = lanes(ROWS)
    rate = couple[...] * mask[...].astype(jnp.float32)

    def packed(last):
        total = jnp.zeros((ROWS, COLS), jnp.float32)

        def put(total, x, at, width):
            shift = at - (COLS - width) if last else at
            return jnp.where((lane >= at) & (lane < at + width), roll(x, shift, 1), total)

        for level in range(LEV):
            total = put(total, state[level], 4 * level, 4)
        for level in range(LEV - 1):
            total = put(total, mix[level], AT_MIX + 2 * level, 2)
        for part in range(2):
            total = put(total, vel[part], AT_VEL + 2 * part, 2)
        total = put(total, rate, AT_RATE, 2)
        for j in range(4):
            total = put(total, weight[j], AT_WEIGHT + 2 * j, 2)
            total = put(total, index[j].astype(jnp.float32), AT_INDEX + 2 * j, 2)
        return total

    first, last = packed(False), packed(True)
    msg0[0:ROWS] = jnp.where(odd, first, last)
    msg1[0:ROWS] = jnp.where(odd, last, first)

    @pl.when(is_atmosphere)
    def _():
        flux = rate * (regrid_tile(prev[0], index, weight) - state[0])
        flux_out[...] = flux
        msg0[ROWS:] = flux
        msg1[ROWS:] = flux

    @pl.when(jnp.logical_not(is_atmosphere))
    def _():
        nothing = jnp.zeros((ROWS, COLS), jnp.float32)
        flux_out[...] = nothing
        msg0[ROWS:] = nothing
        msg1[ROWS:] = nothing


def column_messages(got0, got1):
    odd = lax.rem(lax.axis_index("lon"), 2)
    near = got0[1 - odd]
    far = got1[...]
    return jnp.where(odd == 1, near, far), jnp.where(odd == 1, far, near)


def pack_rows_kernel(
    state, mix, vel, couple, mask, index, weight, flux, got0, got1, msg0, msg1
):
    odd = lax.rem(lax.axis_index("lat"), 2) == 1
    west, east = column_messages(got0, got1)
    rate = couple[...] * mask[...].astype(jnp.float32)

    def put(x, at, width):
        head, tail = x[0:width], x[ROWS - width : ROWS]
        msg0[at : at + width] = jnp.where(odd, head, tail)
        msg1[at : at + width] = jnp.where(odd, tail, head)

    for level in range(LEV):
        put(state[level], 4 * level, 4)
    for level in range(LEV - 1):
        put(mix[level], AT_MIX + 2 * level, 2)
    for part in range(2):
        put(vel[part], AT_VEL + 2 * part, 2)
    put(rate, AT_RATE, 2)
    for j in range(4):
        put(weight[j], AT_WEIGHT + 2 * j, 2)
        put(index[j].astype(jnp.float32), AT_INDEX + 2 * j, 2)
    put(west[0:ROWS], AT_WEST, 4)
    put(east[0:ROWS], AT_EAST, 4)
    for at in (AT_RATE + 2, AT_RATE + 4):
        msg0[at : at + 2] = jnp.zeros((2, COLS), jnp.float32)
        msg1[at : at + 2] = jnp.zeros((2, COLS), jnp.float32)
    msg0[AT_FLUX:] = flux[...]
    msg1[AT_FLUX:] = flux[...]


def row_messages(got0, got1):
    odd = lax.rem(lax.axis_index("lat"), 2)
    near = got0[1 - odd]
    far = got1[...]
    return jnp.where(odd == 1, near, far), jnp.where(odd == 1, far, near)


def east_shift(tile, side, shift, lane):
    rows = side.shape[0]
    moved, moved_side = roll(tile, shift, 1), roll(side, shift, 1)
    cut = lane < shift if shift > 0 else lane >= COLS + shift
    own = jnp.where(cut, moved_side[: tile.shape[0]], moved)
    return own, jnp.where(cut[:rows], moved[:rows], moved_side)


def transport_weights(east, north):
    def weights(v):
        near, far = v * (8.0 / 12.0), v * (1.0 / 12.0)
        return (-far, smoothing + near, smoothing - near, far)

    return weights(east), weights(north)


def horizontal(own, side, own_weights, side_weights, own_rows):
    shifts = (2, 1, -1, -2)
    result = own[:own_rows] * (1.0 - 4.0 * smoothing)
    for shift, factor in zip(shifts, own_weights[1]):
        result = result + factor * roll(own, shift, 0)[:own_rows]
    lane = lanes(own_rows)
    side_result = None
    if side_weights is not None:
        side_result = side[:ROWS] * (1.0 - 4.0 * smoothing)
        for shift, factor in zip(shifts, side_weights[1]):
            side_result = side_result + factor * roll(side, shift, 0)[:ROWS]
    for k, shift in enumerate(shifts):
        moved, moved_side = roll(own[:own_rows], shift, 1), roll(side[:own_rows], shift, 1)
        cut = lane < shift if shift > 0 else lane >= COLS + shift
        result = result + own_weights[0][k] * jnp.where(cut, moved_side, moved)
        if side_weights is not None:
            there = jnp.where(cut[:ROWS], moved[:ROWS], moved_side[:ROWS])
            side_result = side_result + side_weights[0][k] * there
    return result, side_result


def factors(mix):
    inverses, ratios = [], []
    for level in range(LEV):
        pivot = 1.0
        if level < LEV - 1:
            pivot = pivot + mix[level]
        if level > 0:
            pivot = pivot + mix[level - 1] * (1.0 - ratios[-1])
        inverse = 1.0 / pivot
        inverses.append(inverse)
        if level < LEV - 1:
            ratios.append(mix[level] * inverse)
    return inverses, ratios


def solve(rhs, mix, inverses, ratios):
    values = []
    for level in range(LEV):
        source = rhs[level]
        if level > 0:
            source = mix[level - 1] * values[-1] if source is None else source + mix[level - 1] * values[-1]
        values.append(source * inverses[level])
    result = [None] * LEV
    result[-1] = values[-1]
    for level in range(LEV - 2, -1, -1):
        result[level] = values[level] + ratios[level] * result[level + 1]
    return result


def first_step_kernel(
    state, prev, mix, vel, couple, mask, index, weight, flux, col0, col1, row0, row1,
    before, before_side, unit, unit_side, inverse_out, fluxes,
):
    is_atmosphere = lax.axis_index("comp") == 0
    west, east = column_messages(col0, col1)
    north, south = row_messages(row0, row1)
    at_lat = lax.axis_index("lat")
    sub = sublanes()
    valid = ((sub < 4) & (at_lat < lax.axis_size("lat") - 1)) | ((sub >= 4) & (at_lat > 0))

    def rim4(level):
        block, odd = 8 * (level // 2), level % 2
        a, b = south[block : block + 8], north[block : block + 8]
        return jnp.where(sub < 4, roll(a, -4 * odd, 0), roll(b, 4 - 4 * odd, 0))

    def rim2(at):
        block, offset = 8 * (at // 8), at % 8
        a, b = south[block : block + 8], north[block : block + 8]
        a, b = roll(a, -offset, 0), roll(b, 6 - offset, 0)
        return jnp.where(sub < 2, a, jnp.where(sub >= 6, b, 0.0))

    def cornered(packed, at):
        a, b = south[AT_WEST : AT_WEST + 8], north[AT_WEST : AT_WEST + 8]
        if at == AT_WEST:
            rim = jnp.where(sub < 4, a, roll(b, 4, 0))
        else:
            rim = jnp.where(sub < 4, roll(a, 4, 0), b)
        return jnp.concatenate([packed[0:ROWS], rim], axis=0)

    west_tile, east_tile = cornered(west, AT_WEST), cornered(east, AT_EAST)
    wide = lanes(24)

    def side(at, width, rows):
        a, b = roll(east_tile[:rows], -at, 1), roll(west_tile[:rows], COLS - width - at, 1)
        lane = wide[:rows]
        return jnp.where(lane < width, a, jnp.where(lane >= COLS - width, b, 0.0))

    def extended(x, rim):
        return jnp.concatenate([x, rim], axis=0)

    own_mix = [extended(mix[level], rim2(AT_MIX + 2 * level)) for level in range(LEV - 1)]
    side_mix = [side(AT_MIX + 2 * level, 2, ROWS) for level in range(LEV - 1)]
    own_vel = [extended(vel[part], rim2(AT_VEL + 2 * part)) for part in range(2)]
    side_vel = [side(AT_VEL + 2 * part, 2, ROWS) for part in range(2)]
    own_weights, side_weights = transport_weights(*own_vel), transport_weights(*side_vel)

    moved, moved_side = [], []
    for level in range(LEV):
        own = extended(state[level], rim4(level))
        a, b = horizontal(own, side(4 * level, 4, 24), own_weights, side_weights, 24)
        moved.append(a)
        moved_side.append(b)
    inverses, ratios = factors(own_mix)
    solved = solve(moved, own_mix, inverses, ratios)
    impulse = solve([1.0] + [None] * (LEV - 1), own_mix, inverses, ratios)
    rate = couple[...] * mask[...].astype(jnp.float32)

    fluxes[0:ROWS] = flux[...]
    fluxes[ROWS : 2 * ROWS] = west[ROWS:]
    fluxes[2 * ROWS : 3 * ROWS] = east[ROWS:]
    fluxes[3 * ROWS : 4 * ROWS] = north[AT_FLUX:]
    fluxes[4 * ROWS : 5 * ROWS] = south[AT_FLUX:]

    @pl.when(is_atmosphere)
    def _():
        top = solved[0][:ROWS] + flux[...] * impulse[0][:ROWS]
        fluxes[5 * ROWS :] = rate * (regrid_tile(prev[1], index, weight) - top)

    @pl.when(jnp.logical_not(is_atmosphere))
    def _():
        fluxes[5 * ROWS :] = jnp.zeros((ROWS, COLS), jnp.float32)

    for level in range(LEV):
        for out, values in ((before, solved), (unit, impulse)):
            out[level, 0:ROWS] = values[level][:ROWS]
            out[level, ROWS:] = jnp.where(valid, values[level][ROWS:], 0.0)
        inverse_out[level] = inverses[level][:ROWS]
    inverses, ratios = factors(side_mix)
    solved = solve(moved_side, side_mix, inverses, ratios)
    impulse = solve([1.0] + [None] * (LEV - 1), side_mix, inverses, ratios)
    for level in range(LEV):
        before_side[level] = solved[level]
        unit_side[level] = impulse[level]


def second_step_kernel(
    mix, vel, couple, mask, index, weight, col0, col1, row0, row1,
    before, before_side, unit, unit_side, inverse, fluxes, new_state, series, force, force_side, force1,
):
    is_atmosphere = lax.axis_index("comp") == 0
    sub = sublanes()
    lane = lanes(ROWS)
    tables = [fluxes[0, k * ROWS : (k + 1) * ROWS] for k in range(6)]

    @pl.when(is_atmosphere)
    def _():
        force[0:ROWS] = tables[0]
        force[ROWS:] = jnp.where(sub < 4, tables[4][0:8], tables[3][8:16])
        force_side[...] = jnp.where(lane < 64, tables[2], tables[1])
        force1[...] = tables[5]

    @pl.when(jnp.logical_not(is_atmosphere))
    def _():
        rate = couple[...] * mask[...].astype(jnp.float32)
        force[0:ROWS] = rate * regrid_tile(tables[0], index, weight)
        force1[...] = rate * regrid_tile(tables[5], index, weight)
        west, east = column_messages(col0, col1)
        north, south = row_messages(row0, row1)

        def of_rows(message, table, place):
            index8 = message[AT_INDEX : AT_INDEX + 8].astype(jnp.int32)
            total = gather_cells(table, index8) * message[AT_WEIGHT : AT_WEIGHT + 8]
            total = total + roll(total, 4, 0)
            total = total + roll(total, 2, 0)
            block, offset = 8 * (AT_RATE // 8), AT_RATE % 8
            return roll(message[block : block + 8], place - offset, 0) * roll(total, place, 0)

        force[ROWS:] = jnp.where(sub < 4, of_rows(south, tables[4], 0), of_rows(north, tables[3], 6))

        def of_columns(message, table, place):
            tile = message[0:ROWS]
            total = roll(gather_cells(table, tile.astype(jnp.int32)), AT_WEIGHT - AT_INDEX, 1) * tile
            total = total + roll(total, -4, 1)
            total = total + roll(total, -2, 1)
            return roll(tile, place - AT_RATE, 1) * roll(total, place - AT_WEIGHT, 1)

        force_side[...] = jnp.where(
            lane < 64, of_columns(east, tables[2], 0), of_columns(west, tables[1], COLS - 2)
        )

    own_weights = transport_weights(vel[0], vel[1])
    f, f_side = force[...], force_side[...]
    moved = []
    for level in range(LEV):
        own = before[level] + f * unit[level]
        there = before_side[level] + f_side * unit_side[level]
        if level == 0:
            top = own[:ROWS]
        moved.append(horizontal(own, there, own_weights, None, ROWS)[0])
    moved[0] = moved[0] + force1[...]
    own_mix = [mix[level] for level in range(LEV - 1)]
    inverses = [inverse[level] for level in range(LEV)]
    ratios = [own_mix[level] * inverses[level] for level in range(LEV - 1)]
    solved = solve(moved, own_mix, inverses, ratios)
    for level in range(LEV):
        new_state[level] = solved[level]
    series[0] = jnp.where(is_atmosphere, tables[0], top)
    series[1] = jnp.where(is_atmosphere, tables[5], solved[0])


def call(kernel, name, shapes, *args, scratch=()):
    vmem = pl.BlockSpec(memory_space=pltpu.VMEM)
    return pl.pallas_call(
        kernel,
        name=name,
        out_shape=[jax.ShapeDtypeStruct(shape, jnp.float32) for shape in shapes],
        in_specs=[vmem] * len(args),
        out_specs=[vmem] * len(shapes),
        scratch_shapes=[pltpu.VMEM(shape, jnp.float32) for shape in scratch],
        compiler_params=pltpu.CompilerParams(vmem_limit_bytes=16 * 1024 * 1024),
        interpret=INTERPRET,
    )(*args)


def pairs(count, start, wrap):
    found = []
    for i in range(start, count, 2):
        j = i + 1
        if j < count or wrap:
            found += [(i, j % count), (j % count, i)]
    return found


def partners(count):
    return [[i, i + 1] for i in range(0, count, 2)]


def per_device(
    state, prev_surface, mixing, velocity, coupling, sea_mask, interp_index, interp_weight
):
    n_lat, n_lon = lax.axis_size("lat"), lax.axis_size("lon")
    state, mix, vel, couple, mask = state[0], mixing[0], velocity[0], coupling[0], sea_mask[0]
    index, weight = interp_index[0], interp_weight[0]
    tile = (ROWS, COLS)
    column_shape = (COL_MESSAGE, COLS)
    to_near, to_far, flux = call(
        pack_columns_kernel, "pack_columns", [column_shape, column_shape, tile],
        state, prev_surface, mix, vel, couple, mask, index, weight,
    )
    col1 = lax.ppermute(to_far, "lon", pairs(n_lon, 1, True))
    col0 = lax.all_gather(to_near, "lon", axis_index_groups=partners(n_lon))
    row_shape = (ROW_MESSAGE, COLS)
    to_near, to_far = call(
        pack_rows_kernel, "pack_rows", [row_shape, row_shape],
        state, mix, vel, couple, mask, index, weight, flux, col0, col1,
    )
    row1 = lax.ppermute(to_far, "lat", pairs(n_lat, 1, False))
    row0 = lax.all_gather(to_near, "lat", axis_index_groups=partners(n_lat))
    wide, narrow = (LEV, 24, COLS), (LEV, ROWS, COLS)
    *parts, fluxes = call(
        first_step_kernel, "first_step",
        [wide, narrow, wide, narrow, narrow, (6 * ROWS, COLS)],
        state, prev_surface, mix, vel, couple, mask, index, weight, flux, col0, col1, row0, row1,
    )
    fluxes = lax.all_gather(fluxes, "comp")
    new_state, series = call(
        second_step_kernel, "second_step", [(LEV, ROWS, COLS), (NSTEP, ROWS, COLS)],
        mix, vel, couple, mask, index, weight, col0, col1, row0, row1, *parts, fluxes,
        scratch=[(24, COLS), tile, tile],
    )
    return new_state[None], series[None]


def solution(mesh):
    in_specs = (
        P("comp", None, "lat", "lon"),
        P(None, "lat", "lon"),
        P("comp", None, "lat", "lon"),
        P("comp", None, "lat", "lon"),
        P("comp", "lat", "lon"),
        P("comp", "lat", "lon"),
        P("comp", None, "lat", "lon"),
        P("comp", None, "lat", "lon"),
    )
    out_specs = (P("comp", None, "lat", "lon"), P("comp", None, "lat", "lon"))
    return jax.shard_map(
        per_device, mesh=mesh, in_specs=in_specs, out_specs=out_specs, check_vma=False
    )
```

time: 273 us -> 40.8 us (0.15)
  the two profiles are of different devices: /device:TPU:96 before, /device:TPU:32 now
where the time goes in v1:
time: 40.8 us; the launch traced here: 40.2 us
  starting transfers between devices  15.1 us (37%)
  blocking collectives  12.4 us (30%)
  local copies, waits for them, and re-layouts  6.14 us (15%)
  Pallas kernels  3.37 us (8%)
  waiting for transfers between devices  2.5 us (6%)
  between operations  0.72 us (2%)
    ppermute x1, starting transfers between devices, per_device(): col1 = lax.ppermute(to_far, 'lon', pairs(n_lon, 1, True))  13.1 us
    unnamed x24, local copies, waits for them, and re-layouts  6.14 us
    all_gather x1, blocking collectives, per_device(): col0 = lax.all_gather(to_near, 'lon', axis_index_groups=partners(n_lon))  5.31 us
    all_gather x1, blocking collectives, per_device(): fluxes = lax.all_gather(fluxes, 'comp')  4.76 us
    pallas_call x4, Pallas kernels, call(): pl.pallas_call(kernel, name=name, out_shape=[jax.ShapeDtypeStruct(shape,...  3.37 us
    ppermute x1, waiting for transfers between devices, per_device(): row1 = lax.ppermute(to_far, 'lat', pairs(n_lat, 1, False))  2.5 us
    all_gather x1, blocking collectives, per_device(): row0 = lax.all_gather(to_near, 'lat', axis_index_groups=partners(n_lat))  2.32 us
    ppermute x1, starting transfers between devices, per_device(): row1 = lax.ppermute(to_far, 'lat', pairs(n_lat, 1, False))  1.92 us
  transfers between devices with their start and end apart: 2, of which 1 were waited for; matrix products, arithmetic and copies ran while one was open for 0% of the time, Pallas kernels for 0%

profile of v1, /device:TPU:32, one launch (start us, length us, event | category | flops | bytes accessed | tf_op | source)
XLA Modules:
  0.0 40.2 jit_solution(15560173361193389225)
XLA Ops:
  0.6 0.0 copy-start.9
  0.6 0.7 %copy-done.9 = f32[1,16,128]{2,1,0:T(8,128)S(1)} copy-done((f32[1,16,128]{2,1,0:T(8,128)S(1)}, f32[1,16,128]{2,1,0:T(8,128)}, u32[]{:S(2)}) %copy-start.9) | copy-done | bytes 8216
  1.3 0.0 copy-start
  1.3 0.9 %copy-done = f32[1,11,16,128]{3,2,1,0:T(8,128)S(1)} copy-done((f32[1,11,16,128]{3,2,1,0:T(8,128)S(1)}, f32[1,11,16,128]{3,2,1,0:T(8,128)}, u32[]{:S(2)}) %copy-start) | copy-done | bytes 90136
  2.2 0.0 copy-start.2
  2.2 0.9 %copy-done.2 = f32[1,12,16,128]{3,2,1,0:T(8,128)S(1)} copy-done((f32[1,12,16,128]{3,2,1,0:T(8,128)S(1)}, f32[1,12,16,128]{3,2,1,0:T(8,128)}, u32[]{:S(2)}) %copy-start.2) | copy-done | bytes 98328
  3.1 0.0 copy-start.3
  3.1 0.8 %copy-done.3 = s32[1,4,16,128]{3,2,1,0:T(8,128)S(1)} copy-done((s32[1,4,16,128]{3,2,1,0:T(8,128)S(1)}, s32[1,4,16,128]{3,2,1,0:T(8,128)}, u32[]{:S(2)}) %copy-start.3) | copy-done | bytes 32792
  3.9 0.0 copy-start.5
  3.9 0.8 %copy-done.5 = f32[1,4,16,128]{3,2,1,0:T(8,128)S(1)} copy-done((f32[1,4,16,128]{3,2,1,0:T(8,128)S(1)}, f32[1,4,16,128]{3,2,1,0:T(8,128)}, u32[]{:S(2)}) %copy-start.5) | copy-done | bytes 32792
  4.6 0.0 copy-start.7
  4.6 0.7 %copy-done.7 = f32[1,2,16,128]{3,2,1,0:T(8,128)S(1)} copy-done((f32[1,2,16,128]{3,2,1,0:T(8,128)S(1)}, f32[1,2,16,128]{3,2,1,0:T(8,128)}, u32[]{:S(2)}) %copy-start.7) | copy-done | bytes 16408
  5.3 0.0 copy-start.10
  5.3 0.7 %copy-done.10 = s32[1,16,128]{2,1,0:T(8,128)S(1)} copy-done((s32[1,16,128]{2,1,0:T(8,128)S(1)}, s32[1,16,128]{2,1,0:T(8,128)}, u32[]{:S(2)}) %copy-start.10) | copy-done | bytes 8216
  6.0 0.0 copy-start.11
  6.0 0.7 %copy-done.11 = f32[2,16,128]{2,1,0:T(8,128)S(1)} copy-done((f32[2,16,128]{2,1,0:T(8,128)S(1)}, f32[2,16,128]{2,1,0:T(8,128)}, u32[]{:S(2)}) %copy-start.11) | copy-done | bytes 16408
  6.8 0.6 %pack_columns.1 = (f32[32,128]{1,0:T(8,128)S(1)}, f32[32,128]{1,0:T(8,128)S(1)}, f32[16,128]{1,0:T(8,128)S(1)}) custom-call(f32[12,16,128]{2,1,0:T(8,128)S(1)} %bitcast.18, f32[2,16,128]{2,1,0:T(8,128)S(1)} %copy-done.11, f32[11,16,128]{2,1,0:T(8,128)S(1)} %bitcast.12, f32[2,16,128]{2,1,0:T(8,128)S(1)} %bitcast.33, f32[16,128]{1,0:T(8,128)S(1)} %bitcast.37, ...), custom_call_target="tpu_custom_call" | custom-call | tf_op jit(solution)/shard_map/pack_columns/pallas_call | solution.py:367
  7.4 0.0 copy-start.4
  7.4 13.1 %collective-permute-start = (f32[32,128]{1,0:T(8,128)S(1)}, f32[32,128]{1,0:T(8,128)S(1)}, u32[]{:S(2)}, u32[]{:S(2)}) collective-permute-start(f32[32,128]{1,0:T(8,128)S(1)} %get-tuple-element.16), channel_id=1, source_target_pairs={{1,2},{2,1},{3,4},{4,3},{5,6},{6,5},{7,8},{8,7},{9,10},{10,9},{11,... | collective-permute-start | bytes 49160 | tf_op jit(solution)/shard_map/ppermute | solution.py:404
  20.6 0.0 copy-start.8
  20.6 5.3 %all-gather = f32[64,128]{1,0:T(8,128)S(1)} all-gather(f32[32,128]{1,0:T(8,128)S(1)} %get-tuple-element.15), channel_id=2, replica_groups={{0,1},{2,3},{4,5},{6,7},{8,9},{10,11},{12,13},{14,15},{16,17},{18,19},{..., dimensions={0}, use_global_device_ids=true | all-gather | bytes 49152 | tf_op jit(solution)/shard_map/all_gather | solution.py:405
  25.9 0.0 collective-permute-done.got1.col1
  25.9 0.0 copy-done.1
  25.9 0.0 copy-done.6
  25.9 0.0 copy-done.4
  25.9 0.0 copy-done.8
  26.0 1.9 %collective-permute-start.1 = (f32[120,128]{1,0:T(8,128)S(1)}, f32[120,128]{1,0:T(8,128)S(1)}, u32[]{:S(2)}, u32[]{:S(2)}) collective-permute-start(f32[120,128]{1,0:T(8,128)S(1)} %get-tuple-element.19), channel_id=1, source_target_pairs={{16,32},{32,16},{48,64},{64,48},{80,96},{96,80},{112,128},{128,112... | collective-permute-start | bytes 184328 | tf_op jit(solution)/shard_map/ppermute | solution.py:411
  27.9 2.3 %all-gather.1 = f32[240,128]{1,0:T(8,128)S(1)} all-gather(f32[120,128]{1,0:T(8,128)S(1)} %get-tuple-element.18), channel_id=3, replica_groups={{0,16},{32,48},{64,80},{96,112},{128,144},{160,176},{192,208},{224,240}..., dimensions={0}, use_global_device_ids=true | all-gather | bytes 184320 | tf_op jit(solution)/shard_map/all_gather | solution.py:412
  30.2 2.5 %collective-permute-done.1.row1 = f32[120,128]{1,0:T(8,128)S(1)} collective-permute-done((f32[120,128]{1,0:T(8,128)S(1)}, f32[120,128]{1,0:T(8,128)S(1)}, u32[]{:S(2)}, u32[]{:S(2)}) %collective-permute-start.1) | collective-permute-done | bytes 61472 | tf_op jit(solution)/shard_map/ppermute | solution.py:411
  32.7 1.7 %first_step.1 = (f32[12,24,128]{2,1,0:T(8,128)S(1)}, f32[12,16,128]{2,1,0:T(8,128)S(1)}, f32[12,24,128]{2,1,0:T(8,128)S(1)}, f32[12,16,128]{2,1,0:T(8,128)S(1)},...) custom-call(f32[12,16,128]{2,1,0:T(8,128)S(1)} %bitcast.20, f32[2,16,128]{2,1,0:T(8,128)S(1)} %copy-done.11, ...), custom_call_target="tpu_custom_call" | custom-call | tf_op jit(solution)/shard_map/first_step/pallas_call | solution.py:367
  34.5 4.8 %all-gather.2 = f32[192,128]{1,0:T(8,128)S(1)} all-gather(f32[96,128]{1,0:T(8,128)S(1)} %get-tuple-element.25), channel_id=4, replica_groups=mesh['comp'=2,'lat'=16,'lon'=16] {'comp'}, dimensions={0}, use_global_device_ids=true | all-gather | bytes 147456 | tf_op jit(solution)/shard_map/all_gather | solution.py:419
  39.2 1.0 %second_step.1 = (f32[12,16,128]{2,1,0:T(8,128)}, f32[2,16,128]{2,1,0:T(8,128)}) custom-call(f32[11,16,128]{2,1,0:T(8,128)S(1)} %bitcast.15, f32[2,16,128]{2,1,0:T(8,128)S(1)} %bitcast.36, f32[16,128]{1,0:T(8,128)S(1)} %bitcast.40, s32[16,128]{1,0:T(8,128)S(1)} %bitcast.44, s32[4,16,128]{2,1,0:T(8,128)S(1)} %bitcast.24, f32[4,16,128]{2,1,0:T(8,128)S(1)} %bitcast.28, ...), custom_call_target="tpu_custom_call" | custom-call | tf_op jit(solution)/shard_map/second_step/pallas_call | solution.py:367
  (3 shorter events, 0.0 us)
Async XLA Ops:
  0.6 0.7 %copy-start.9 = (f32[1,16,128]{2,1,0:T(8,128)S(1)}, f32[1,16,128]{2,1,0:T(8,128)}, u32[]{:S(2)}) copy-start(f32[1,16,128]{2,1,0:T(8,128)} %param.12) | copy-start | bytes 24580
  1.3 0.9 %copy-start = (f32[1,11,16,128]{3,2,1,0:T(8,128)S(1)}, f32[1,11,16,128]{3,2,1,0:T(8,128)}, u32[]{:S(2)}) copy-start(f32[1,11,16,128]{3,2,1,0:T(8,128)} %param.10) | copy-start | bytes 270340
  2.2 0.9 %copy-start.2 = (f32[1,12,16,128]{3,2,1,0:T(8,128)S(1)}, f32[1,12,16,128]{3,2,1,0:T(8,128)}, u32[]{:S(2)}) copy-start(f32[1,12,16,128]{3,2,1,0:T(8,128)} %param.8) | copy-start | bytes 294916
  3.1 0.8 %copy-start.3 = (s32[1,4,16,128]{3,2,1,0:T(8,128)S(1)}, s32[1,4,16,128]{3,2,1,0:T(8,128)}, u32[]{:S(2)}) copy-start(s32[1,4,16,128]{3,2,1,0:T(8,128)} %param.14) | copy-start | bytes 98308
  3.9 0.8 %copy-start.5 = (f32[1,4,16,128]{3,2,1,0:T(8,128)S(1)}, f32[1,4,16,128]{3,2,1,0:T(8,128)}, u32[]{:S(2)}) copy-start(f32[1,4,16,128]{3,2,1,0:T(8,128)} %param.15) | copy-start | bytes 98308
  4.6 0.7 %copy-start.7 = (f32[1,2,16,128]{3,2,1,0:T(8,128)S(1)}, f32[1,2,16,128]{3,2,1,0:T(8,128)}, u32[]{:S(2)}) copy-start(f32[1,2,16,128]{3,2,1,0:T(8,128)} %param.11) | copy-start | bytes 49156
  5.3 0.7 %copy-start.10 = (s32[1,16,128]{2,1,0:T(8,128)S(1)}, s32[1,16,128]{2,1,0:T(8,128)}, u32[]{:S(2)}) copy-start(s32[1,16,128]{2,1,0:T(8,128)} %param.13) | copy-start | bytes 24580
  6.0 0.7 %copy-start.11 = (f32[2,16,128]{2,1,0:T(8,128)S(1)}, f32[2,16,128]{2,1,0:T(8,128)}, u32[]{:S(2)}) copy-start(f32[2,16,128]{2,1,0:T(8,128)} %prev.3) | copy-start | bytes 49156
  6.8 19.1 %copy-start.1 = (f32[1,11,16,128]{3,2,1,0:T(8,128)S(1)}, f32[1,11,16,128]{3,2,1,0:T(8,128)}, u32[]{:S(2)}) copy-start(f32[1,11,16,128]{3,2,1,0:T(8,128)} %param.10) | copy-start | bytes 270340
  6.8 19.1 %copy-start.6 = (f32[1,4,16,128]{3,2,1,0:T(8,128)S(1)}, f32[1,4,16,128]{3,2,1,0:T(8,128)}, u32[]{:S(2)}) copy-start(f32[1,4,16,128]{3,2,1,0:T(8,128)} %param.15) | copy-start | bytes 98308
  7.4 18.5 %copy-start.4 = (s32[1,4,16,128]{3,2,1,0:T(8,128)S(1)}, s32[1,4,16,128]{3,2,1,0:T(8,128)}, u32[]{:S(2)}) copy-start(s32[1,4,16,128]{3,2,1,0:T(8,128)} %param.14) | copy-start | bytes 98308
  7.4 18.5 %collective-permute-start = (f32[32,128]{1,0:T(8,128)S(1)}, f32[32,128]{1,0:T(8,128)S(1)}, u32[]{:S(2)}, u32[]{:S(2)}) collective-permute-start(f32[32,128]{1,0:T(8,128)S(1)} %get-tuple-element.16), channel_id=1, source_target_pairs={{1,2},{2,1},{3,4},{4,3},{5,6},{6,5},{7,8},{8,7},{9,10},{10,9},{11,... | collective-permute-start | bytes 49160 | tf_op jit(solution)/shard_map/ppermute | solution.py:404
  20.6 5.3 %copy-start.8 = (f32[1,2,16,128]{3,2,1,0:T(8,128)S(1)}, f32[1,2,16,128]{3,2,1,0:T(8,128)}, u32[]{:S(2)}) copy-start(f32[1,2,16,128]{3,2,1,0:T(8,128)} %param.11) | copy-start | bytes 49156
  26.0 6.8 %collective-permute-start.1 = (f32[120,128]{1,0:T(8,128)S(1)}, f32[120,128]{1,0:T(8,128)S(1)}, u32[]{:S(2)}, u32[]{:S(2)}) collective-permute-start(f32[120,128]{1,0:T(8,128)S(1)} %get-tuple-element.19), channel_id=1, source_target_pairs={{16,32},{32,16},{48,64},{64,48},{80,96},{96,80},{112,128},{128,112... | collective-permute-start | bytes 184328 | tf_op jit(solution)/shard_map/ppermute | solution.py:411

commit v2 on v1

--- a/solution.py
+++ b/solution.py
@@ -38,14 +38,22 @@
 
 
 def gather_cells(table, index):
-    row = lax.shift_right_logical(index, 7)
-    column = lax.bitwise_and(index, COLS - 1)
-    total = jnp.zeros(index.shape, jnp.float32)
-    for r in range(ROWS):
-        source = jnp.broadcast_to(table[r : r + 1], index.shape)
-        picked = jnp.take_along_axis(source, column, axis=1, mode="promise_in_bounds")
-        total = jnp.where(row == r, picked, total)
-    return total
+    sources = [jnp.broadcast_to(table[r : r + 1], (8, COLS)) for r in range(ROWS)]
+    blocks = []
+    for at in range(0, index.shape[0], 8):
+        cell = index[at : at + 8]
+        column = lax.bitwise_and(cell, COLS - 1)
+        picked = [
+            jnp.take_along_axis(source, column, axis=1, mode="promise_in_bounds")
+            for source in sources
+        ]
+        bit = COLS
+        while len(picked) > 1:
+            chosen = lax.bitwise_and(cell, bit) != 0
+            picked = [jnp.where(chosen, b, a) for a, b in zip(picked[::2], picked[1::2])]
+            bit *= 2
+        blocks.append(picked[0])
+    return jnp.concatenate(blocks, axis=0)
 
 
 def regrid_tile(table, index_ref, weight_ref):
@@ -55,12 +63,33 @@
 
 
 def pack_columns_kernel(
-    state, prev, mix, vel, couple, mask, index, weight, msg0, msg1, flux_out
+    state_hbm, prev_hbm, mix_hbm, vel_hbm, couple_hbm, mask_hbm, index_hbm, weight_hbm,
+    msg0, msg1, flux_out, rate_out, state, prev, mix, vel, index, weight, couple, mask, arrived,
 ):
+    moves = [
+        pltpu.make_async_copy(source, target, arrived.at[k])
+        for k, (source, target) in enumerate(
+            (
+                (state_hbm, state),
+                (mix_hbm, mix),
+                (index_hbm, index),
+                (weight_hbm, weight),
+                (prev_hbm, prev),
+                (vel_hbm, vel),
+                (couple_hbm, couple),
+                (mask_hbm, mask),
+            )
+        )
+    ]
+    for move in moves:
+        move.start()
     is_atmosphere = lax.axis_index("comp") == 0
     odd = lax.rem(lax.axis_index("lon"), 2) == 1
     lane = lanes(ROWS)
+    for move in moves:
+        move.wait()
     rate = couple[...] * mask[...].astype(jnp.float32)
+    rate_out[...] = rate
 
     def packed(last):
         total = jnp.zeros((ROWS, COLS), jnp.float32)
@@ -108,11 +137,11 @@
 
 
 def pack_rows_kernel(
-    state, mix, vel, couple, mask, index, weight, flux, got0, got1, msg0, msg1
+    state, mix, vel, rate_in, index, weight, flux, got0, got1, msg0, msg1
 ):
     odd = lax.rem(lax.axis_index("lat"), 2) == 1
     west, east = column_messages(got0, got1)
-    rate = couple[...] * mask[...].astype(jnp.float32)
+    rate = rate_in[...]
 
     def put(x, at, width):
         head, tail = x[0:width], x[ROWS - width : ROWS]
@@ -212,7 +241,7 @@
 
 
 def first_step_kernel(
-    state, prev, mix, vel, couple, mask, index, weight, flux, col0, col1, row0, row1,
+    state, prev, mix, vel, rate_in, index, weight, flux, col0, col1, row0, row1,
     before, before_side, unit, unit_side, inverse_out, fluxes,
 ):
     is_atmosphere = lax.axis_index("comp") == 0
@@ -267,7 +296,7 @@
     inverses, ratios = factors(own_mix)
     solved = solve(moved, own_mix, inverses, ratios)
     impulse = solve([1.0] + [None] * (LEV - 1), own_mix, inverses, ratios)
-    rate = couple[...] * mask[...].astype(jnp.float32)
+    rate = rate_in[...]
 
     fluxes[0:ROWS] = flux[...]
     fluxes[ROWS : 2 * ROWS] = west[ROWS:]
@@ -298,7 +327,7 @@
 
 
 def second_step_kernel(
-    mix, vel, couple, mask, index, weight, col0, col1, row0, row1,
+    mix, vel, rate_in, index, weight, col0, col1, row0, row1,
     before, before_side, unit, unit_side, inverse, fluxes, new_state, series, force, force_side, force1,
 ):
     is_atmosphere = lax.axis_index("comp") == 0
@@ -315,7 +344,7 @@
 
     @pl.when(jnp.logical_not(is_atmosphere))
     def _():
-        rate = couple[...] * mask[...].astype(jnp.float32)
+        rate = rate_in[...]
         force[0:ROWS] = rate * regrid_tile(tables[0], index, weight)
         force1[...] = rate * regrid_tile(tables[5], index, weight)
         west, east = column_messages(col0, col1)
@@ -362,15 +391,14 @@
     series[1] = jnp.where(is_atmosphere, tables[5], solved[0])
 
 
-def call(kernel, name, shapes, *args, scratch=()):
-    vmem = pl.BlockSpec(memory_space=pltpu.VMEM)
+def call(kernel, name, shapes, *args, scratch=(), place=pltpu.VMEM):
     return pl.pallas_call(
         kernel,
         name=name,
-        out_shape=[jax.ShapeDtypeStruct(shape, jnp.float32) for shape in shapes],
-        in_specs=[vmem] * len(args),
-        out_specs=[vmem] * len(shapes),
-        scratch_shapes=[pltpu.VMEM(shape, jnp.float32) for shape in scratch],
+        out_shape=[s if hasattr(s, "dtype") else jax.ShapeDtypeStruct(s, jnp.float32) for s in shapes],
+        in_specs=[pl.BlockSpec(memory_space=place)] * len(args),
+        out_specs=[pl.BlockSpec(memory_space=pltpu.VMEM)] * len(shapes),
+        scratch_shapes=list(scratch),
         compiler_params=pltpu.CompilerParams(vmem_limit_bytes=16 * 1024 * 1024),
         interpret=INTERPRET,
     )(*args)
@@ -393,20 +421,25 @@
     state, prev_surface, mixing, velocity, coupling, sea_mask, interp_index, interp_weight
 ):
     n_lat, n_lon = lax.axis_size("lat"), lax.axis_size("lon")
-    state, mix, vel, couple, mask = state[0], mixing[0], velocity[0], coupling[0], sea_mask[0]
-    index, weight = interp_index[0], interp_weight[0]
+    given = (
+        state[0], prev_surface, mixing[0], velocity[0],
+        coupling[0], sea_mask[0], interp_index[0], interp_weight[0],
+    )
+    state, prev, mix, vel, couple, mask, index, weight = given
     tile = (ROWS, COLS)
     column_shape = (COL_MESSAGE, COLS)
-    to_near, to_far, flux = call(
-        pack_columns_kernel, "pack_columns", [column_shape, column_shape, tile],
-        state, prev_surface, mix, vel, couple, mask, index, weight,
+    to_near, to_far, flux, rate, state, prev, mix, vel, index, weight = call(
+        pack_columns_kernel, "pack_columns",
+        [column_shape, column_shape, tile, tile, state, prev, mix, vel, index, weight],
+        *given, place=pltpu.HBM,
+        scratch=[pltpu.VMEM(tile, couple.dtype), pltpu.VMEM(tile, mask.dtype), pltpu.SemaphoreType.DMA((8,))],
     )
     col1 = lax.ppermute(to_far, "lon", pairs(n_lon, 1, True))
     col0 = lax.all_gather(to_near, "lon", axis_index_groups=partners(n_lon))
     row_shape = (ROW_MESSAGE, COLS)
     to_near, to_far = call(
         pack_rows_kernel, "pack_rows", [row_shape, row_shape],
-        state, mix, vel, couple, mask, index, weight, flux, col0, col1,
+        state, mix, vel, rate, index, weight, flux, col0, col1,
     )
     row1 = lax.ppermute(to_far, "lat", pairs(n_lat, 1, False))
     row0 = lax.all_gather(to_near, "lat", axis_index_groups=partners(n_lat))
@@ -414,13 +447,13 @@
     *parts, fluxes = call(
         first_step_kernel, "first_step",
         [wide, narrow, wide, narrow, narrow, (6 * ROWS, COLS)],
-        state, prev_surface, mix, vel, couple, mask, index, weight, flux, col0, col1, row0, row1,
+        state, prev, mix, vel, rate, index, weight, flux, col0, col1, row0, row1,
     )
     fluxes = lax.all_gather(fluxes, "comp")
     new_state, series = call(
         second_step_kernel, "second_step", [(LEV, ROWS, COLS), (NSTEP, ROWS, COLS)],
-        mix, vel, couple, mask, index, weight, col0, col1, row0, row1, *parts, fluxes,
-        scratch=[(24, COLS), tile, tile],
+        mix, vel, rate, index, weight, col0, col1, row0, row1, *parts, fluxes,
+        scratch=[pltpu.VMEM(shape, jnp.float32) for shape in ((24, COLS), tile, tile)],
     )
     return new_state[None], series[None]
 

time: 40.8 us -> 40.8 us (level)
    unnamed x24 -> x16, local copies, waits for them, and re-layouts: 6.14 us -> 6.12 us
where the time goes in v2:
time: 40.8 us; the launch traced here: 40.2 us
  starting transfers between devices  15.1 us (37%)
  blocking collectives  12.4 us (30%)
  local copies, waits for them, and re-layouts  6.12 us (15%)
  Pallas kernels  3.46 us (8%)
  waiting for transfers between devices  2.5 us (6%)
  between operations  0.69 us (2%)
    ppermute x1, starting transfers between devices, per_device(): col1 = lax.ppermute(to_far, 'lon', pairs(n_lon, 1, True))  13.1 us
    unnamed x16, local copies, waits for them, and re-layouts  6.12 us
    all_gather x1, blocking collectives, per_device(): col0 = lax.all_gather(to_near, 'lon', axis_index_groups=partners(n_lon))  5.31 us
    all_gather x1, blocking collectives, per_device(): fluxes = lax.all_gather(fluxes, 'comp')  4.76 us
    pallas_call x4, Pallas kernels, call(): pl.pallas_call(kernel, name=name, out_shape=[s if hasattr(s, 'dtype') els...  3.46 us
    ppermute x1, waiting for transfers between devices, per_device(): row1 = lax.ppermute(to_far, 'lat', pairs(n_lat, 1, False))  2.5 us
    all_gather x1, blocking collectives, per_device(): row0 = lax.all_gather(to_near, 'lat', axis_index_groups=partners(n_lat))  2.32 us
    ppermute x1, starting transfers between devices, per_device(): row1 = lax.ppermute(to_far, 'lat', pairs(n_lat, 1, False))  1.92 us
  transfers between devices with their start and end apart: 2, of which 1 were waited for; matrix products, arithmetic and copies ran while one was open for 0% of the time, Pallas kernels for 0%

profile of v2, /device:TPU:32, one launch (start us, length us, event | category | flops | bytes accessed | tf_op | source)
XLA Modules:
  0.0 40.2 jit_solution(6775140126720663590)
XLA Ops:
  0.6 0.0 copy-start.6
  0.6 0.7 %copy-done.6 = f32[1,16,128]{2,1,0:T(8,128)S(1)} copy-done((f32[1,16,128]{2,1,0:T(8,128)S(1)}, f32[1,16,128]{2,1,0:T(8,128)}, u32[]{:S(2)}) %copy-start.6) | copy-done | bytes 8216
  1.3 0.0 copy-start
  1.3 0.9 %copy-done = f32[1,12,16,128]{3,2,1,0:T(8,128)S(1)} copy-done((f32[1,12,16,128]{3,2,1,0:T(8,128)S(1)}, f32[1,12,16,128]{3,2,1,0:T(8,128)}, u32[]{:S(2)}) %copy-start) | copy-done | bytes 98328
  2.2 0.0 copy-start.1
  2.2 0.9 %copy-done.1 = f32[1,11,16,128]{3,2,1,0:T(8,128)S(1)} copy-done((f32[1,11,16,128]{3,2,1,0:T(8,128)S(1)}, f32[1,11,16,128]{3,2,1,0:T(8,128)}, u32[]{:S(2)}) %copy-start.1) | copy-done | bytes 90136
  3.1 0.0 copy-start.2
  3.1 0.8 %copy-done.2 = s32[1,4,16,128]{3,2,1,0:T(8,128)S(1)} copy-done((s32[1,4,16,128]{3,2,1,0:T(8,128)S(1)}, s32[1,4,16,128]{3,2,1,0:T(8,128)}, u32[]{:S(2)}) %copy-start.2) | copy-done | bytes 32792
  3.9 0.0 copy-start.3
  3.9 0.8 %copy-done.3 = f32[1,4,16,128]{3,2,1,0:T(8,128)S(1)} copy-done((f32[1,4,16,128]{3,2,1,0:T(8,128)S(1)}, f32[1,4,16,128]{3,2,1,0:T(8,128)}, u32[]{:S(2)}) %copy-start.3) | copy-done | bytes 32792
  4.6 0.0 copy-start.4
  4.6 0.7 %copy-done.4 = f32[2,16,128]{2,1,0:T(8,128)S(1)} copy-done((f32[2,16,128]{2,1,0:T(8,128)S(1)}, f32[2,16,128]{2,1,0:T(8,128)}, u32[]{:S(2)}) %copy-start.4) | copy-done | bytes 16408
  5.3 0.0 copy-start.5
  5.4 0.7 %copy-done.5 = f32[1,2,16,128]{3,2,1,0:T(8,128)S(1)} copy-done((f32[1,2,16,128]{3,2,1,0:T(8,128)S(1)}, f32[1,2,16,128]{3,2,1,0:T(8,128)}, u32[]{:S(2)}) %copy-start.5) | copy-done | bytes 16408
  6.1 0.0 copy-start.7
  6.1 0.7 %copy-done.7 = s32[1,16,128]{2,1,0:T(8,128)S(1)} copy-done((s32[1,16,128]{2,1,0:T(8,128)S(1)}, s32[1,16,128]{2,1,0:T(8,128)}, u32[]{:S(2)}) %copy-start.7) | copy-done | bytes 8216
  6.8 0.9 %pack_columns.1 = (f32[32,128]{1,0:T(8,128)S(1)}, f32[32,128]{1,0:T(8,128)S(1)}, f32[16,128]{1,0:T(8,128)S(1)}, f32[16,128]{1,0:T(8,128)S(1)}, f32[12,16,128]{2,...) custom-call(f32[12,16,128]{2,1,0:T(8,128)S(1)} %bitcast.18, ...), custom_call_target="tpu_custom_call" | custom-call | tf_op jit(solution)/shard_map/pack_columns/pallas_call | solution.py:395
  7.7 13.1 %collective-permute-start = (f32[32,128]{1,0:T(8,128)S(1)}, f32[32,128]{1,0:T(8,128)S(1)}, u32[]{:S(2)}, u32[]{:S(2)}) collective-permute-start(f32[32,128]{1,0:T(8,128)S(1)} %get-tuple-element.28), channel_id=1, source_target_pairs={{1,2},{2,1},{3,4},{4,3},{5,6},{6,5},{7,8},{8,7},{9,10},{10,9},{11,... | collective-permute-start | bytes 49160 | tf_op jit(solution)/shard_map/ppermute | solution.py:437
  20.8 5.3 %all-gather = f32[64,128]{1,0:T(8,128)S(1)} all-gather(f32[32,128]{1,0:T(8,128)S(1)} %get-tuple-element.27), channel_id=2, replica_groups={{0,1},{2,3},{4,5},{6,7},{8,9},{10,11},{12,13},{14,15},{16,17},{18,19},{..., dimensions={0}, use_global_device_ids=true | all-gather | bytes 49152 | tf_op jit(solution)/shard_map/all_gather | solution.py:438
  26.1 0.0 collective-permute-done.got1.col1
  26.2 1.9 %collective-permute-start.1 = (f32[120,128]{1,0:T(8,128)S(1)}, f32[120,128]{1,0:T(8,128)S(1)}, u32[]{:S(2)}, u32[]{:S(2)}) collective-permute-start(f32[120,128]{1,0:T(8,128)S(1)} %get-tuple-element.32), channel_id=1, source_target_pairs={{16,32},{32,16},{48,64},{64,48},{80,96},{96,80},{112,128},{128,112... | collective-permute-start | bytes 184328 | tf_op jit(solution)/shard_map/ppermute | solution.py:444
  28.1 2.3 %all-gather.1 = f32[240,128]{1,0:T(8,128)S(1)} all-gather(f32[120,128]{1,0:T(8,128)S(1)} %get-tuple-element.31), channel_id=3, replica_groups={{0,16},{32,48},{64,80},{96,112},{128,144},{160,176},{192,208},{224,240}..., dimensions={0}, use_global_device_ids=true | all-gather | bytes 184320 | tf_op jit(solution)/shard_map/all_gather | solution.py:445
  30.4 2.5 %collective-permute-done.1.row1 = f32[120,128]{1,0:T(8,128)S(1)} collective-permute-done((f32[120,128]{1,0:T(8,128)S(1)}, f32[120,128]{1,0:T(8,128)S(1)}, u32[]{:S(2)}, u32[]{:S(2)}) %collective-permute-start.1) | collective-permute-done | bytes 61472 | tf_op jit(solution)/shard_map/ppermute | solution.py:444
  32.9 1.5 %first_step.1 = (f32[12,24,128]{2,1,0:T(8,128)S(1)}, f32[12,16,128]{2,1,0:T(8,128)S(1)}, f32[12,24,128]{2,1,0:T(8,128)S(1)}, f32[12,16,128]{2,1,0:T(8,128)S(1)},...) custom-call(f32[12,16,128]{2,1,0:T(8,128)S(1)} %get-tuple-element.29.state, f32[2,16,128]{2,1,0:T(8,128)S(1)} %get-tuple-element.33.prev, ...), custom_call_target="tpu_custom_call" | custom-call | tf_op jit(solution)/shard_map/first_step/pallas_call | solution.py:395
  34.5 4.8 %all-gather.2 = f32[192,128]{1,0:T(8,128)S(1)} all-gather(f32[96,128]{1,0:T(8,128)S(1)} %get-tuple-element.39), channel_id=4, replica_groups=mesh['comp'=2,'lat'=16,'lon'=16] {'comp'}, dimensions={0}, use_global_device_ids=true | all-gather | bytes 147456 | tf_op jit(solution)/shard_map/all_gather | solution.py:452
  39.2 1.0 %second_step.1 = (f32[12,16,128]{2,1,0:T(8,128)}, f32[2,16,128]{2,1,0:T(8,128)}) custom-call(f32[11,16,128]{2,1,0:T(8,128)S(1)} %get-tuple-element.22.mix, f32[2,16,128]{2,1,0:T(8,128)S(1)} %get-tuple-element.23.vel, f32[16,128]{1,0:T(8,128)S(1)} %get-tuple-element.24.rate_in, s32[4,16,128]{2,1,0:T(8,128)S(1)} %get-tuple-element.25.index, ...), custom_call_target="tpu_custom_call" | custom-call | tf_op jit(solution)/shard_map/second_step/pallas_call | solution.py:395
  (1 shorter events, 0.0 us)
Async XLA Ops:
  0.6 0.7 %copy-start.6 = (f32[1,16,128]{2,1,0:T(8,128)S(1)}, f32[1,16,128]{2,1,0:T(8,128)}, u32[]{:S(2)}) copy-start(f32[1,16,128]{2,1,0:T(8,128)} %param.12) | copy-start | bytes 24580
  1.3 0.9 %copy-start = (f32[1,12,16,128]{3,2,1,0:T(8,128)S(1)}, f32[1,12,16,128]{3,2,1,0:T(8,128)}, u32[]{:S(2)}) copy-start(f32[1,12,16,128]{3,2,1,0:T(8,128)} %param.8) | copy-start | bytes 294916
  2.2 0.9 %copy-start.1 = (f32[1,11,16,128]{3,2,1,0:T(8,128)S(1)}, f32[1,11,16,128]{3,2,1,0:T(8,128)}, u32[]{:S(2)}) copy-start(f32[1,11,16,128]{3,2,1,0:T(8,128)} %param.10) | copy-start | bytes 270340
  3.1 0.8 %copy-start.2 = (s32[1,4,16,128]{3,2,1,0:T(8,128)S(1)}, s32[1,4,16,128]{3,2,1,0:T(8,128)}, u32[]{:S(2)}) copy-start(s32[1,4,16,128]{3,2,1,0:T(8,128)} %param.14) | copy-start | bytes 98308
  3.9 0.8 %copy-start.3 = (f32[1,4,16,128]{3,2,1,0:T(8,128)S(1)}, f32[1,4,16,128]{3,2,1,0:T(8,128)}, u32[]{:S(2)}) copy-start(f32[1,4,16,128]{3,2,1,0:T(8,128)} %param.15) | copy-start | bytes 98308
  4.6 0.7 %copy-start.4 = (f32[2,16,128]{2,1,0:T(8,128)S(1)}, f32[2,16,128]{2,1,0:T(8,128)}, u32[]{:S(2)}) copy-start(f32[2,16,128]{2,1,0:T(8,128)} %prev_hbm.1) | copy-start | bytes 49156
  5.3 0.7 %copy-start.5 = (f32[1,2,16,128]{3,2,1,0:T(8,128)S(1)}, f32[1,2,16,128]{3,2,1,0:T(8,128)}, u32[]{:S(2)}) copy-start(f32[1,2,16,128]{3,2,1,0:T(8,128)} %param.11) | copy-start | bytes 49156
  6.1 0.7 %copy-start.7 = (s32[1,16,128]{2,1,0:T(8,128)S(1)}, s32[1,16,128]{2,1,0:T(8,128)}, u32[]{:S(2)}) copy-start(s32[1,16,128]{2,1,0:T(8,128)} %param.13) | copy-start | bytes 24580
  7.7 18.4 %collective-permute-start = (f32[32,128]{1,0:T(8,128)S(1)}, f32[32,128]{1,0:T(8,128)S(1)}, u32[]{:S(2)}, u32[]{:S(2)}) collective-permute-start(f32[32,128]{1,0:T(8,128)S(1)} %get-tuple-element.28), channel_id=1, source_target_pairs={{1,2},{2,1},{3,4},{4,3},{5,6},{6,5},{7,8},{8,7},{9,10},{10,9},{11,... | collective-permute-start | bytes 49160 | tf_op jit(solution)/shard_map/ppermute | solution.py:437
  26.2 6.8 %collective-permute-start.1 = (f32[120,128]{1,0:T(8,128)S(1)}, f32[120,128]{1,0:T(8,128)S(1)}, u32[]{:S(2)}, u32[]{:S(2)}) collective-permute-start(f32[120,128]{1,0:T(8,128)S(1)} %get-tuple-element.32), channel_id=1, source_target_pairs={{16,32},{32,16},{48,64},{64,48},{80,96},{96,80},{112,128},{128,112... | collective-permute-start | bytes 184328 | tf_op jit(solution)/shard_map/ppermute | solution.py:444

commit v3 on v2

--- a/solution.py
+++ b/solution.py
@@ -431,7 +431,7 @@
     to_near, to_far, flux, rate, state, prev, mix, vel, index, weight = call(
         pack_columns_kernel, "pack_columns",
         [column_shape, column_shape, tile, tile, state, prev, mix, vel, index, weight],
-        *given, place=pltpu.HBM,
+        *(pltpu.with_memory_space_constraint(x, pltpu.HBM) for x in given), place=pltpu.HBM,
         scratch=[pltpu.VMEM(tile, couple.dtype), pltpu.VMEM(tile, mask.dtype), pltpu.SemaphoreType.DMA((8,))],
     )
     col1 = lax.ppermute(to_far, "lon", pairs(n_lon, 1, True))

time: 40.8 us -> 34.8 us (0.85); the launches traced: 40.2 us -> 34.6 us
  local copies, waits for them, and re-layouts: 6.12 us -> 0 us
  Pallas kernels: 3.46 us -> 4.01 us
    unnamed x16 -> x0, local copies, waits for them, and re-layouts: 6.12 us -> none
    pallas_call x4, Pallas kernels: 3.46 us -> 4.01 us  [call(): pl.pallas_call(kernel, name=name, out_shape=[s if hasattr(s, 'dtype') els...]
where the time goes in v3:
time: 34.8 us; the launch traced here: 34.6 us
  starting transfers between devices  15.1 us (43%)
  blocking collectives  12.4 us (36%)
  Pallas kernels  4.01 us (12%)
  waiting for transfers between devices  2.5 us (7%)
  between operations  0.67 us (2%)
    ppermute x1, starting transfers between devices, per_device(): col1 = lax.ppermute(to_far, 'lon', pairs(n_lon, 1, True))  13.1 us
    all_gather x1, blocking collectives, per_device(): col0 = lax.all_gather(to_near, 'lon', axis_index_groups=partners(n_lon))  5.31 us
    all_gather x1, blocking collectives, per_device(): fluxes = lax.all_gather(fluxes, 'comp')  4.76 us
    pallas_call x4, Pallas kernels, call(): pl.pallas_call(kernel, name=name, out_shape=[s if hasattr(s, 'dtype') els...  4.01 us
    ppermute x1, waiting for transfers between devices, per_device(): row1 = lax.ppermute(to_far, 'lat', pairs(n_lat, 1, False))  2.5 us
    all_gather x1, blocking collectives, per_device(): row0 = lax.all_gather(to_near, 'lat', axis_index_groups=partners(n_lat))  2.32 us
    ppermute x1, starting transfers between devices, per_device(): row1 = lax.ppermute(to_far, 'lat', pairs(n_lat, 1, False))  1.92 us
  transfers between devices with their start and end apart: 2, of which 1 were waited for; matrix products, arithmetic and copies ran while one was open for 0% of the time, Pallas kernels for 0%

profile of v3, /device:TPU:32, one launch (start us, length us, event | category | flops | bytes accessed | tf_op | source)
XLA Modules:
  0.0 34.6 jit_solution(4866858081795014400)
XLA Ops:
  0.6 1.5 %pack_columns.1 = (f32[32,128]{1,0:T(8,128)S(1)}, f32[32,128]{1,0:T(8,128)S(1)}, f32[16,128]{1,0:T(8,128)S(1)}, f32[16,128]{1,0:T(8,128)S(1)}, f32[12,16,128]{2,...) custom-call(f32[12,16,128]{2,1,0:T(8,128)} %bitcast.18, ...), custom_call_target="tpu_custom_call" | custom-call | tf_op jit(solution)/shard_map/pack_columns/pallas_call | solution.py:395
  2.1 13.1 %collective-permute-start = (f32[32,128]{1,0:T(8,128)S(1)}, f32[32,128]{1,0:T(8,128)S(1)}, u32[]{:S(2)}, u32[]{:S(2)}) collective-permute-start(f32[32,128]{1,0:T(8,128)S(1)} %get-tuple-element.28), channel_id=1, source_target_pairs={{1,2},{2,1},{3,4},{4,3},{5,6},{6,5},{7,8},{8,7},{9,10},{10,9},{11,... | collective-permute-start | bytes 49160 | tf_op jit(solution)/shard_map/ppermute | solution.py:437
  15.3 5.3 %all-gather = f32[64,128]{1,0:T(8,128)S(1)} all-gather(f32[32,128]{1,0:T(8,128)S(1)} %get-tuple-element.27), channel_id=2, replica_groups={{0,1},{2,3},{4,5},{6,7},{8,9},{10,11},{12,13},{14,15},{16,17},{18,19},{..., dimensions={0}, use_global_device_ids=true | all-gather | bytes 49152 | tf_op jit(solution)/shard_map/all_gather | solution.py:438
  20.6 0.0 collective-permute-done.got1.col1
  20.6 1.9 %collective-permute-start.1 = (f32[120,128]{1,0:T(8,128)S(1)}, f32[120,128]{1,0:T(8,128)S(1)}, u32[]{:S(2)}, u32[]{:S(2)}) collective-permute-start(f32[120,128]{1,0:T(8,128)S(1)} %get-tuple-element.32), channel_id=1, source_target_pairs={{16,32},{32,16},{48,64},{64,48},{80,96},{96,80},{112,128},{128,112... | collective-permute-start | bytes 184328 | tf_op jit(solution)/shard_map/ppermute | solution.py:444
  22.5 2.3 %all-gather.1 = f32[240,128]{1,0:T(8,128)S(1)} all-gather(f32[120,128]{1,0:T(8,128)S(1)} %get-tuple-element.31), channel_id=3, replica_groups={{0,16},{32,48},{64,80},{96,112},{128,144},{160,176},{192,208},{224,240}..., dimensions={0}, use_global_device_ids=true | all-gather | bytes 184320 | tf_op jit(solution)/shard_map/all_gather | solution.py:445
  24.9 2.5 %collective-permute-done.1.row1 = f32[120,128]{1,0:T(8,128)S(1)} collective-permute-done((f32[120,128]{1,0:T(8,128)S(1)}, f32[120,128]{1,0:T(8,128)S(1)}, u32[]{:S(2)}, u32[]{:S(2)}) %collective-permute-start.1) | collective-permute-done | bytes 61472 | tf_op jit(solution)/shard_map/ppermute | solution.py:444
  27.4 1.5 %first_step.1 = (f32[12,24,128]{2,1,0:T(8,128)S(1)}, f32[12,16,128]{2,1,0:T(8,128)S(1)}, f32[12,24,128]{2,1,0:T(8,128)S(1)}, f32[12,16,128]{2,1,0:T(8,128)S(1)},...) custom-call(f32[12,16,128]{2,1,0:T(8,128)S(1)} %get-tuple-element.29.state, f32[2,16,128]{2,1,0:T(8,128)S(1)} %get-tuple-element.33.prev, ...), custom_call_target="tpu_custom_call" | custom-call | tf_op jit(solution)/shard_map/first_step/pallas_call | solution.py:395
  28.9 4.8 %all-gather.2 = f32[192,128]{1,0:T(8,128)S(1)} all-gather(f32[96,128]{1,0:T(8,128)S(1)} %get-tuple-element.39), channel_id=4, replica_groups=mesh['comp'=2,'lat'=16,'lon'=16] {'comp'}, dimensions={0}, use_global_device_ids=true | all-gather | bytes 147456 | tf_op jit(solution)/shard_map/all_gather | solution.py:452
  33.7 1.0 %second_step.1 = (f32[12,16,128]{2,1,0:T(8,128)}, f32[2,16,128]{2,1,0:T(8,128)}) custom-call(f32[11,16,128]{2,1,0:T(8,128)S(1)} %get-tuple-element.22.mix, f32[2,16,128]{2,1,0:T(8,128)S(1)} %get-tuple-element.23.vel, f32[16,128]{1,0:T(8,128)S(1)} %get-tuple-element.24.rate_in, s32[4,16,128]{2,1,0:T(8,128)S(1)} %get-tuple-element.25.index, ...), custom_call_target="tpu_custom_call" | custom-call | tf_op jit(solution)/shard_map/second_step/pallas_call | solution.py:395
  (1 shorter events, 0.0 us)
Async XLA Ops:
  2.1 18.4 %collective-permute-start = (f32[32,128]{1,0:T(8,128)S(1)}, f32[32,128]{1,0:T(8,128)S(1)}, u32[]{:S(2)}, u32[]{:S(2)}) collective-permute-start(f32[32,128]{1,0:T(8,128)S(1)} %get-tuple-element.28), channel_id=1, source_target_pairs={{1,2},{2,1},{3,4},{4,3},{5,6},{6,5},{7,8},{8,7},{9,10},{10,9},{11,... | collective-permute-start | bytes 49160 | tf_op jit(solution)/shard_map/ppermute | solution.py:437
  20.6 6.8 %collective-permute-start.1 = (f32[120,128]{1,0:T(8,128)S(1)}, f32[120,128]{1,0:T(8,128)S(1)}, u32[]{:S(2)}, u32[]{:S(2)}) collective-permute-start(f32[120,128]{1,0:T(8,128)S(1)} %get-tuple-element.32), channel_id=1, source_target_pairs={{16,32},{32,16},{48,64},{64,48},{80,96},{96,80},{112,128},{128,112... | collective-permute-start | bytes 184328 | tf_op jit(solution)/shard_map/ppermute | solution.py:444

commit v4 on v3

--- a/solution.py
+++ b/solution.py
@@ -4,6 +4,7 @@
 from jax.experimental import pallas as pl
 from jax.experimental.pallas import tpu as pltpu
 from jax.sharding import PartitionSpec as P
+
 
 INTERPRET = False
 NSTEP = 2
@@ -130,17 +131,18 @@
 
 
 def column_messages(got0, got1):
-    odd = lax.rem(lax.axis_index("lon"), 2)
-    near = got0[1 - odd]
+    at_lon = lax.axis_index("lon")
+    odd = lax.rem(at_lon, 2) == 1
+    near = jnp.where(lax.rem(at_lon, 4) < 2, got0[0][...], got0[1][...])
     far = got1[...]
-    return jnp.where(odd == 1, near, far), jnp.where(odd == 1, far, near)
+    return jnp.where(odd, near, far), jnp.where(odd, far, near)
 
 
 def pack_rows_kernel(
-    state, mix, vel, rate_in, index, weight, flux, got0, got1, msg0, msg1
+    state, mix, vel, rate_in, index, weight, flux, got0a, got0b, got1, msg0, msg1
 ):
     odd = lax.rem(lax.axis_index("lat"), 2) == 1
-    west, east = column_messages(got0, got1)
+    west, east = column_messages((got0a, got0b), got1)
     rate = rate_in[...]
 
     def put(x, at, width):
@@ -172,14 +174,6 @@
     near = got0[1 - odd]
     far = got1[...]
     return jnp.where(odd == 1, near, far), jnp.where(odd == 1, far, near)
-
-
-def east_shift(tile, side, shift, lane):
-    rows = side.shape[0]
-    moved, moved_side = roll(tile, shift, 1), roll(side, shift, 1)
-    cut = lane < shift if shift > 0 else lane >= COLS + shift
-    own = jnp.where(cut, moved_side[: tile.shape[0]], moved)
-    return own, jnp.where(cut[:rows], moved[:rows], moved_side)
 
 
 def transport_weights(east, north):
@@ -241,11 +235,11 @@
 
 
 def first_step_kernel(
-    state, prev, mix, vel, rate_in, index, weight, flux, col0, col1, row0, row1,
+    state, prev, mix, vel, rate_in, index, weight, flux, col0a, col0b, col1, row0, row1,
     before, before_side, unit, unit_side, inverse_out, fluxes,
 ):
     is_atmosphere = lax.axis_index("comp") == 0
-    west, east = column_messages(col0, col1)
+    west, east = column_messages((col0a, col0b), col1)
     north, south = row_messages(row0, row1)
     at_lat = lax.axis_index("lat")
     sub = sublanes()
@@ -327,7 +321,7 @@
 
 
 def second_step_kernel(
-    mix, vel, rate_in, index, weight, col0, col1, row0, row1,
+    mix, vel, rate_in, index, weight, col0a, col0b, col1, row0, row1,
     before, before_side, unit, unit_side, inverse, fluxes, new_state, series, force, force_side, force1,
 ):
     is_atmosphere = lax.axis_index("comp") == 0
@@ -347,7 +341,7 @@
         rate = rate_in[...]
         force[0:ROWS] = rate * regrid_tile(tables[0], index, weight)
         force1[...] = rate * regrid_tile(tables[5], index, weight)
-        west, east = column_messages(col0, col1)
+        west, east = column_messages((col0a, col0b), col1)
         north, south = row_messages(row0, row1)
 
         def of_rows(message, table, place):
@@ -391,10 +385,9 @@
     series[1] = jnp.where(is_atmosphere, tables[5], solved[0])
 
 
-def call(kernel, name, shapes, *args, scratch=(), place=pltpu.VMEM):
+def call(kernel, shapes, *args, scratch=(), place=pltpu.VMEM):
     return pl.pallas_call(
         kernel,
-        name=name,
         out_shape=[s if hasattr(s, "dtype") else jax.ShapeDtypeStruct(s, jnp.float32) for s in shapes],
         in_specs=[pl.BlockSpec(memory_space=place)] * len(args),
         out_specs=[pl.BlockSpec(memory_space=pltpu.VMEM)] * len(shapes),
@@ -404,9 +397,9 @@
     )(*args)
 
 
-def pairs(count, start, wrap):
+def pairs(count, start, wrap, step=2):
     found = []
-    for i in range(start, count, 2):
+    for i in range(start, count, step):
         j = i + 1
         if j < count or wrap:
             found += [(i, j % count), (j % count, i)]
@@ -429,30 +422,32 @@
     tile = (ROWS, COLS)
     column_shape = (COL_MESSAGE, COLS)
     to_near, to_far, flux, rate, state, prev, mix, vel, index, weight = call(
-        pack_columns_kernel, "pack_columns",
+        pack_columns_kernel,
         [column_shape, column_shape, tile, tile, state, prev, mix, vel, index, weight],
         *(pltpu.with_memory_space_constraint(x, pltpu.HBM) for x in given), place=pltpu.HBM,
         scratch=[pltpu.VMEM(tile, couple.dtype), pltpu.VMEM(tile, mask.dtype), pltpu.SemaphoreType.DMA((8,))],
     )
+    early = lax.ppermute(to_near, "lon", pairs(n_lon, 0, True, 4))
     col1 = lax.ppermute(to_far, "lon", pairs(n_lon, 1, True))
-    col0 = lax.all_gather(to_near, "lon", axis_index_groups=partners(n_lon))
+    late = lax.ppermute(to_near, "lon", pairs(n_lon, 2, True, 4))
+    col0 = (early, late)
     row_shape = (ROW_MESSAGE, COLS)
     to_near, to_far = call(
-        pack_rows_kernel, "pack_rows", [row_shape, row_shape],
-        state, mix, vel, rate, index, weight, flux, col0, col1,
+        pack_rows_kernel, [row_shape, row_shape],
+        state, mix, vel, rate, index, weight, flux, *col0, col1,
     )
     row1 = lax.ppermute(to_far, "lat", pairs(n_lat, 1, False))
     row0 = lax.all_gather(to_near, "lat", axis_index_groups=partners(n_lat))
     wide, narrow = (LEV, 24, COLS), (LEV, ROWS, COLS)
     *parts, fluxes = call(
-        first_step_kernel, "first_step",
+        first_step_kernel,
         [wide, narrow, wide, narrow, narrow, (6 * ROWS, COLS)],
-        state, prev, mix, vel, rate, index, weight, flux, col0, col1, row0, row1,
+        state, prev, mix, vel, rate, index, weight, flux, *col0, col1, row0, row1,
     )
     fluxes = lax.all_gather(fluxes, "comp")
     new_state, series = call(
-        second_step_kernel, "second_step", [(LEV, ROWS, COLS), (NSTEP, ROWS, COLS)],
-        mix, vel, rate, index, weight, col0, col1, row0, row1, *parts, fluxes,
+        second_step_kernel, [(LEV, ROWS, COLS), (NSTEP, ROWS, COLS)],
+        mix, vel, rate, index, weight, *col0, col1, row0, row1, *parts, fluxes,
         scratch=[pltpu.VMEM(shape, jnp.float32) for shape in ((24, COLS), tile, tile)],
     )
     return new_state[None], series[None]
@@ -470,6 +465,7 @@
         P("comp", None, "lat", "lon"),
     )
     out_specs = (P("comp", None, "lat", "lon"), P("comp", None, "lat", "lon"))
+
     return jax.shard_map(
         per_device, mesh=mesh, in_specs=in_specs, out_specs=out_specs, check_vma=False
     )

time: 34.8 us -> 36.7 us (1.055)
  blocking collectives: 12.4 us -> 7.08 us
  waiting for transfers between devices: 2.5 us -> 7.09 us
  starting transfers between devices: 15.1 us -> 17.6 us
    all_gather x1 -> x0, blocking collectives: 5.31 us -> none  [per_device(): col0 = lax.all_gather(to_near, 'lon', axis_index_groups=partners(n_lon))]
    ppermute x0 -> x2, waiting for transfers between devices: none -> 4.58 us  [the longest x1 4.58 us: per_device(): early = lax.ppermute(to_near, 'lon', pairs(n_lon, 0, True, 4))]
    ppermute x0 -> x2, starting transfers between devices: none -> 2.58 us  [the longest x1 1.92 us: per_device(): early = lax.ppermute(to_near, 'lon', pairs(n_lon, 0, True, 4))]
  transfers between devices with their start and end apart: 2 -> 4, of which waited for: 1 -> 2; matrix products, arithmetic and copies ran while one was open for 0% -> 0% of each run, Pallas kernels for 0% -> 0%
where the time goes in v4:
time: 36.7 us; the launch traced here: 36.5 us
  starting transfers between devices  17.6 us (48%)
  waiting for transfers between devices  7.09 us (19%)
  blocking collectives  7.08 us (19%)
  Pallas kernels  4.02 us (11%)
  between operations  0.7 us (2%)
    ppermute x1, starting transfers between devices, per_device(): col1 = lax.ppermute(to_far, 'lon', pairs(n_lon, 1, True))  13.1 us
    all_gather x1, blocking collectives, per_device(): fluxes = lax.all_gather(fluxes, 'comp')  4.76 us
    ppermute x1, waiting for transfers between devices, per_device(): early = lax.ppermute(to_near, 'lon', pairs(n_lon, 0, True, 4))  4.58 us
    pallas_call x4, Pallas kernels, call(): pl.pallas_call(kernel, out_shape=[s if hasattr(s, 'dtype') else jax.Shape...  4.02 us
    ppermute x1, waiting for transfers between devices, per_device(): row1 = lax.ppermute(to_far, 'lat', pairs(n_lat, 1, False))  2.5 us
    all_gather x1, blocking collectives, per_device(): row0 = lax.all_gather(to_near, 'lat', axis_index_groups=partners(n_lat))  2.32 us
    ppermute x1, starting transfers between devices, per_device(): early = lax.ppermute(to_near, 'lon', pairs(n_lon, 0, True, 4))  1.92 us
    ppermute x1, starting transfers between devices, per_device(): row1 = lax.ppermute(to_far, 'lat', pairs(n_lat, 1, False))  1.92 us
  transfers between devices with their start and end apart: 4, of which 2 were waited for; matrix products, arithmetic and copies ran while one was open for 0% of the time, Pallas kernels for 0%

profile of v4, /device:TPU:32, one launch (start us, length us, event | category | flops | bytes accessed | tf_op | source)
XLA Modules:
  0.0 36.5 jit_solution(3881733613170301894)
XLA Ops:
  0.6 1.5 %shard_map.95 = (f32[32,128]{1,0:T(8,128)S(1)}, f32[32,128]{1,0:T(8,128)S(1)}, f32[16,128]{1,0:T(8,128)S(1)}, f32[16,128]{1,0:T(8,128)S(1)}, f32[12,16,128]{2,1,...) custom-call(f32[12,16,128]{2,1,0:T(8,128)} %bitcast.14, ...), custom_call_target="tpu_custom_call" | custom-call | tf_op jit(solution)/shard_map/pallas_call | solution.py:389
  2.1 13.1 %collective-permute-start.2 = (f32[32,128]{1,0:T(8,128)S(1)}, f32[32,128]{1,0:T(8,128)S(1)}, u32[]{:S(2)}, u32[]{:S(2)}) collective-permute-start(f32[32,128]{1,0:T(8,128)S(1)} %get-tuple-element.28), channel_id=1, source_target_pairs={{1,2},{2,1},{3,4},{4,3},{5,6},{6,5},{7,8},{8,7},{9,10},{10,9},{11,... | collective-permute-start | bytes 49160 | tf_op jit(solution)/shard_map/ppermute | solution.py:431
  15.3 0.7 %collective-permute-start.1 = (f32[32,128]{1,0:T(8,128)S(1)}, f32[32,128]{1,0:T(8,128)S(1)}, u32[]{:S(2)}, u32[]{:S(2)}) collective-permute-start(f32[32,128]{1,0:T(8,128)S(1)} %get-tuple-element.27), channel_id=1, source_target_pairs={{2,3},{3,2},{6,7},{7,6},{10,11},{11,10},{14,15},{15,14},{18,19},{1... | collective-permute-start | bytes 49160 | tf_op jit(solution)/shard_map/ppermute | solution.py:432
  15.9 1.9 %collective-permute-start = (f32[32,128]{1,0:T(8,128)S(1)}, f32[32,128]{1,0:T(8,128)S(1)}, u32[]{:S(2)}, u32[]{:S(2)}) collective-permute-start(f32[32,128]{1,0:T(8,128)S(1)} %get-tuple-element.27), channel_id=1, source_target_pairs={{0,1},{1,0},{4,5},{5,4},{8,9},{9,8},{12,13},{13,12},{16,17},{17,16... | collective-permute-start | bytes 49160 | tf_op jit(solution)/shard_map/ppermute | solution.py:430
  17.8 0.0 collective-permute-done.2.got1.col1
  17.9 0.0 collective-permute-done.1.got0b.col0b
  17.9 4.6 %collective-permute-done.got0a.col0a = f32[32,128]{1,0:T(8,128)S(1)} collective-permute-done((f32[32,128]{1,0:T(8,128)S(1)}, f32[32,128]{1,0:T(8,128)S(1)}, u32[]{:S(2)}, u32[]{:S(2)}) %collective-permute-start) | collective-permute-done | bytes 16416 | tf_op jit(solution)/shard_map/ppermute | solution.py:430
  22.5 1.9 %collective-permute-start.3 = (f32[120,128]{1,0:T(8,128)S(1)}, f32[120,128]{1,0:T(8,128)S(1)}, u32[]{:S(2)}, u32[]{:S(2)}) collective-permute-start(f32[120,128]{1,0:T(8,128)S(1)} %get-tuple-element.32), channel_id=1, source_target_pairs={{16,32},{32,16},{48,64},{64,48},{80,96},{96,80},{112,128},{128,112... | collective-permute-start | bytes 184328 | tf_op jit(solution)/shard_map/ppermute | solution.py:439
  24.4 2.3 %all-gather = f32[240,128]{1,0:T(8,128)S(1)} all-gather(f32[120,128]{1,0:T(8,128)S(1)} %get-tuple-element.31), channel_id=2, replica_groups={{0,16},{32,48},{64,80},{96,112},{128,144},{160,176},{192,208},{224,240}..., dimensions={0}, use_global_device_ids=true | all-gather | bytes 184320 | tf_op jit(solution)/shard_map/all_gather | solution.py:440
  26.7 2.5 %collective-permute-done.3.row1 = f32[120,128]{1,0:T(8,128)S(1)} collective-permute-done((f32[120,128]{1,0:T(8,128)S(1)}, f32[120,128]{1,0:T(8,128)S(1)}, u32[]{:S(2)}, u32[]{:S(2)}) %collective-permute-start.3) | collective-permute-done | bytes 61472 | tf_op jit(solution)/shard_map/ppermute | solution.py:439
  29.2 1.5 %shard_map.97 = (f32[12,24,128]{2,1,0:T(8,128)S(1)}, f32[12,16,128]{2,1,0:T(8,128)S(1)}, f32[12,24,128]{2,1,0:T(8,128)S(1)}, f32[12,16,128]{2,1,0:T(8,128)S(1)},...) custom-call(f32[12,16,128]{2,1,0:T(8,128)S(1)} %get-tuple-element.29.state, f32[2,16,128]{2,1,0:T(8,128)S(1)} %get-tuple-element.33.prev, ...), custom_call_target="tpu_custom_call" | custom-call | tf_op jit(solution)/shard_map/pallas_call | solution.py:389
  30.8 4.8 %all-gather.1 = f32[192,128]{1,0:T(8,128)S(1)} all-gather(f32[96,128]{1,0:T(8,128)S(1)} %get-tuple-element.39), channel_id=3, replica_groups=mesh['comp'=2,'lat'=16,'lon'=16] {'comp'}, dimensions={0}, use_global_device_ids=true | all-gather | bytes 147456 | tf_op jit(solution)/shard_map/all_gather | solution.py:447
  35.6 1.0 %shard_map.98 = (f32[12,16,128]{2,1,0:T(8,128)}, f32[2,16,128]{2,1,0:T(8,128)}) custom-call(f32[11,16,128]{2,1,0:T(8,128)S(1)} %get-tuple-element.22.mix, f32[2,16,128]{2,1,0:T(8,128)S(1)} %get-tuple-element.23.vel, f32[16,128]{1,0:T(8,128)S(1)} %get-tuple-element.24.rate_in, s32[4,16,128]{2,1,0:T(8,128)S(1)} %get-tuple-element.25.index, ...), custom_call_target="tpu_custom_call" | custom-call | tf_op jit(solution)/shard_map/pallas_call | solution.py:389
  (1 shorter events, 0.0 us)
Async XLA Ops:
  2.1 15.7 %collective-permute-start.2 = (f32[32,128]{1,0:T(8,128)S(1)}, f32[32,128]{1,0:T(8,128)S(1)}, u32[]{:S(2)}, u32[]{:S(2)}) collective-permute-start(f32[32,128]{1,0:T(8,128)S(1)} %get-tuple-element.28), channel_id=1, source_target_pairs={{1,2},{2,1},{3,4},{4,3},{5,6},{6,5},{7,8},{8,7},{9,10},{10,9},{11,... | collective-permute-start | bytes 49160 | tf_op jit(solution)/shard_map/ppermute | solution.py:431
  15.3 2.6 %collective-permute-start.1 = (f32[32,128]{1,0:T(8,128)S(1)}, f32[32,128]{1,0:T(8,128)S(1)}, u32[]{:S(2)}, u32[]{:S(2)}) collective-permute-start(f32[32,128]{1,0:T(8,128)S(1)} %get-tuple-element.27), channel_id=1, source_target_pairs={{2,3},{3,2},{6,7},{7,6},{10,11},{11,10},{14,15},{15,14},{18,19},{1... | collective-permute-start | bytes 49160 | tf_op jit(solution)/shard_map/ppermute | solution.py:432
  15.9 6.5 %collective-permute-start = (f32[32,128]{1,0:T(8,128)S(1)}, f32[32,128]{1,0:T(8,128)S(1)}, u32[]{:S(2)}, u32[]{:S(2)}) collective-permute-start(f32[32,128]{1,0:T(8,128)S(1)} %get-tuple-element.27), channel_id=1, source_target_pairs={{0,1},{1,0},{4,5},{5,4},{8,9},{9,8},{12,13},{13,12},{16,17},{17,16... | collective-permute-start | bytes 49160 | tf_op jit(solution)/shard_map/ppermute | solution.py:430
  22.5 6.8 %collective-permute-start.3 = (f32[120,128]{1,0:T(8,128)S(1)}, f32[120,128]{1,0:T(8,128)S(1)}, u32[]{:S(2)}, u32[]{:S(2)}) collective-permute-start(f32[120,128]{1,0:T(8,128)S(1)} %get-tuple-element.32), channel_id=1, source_target_pairs={{16,32},{32,16},{48,64},{64,48},{80,96},{96,80},{112,128},{128,112... | collective-permute-start | bytes 184328 | tf_op jit(solution)/shard_map/ppermute | solution.py:439

commit v5 on v4

--- a/solution.py
+++ b/solution.py
@@ -18,10 +18,10 @@
 AT_RATE = AT_VEL + 4
 AT_WEIGHT = 80
 AT_INDEX = 88
+AT_FLUX = AT_WEIGHT
 AT_WEST = 96
 AT_EAST = 100
-AT_FLUX = 104
-ROW_MESSAGE = AT_FLUX + ROWS
+ROW_MESSAGE = 104
 COL_MESSAGE = 2 * ROWS
 
 
@@ -130,19 +130,20 @@
         msg1[ROWS:] = nothing
 
 
-def column_messages(got0, got1):
+def column_messages(got):
     at_lon = lax.axis_index("lon")
     odd = lax.rem(at_lon, 2) == 1
-    near = jnp.where(lax.rem(at_lon, 4) < 2, got0[0][...], got0[1][...])
-    far = got1[...]
+    starts_early = lax.rem(at_lon, 4) < 2
+    near = jnp.where(starts_early, got[0][...], got[1][...])
+    far = jnp.where(starts_early, got[2][...], got[3][...])
     return jnp.where(odd, near, far), jnp.where(odd, far, near)
 
 
 def pack_rows_kernel(
-    state, mix, vel, rate_in, index, weight, flux, got0a, got0b, got1, msg0, msg1
+    state, mix, vel, rate_in, index, weight, flux, early, late, to_early, to_late, msg0, msg1
 ):
     odd = lax.rem(lax.axis_index("lat"), 2) == 1
-    west, east = column_messages((got0a, got0b), got1)
+    west, east = column_messages((early, late, to_early, to_late))
     rate = rate_in[...]
 
     def put(x, at, width):
@@ -157,16 +158,23 @@
     for part in range(2):
         put(vel[part], AT_VEL + 2 * part, 2)
     put(rate, AT_RATE, 2)
-    for j in range(4):
-        put(weight[j], AT_WEIGHT + 2 * j, 2)
-        put(index[j].astype(jnp.float32), AT_INDEX + 2 * j, 2)
+
+    @pl.when(lax.axis_index("comp") == 0)
+    def _():
+        msg0[AT_FLUX : AT_FLUX + ROWS] = flux[...]
+        msg1[AT_FLUX : AT_FLUX + ROWS] = flux[...]
+
+    @pl.when(lax.axis_index("comp") != 0)
+    def _():
+        for j in range(4):
+            put(weight[j], AT_WEIGHT + 2 * j, 2)
+            put(index[j].astype(jnp.float32), AT_INDEX + 2 * j, 2)
+
     put(west[0:ROWS], AT_WEST, 4)
     put(east[0:ROWS], AT_EAST, 4)
     for at in (AT_RATE + 2, AT_RATE + 4):
         msg0[at : at + 2] = jnp.zeros((2, COLS), jnp.float32)
         msg1[at : at + 2] = jnp.zeros((2, COLS), jnp.float32)
-    msg0[AT_FLUX:] = flux[...]
-    msg1[AT_FLUX:] = flux[...]
 
 
 def row_messages(got0, got1):
@@ -234,21 +242,64 @@
     return result
 
 
+def rim_of_levels(north, south, level):
+    sub, block, odd = sublanes(), 8 * (level // 2), level % 2
+    a, b = south[block : block + 8], north[block : block + 8]
+    return jnp.where(sub < 4, roll(a, -4 * odd, 0), roll(b, 4 - 4 * odd, 0))
+
+
+def side_of(west_tile, east_tile, at, width, rows):
+    lane = lanes(rows)
+    a, b = roll(east_tile[:rows], -at, 1), roll(west_tile[:rows], COLS - width - at, 1)
+    return jnp.where(lane < width, a, jnp.where(lane >= COLS - width, b, 0.0))
+
+
+def prepare_kernel(prev, mix, index, weight, inverse_out, unit_top, seen):
+    inverses, ratios = factors([mix[level] for level in range(LEV - 1)])
+    for level in range(LEV):
+        inverse_out[level] = inverses[level]
+    own_mix = [mix[level] for level in range(LEV - 1)]
+    unit_top[...] = solve([1.0] + [None] * (LEV - 1), own_mix, inverses, ratios)[0]
+
+    @pl.when(lax.axis_index("comp") == 0)
+    def _():
+        seen[...] = regrid_tile(prev[1], index, weight)
+
+
+def top_kernel(
+    state, mix, vel, rate, flux, early, late, to_early, to_late, row0, row1, inverse, unit_top, seen,
+    fluxes,
+):
+    @pl.when(lax.axis_index("comp") == 0)
+    def _():
+        west, east = column_messages((early, late, to_early, to_late))
+        north, south = row_messages(row0, row1)
+        weights = transport_weights(vel[0], vel[1])
+        moved = []
+        for level in range(LEV):
+            own = jnp.concatenate([state[level], rim_of_levels(north, south, level)], axis=0)
+            there = side_of(west[0:ROWS], east[0:ROWS], 4 * level, 4, ROWS)
+            moved.append(horizontal(own, there, weights, None, ROWS)[0])
+        own_mix = [mix[level] for level in range(LEV - 1)]
+        inverses = [inverse[level] for level in range(LEV)]
+        ratios = [own_mix[level] * inverses[level] for level in range(LEV - 1)]
+        top = solve(moved, own_mix, inverses, ratios)[0] + flux[...] * unit_top[...]
+        fluxes[0:ROWS] = flux[...]
+        fluxes[ROWS : 2 * ROWS] = west[ROWS:]
+        fluxes[2 * ROWS : 3 * ROWS] = east[ROWS:]
+        fluxes[3 * ROWS : 4 * ROWS] = north[AT_FLUX : AT_FLUX + ROWS]
+        fluxes[4 * ROWS : 5 * ROWS] = south[AT_FLUX : AT_FLUX + ROWS]
+        fluxes[5 * ROWS :] = rate[...] * (seen[...] - top)
+
+
 def first_step_kernel(
-    state, prev, mix, vel, rate_in, index, weight, flux, col0a, col0b, col1, row0, row1,
-    before, before_side, unit, unit_side, inverse_out, fluxes,
+    state, mix, vel, early, late, to_early, to_late, row0, row1, before, before_side, unit, unit_side,
 ):
-    is_atmosphere = lax.axis_index("comp") == 0
-    west, east = column_messages((col0a, col0b), col1)
+    west, east = column_messages((early, late, to_early, to_late))
     north, south = row_messages(row0, row1)
     at_lat = lax.axis_index("lat")
     sub = sublanes()
     valid = ((sub < 4) & (at_lat < lax.axis_size("lat") - 1)) | ((sub >= 4) & (at_lat > 0))
-
-    def rim4(level):
-        block, odd = 8 * (level // 2), level % 2
-        a, b = south[block : block + 8], north[block : block + 8]
-        return jnp.where(sub < 4, roll(a, -4 * odd, 0), roll(b, 4 - 4 * odd, 0))
 
     def rim2(at):
         block, offset = 8 * (at // 8), at % 8
@@ -265,12 +316,9 @@
         return jnp.concatenate([packed[0:ROWS], rim], axis=0)
 
     west_tile, east_tile = cornered(west, AT_WEST), cornered(east, AT_EAST)
-    wide = lanes(24)
 
     def side(at, width, rows):
-        a, b = roll(east_tile[:rows], -at, 1), roll(west_tile[:rows], COLS - width - at, 1)
-        lane = wide[:rows]
-        return jnp.where(lane < width, a, jnp.where(lane >= COLS - width, b, 0.0))
+        return side_of(west_tile, east_tile, at, width, rows)
 
     def extended(x, rim):
         return jnp.concatenate([x, rim], axis=0)
@@ -283,35 +331,17 @@
 
     moved, moved_side = [], []
     for level in range(LEV):
-        own = extended(state[level], rim4(level))
+        own = extended(state[level], rim_of_levels(north, south, level))
         a, b = horizontal(own, side(4 * level, 4, 24), own_weights, side_weights, 24)
         moved.append(a)
         moved_side.append(b)
     inverses, ratios = factors(own_mix)
     solved = solve(moved, own_mix, inverses, ratios)
     impulse = solve([1.0] + [None] * (LEV - 1), own_mix, inverses, ratios)
-    rate = rate_in[...]
-
-    fluxes[0:ROWS] = flux[...]
-    fluxes[ROWS : 2 * ROWS] = west[ROWS:]
-    fluxes[2 * ROWS : 3 * ROWS] = east[ROWS:]
-    fluxes[3 * ROWS : 4 * ROWS] = north[AT_FLUX:]
-    fluxes[4 * ROWS : 5 * ROWS] = south[AT_FLUX:]
-
-    @pl.when(is_atmosphere)
-    def _():
-        top = solved[0][:ROWS] + flux[...] * impulse[0][:ROWS]
-        fluxes[5 * ROWS :] = rate * (regrid_tile(prev[1], index, weight) - top)
-
-    @pl.when(jnp.logical_not(is_atmosphere))
-    def _():
-        fluxes[5 * ROWS :] = jnp.zeros((ROWS, COLS), jnp.float32)
-
     for level in range(LEV):
         for out, values in ((before, solved), (unit, impulse)):
             out[level, 0:ROWS] = values[level][:ROWS]
             out[level, ROWS:] = jnp.where(valid, values[level][ROWS:], 0.0)
-        inverse_out[level] = inverses[level][:ROWS]
     inverses, ratios = factors(side_mix)
     solved = solve(moved_side, side_mix, inverses, ratios)
     impulse = solve([1.0] + [None] * (LEV - 1), side_mix, inverses, ratios)
@@ -321,16 +351,16 @@
 
 
 def second_step_kernel(
-    mix, vel, rate_in, index, weight, col0a, col0b, col1, row0, row1,
-    before, before_side, unit, unit_side, inverse, fluxes, new_state, series, force, force_side, force1,
+    mix, vel, rate_in, index, weight, early, late, to_early, to_late, row0, row1,
+    before, before_side, unit, unit_side, inverse, sent, got, new_state, series, force, force_side, force1,
 ):
     is_atmosphere = lax.axis_index("comp") == 0
     sub = sublanes()
     lane = lanes(ROWS)
-    tables = [fluxes[0, k * ROWS : (k + 1) * ROWS] for k in range(6)]
 
     @pl.when(is_atmosphere)
     def _():
+        tables = [sent[k * ROWS : (k + 1) * ROWS] for k in range(6)]
         force[0:ROWS] = tables[0]
         force[ROWS:] = jnp.where(sub < 4, tables[4][0:8], tables[3][8:16])
         force_side[...] = jnp.where(lane < 64, tables[2], tables[1])
@@ -338,10 +368,11 @@
 
     @pl.when(jnp.logical_not(is_atmosphere))
     def _():
+        tables = [got[k * ROWS : (k + 1) * ROWS] for k in range(6)]
         rate = rate_in[...]
         force[0:ROWS] = rate * regrid_tile(tables[0], index, weight)
         force1[...] = rate * regrid_tile(tables[5], index, weight)
-        west, east = column_messages((col0a, col0b), col1)
+        west, east = column_messages((early, late, to_early, to_late))
         north, south = row_messages(row0, row1)
 
         def of_rows(message, table, place):
@@ -381,8 +412,8 @@
     solved = solve(moved, own_mix, inverses, ratios)
     for level in range(LEV):
         new_state[level] = solved[level]
-    series[0] = jnp.where(is_atmosphere, tables[0], top)
-    series[1] = jnp.where(is_atmosphere, tables[5], solved[0])
+    series[0] = jnp.where(is_atmosphere, f[:ROWS], top)
+    series[1] = jnp.where(is_atmosphere, force1[...], solved[0])
 
 
 def call(kernel, shapes, *args, scratch=(), place=pltpu.VMEM):
@@ -397,13 +428,8 @@
     )(*args)
 
 
-def pairs(count, start, wrap, step=2):
-    found = []
-    for i in range(start, count, step):
-        j = i + 1
-        if j < count or wrap:
-            found += [(i, j % count), (j % count, i)]
-    return found
+def pairs(count, start, step):
+    return [pair for i in range(start, count - 1, step) for pair in ((i, i + 1), (i + 1, i))]
 
 
 def partners(count):
@@ -427,27 +453,34 @@
         *(pltpu.with_memory_space_constraint(x, pltpu.HBM) for x in given), place=pltpu.HBM,
         scratch=[pltpu.VMEM(tile, couple.dtype), pltpu.VMEM(tile, mask.dtype), pltpu.SemaphoreType.DMA((8,))],
     )
-    early = lax.ppermute(to_near, "lon", pairs(n_lon, 0, True, 4))
-    col1 = lax.ppermute(to_far, "lon", pairs(n_lon, 1, True))
-    late = lax.ppermute(to_near, "lon", pairs(n_lon, 2, True, 4))
-    col0 = (early, late)
+    joints = range(1, n_lon, 2)
+    sent = [((i, (i + 1) % n_lon) if i % 4 == 3 else (i + 1, i)) for i in joints]
+    to_early = lax.ppermute(to_far, "lon", sent)
+    early = lax.ppermute(to_near, "lon", pairs(n_lon, 0, 4))
+    to_late = lax.ppermute(to_far, "lon", [(j, i) for i, j in sent])
+    late = lax.ppermute(to_near, "lon", pairs(n_lon, 2, 4))
+    columns = (early, late, to_early, to_late)
     row_shape = (ROW_MESSAGE, COLS)
     to_near, to_far = call(
         pack_rows_kernel, [row_shape, row_shape],
-        state, mix, vel, rate, index, weight, flux, *col0, col1,
-    )
-    row1 = lax.ppermute(to_far, "lat", pairs(n_lat, 1, False))
+        state, mix, vel, rate, index, weight, flux, *columns,
+    )
+    row1 = lax.ppermute(to_far, "lat", pairs(n_lat, 1, 2))
     row0 = lax.all_gather(to_near, "lat", axis_index_groups=partners(n_lat))
     wide, narrow = (LEV, 24, COLS), (LEV, ROWS, COLS)
-    *parts, fluxes = call(
-        first_step_kernel,
-        [wide, narrow, wide, narrow, narrow, (6 * ROWS, COLS)],
-        state, prev, mix, vel, rate, index, weight, flux, *col0, col1, row0, row1,
-    )
-    fluxes = lax.all_gather(fluxes, "comp")
+    inverse, unit_top, seen = call(prepare_kernel, [narrow, tile, tile], prev, mix, index, weight)
+    (fluxes,) = call(
+        top_kernel, [(6 * ROWS, COLS)],
+        state, mix, vel, rate, flux, *columns, row0, row1, inverse, unit_top, seen,
+    )
+    got = lax.ppermute(fluxes, "comp", [(0, 1)])
+    parts = call(
+        first_step_kernel, [wide, narrow, wide, narrow],
+        state, mix, vel, *columns, row0, row1,
+    )
     new_state, series = call(
         second_step_kernel, [(LEV, ROWS, COLS), (NSTEP, ROWS, COLS)],
-        mix, vel, rate, index, weight, *col0, col1, row0, row1, *parts, fluxes,
+        mix, vel, rate, index, weight, *columns, row0, row1, *parts, inverse, fluxes, got,
         scratch=[pltpu.VMEM(shape, jnp.float32) for shape in ((24, COLS), tile, tile)],
     )
     return new_state[None], series[None]

time: 36.7 us -> 41.8 us (1.14)
  the two profiles are of different devices: /device:TPU:32 before, /device:TPU:96 now
where the time goes in v5:
time: 41.8 us; the launch traced here: 41.5 us
  starting transfers between devices  19.8 us (47%)
  waiting for transfers between devices  14.3 us (34%)
  Pallas kernels  4.32 us (10%)
  blocking collectives  2.31 us (6%)
  between operations  0.73 us (2%)
    ppermute x1, starting transfers between devices, per_device(): to_late = lax.ppermute(to_far, 'lon', [(j, i) for i, j in sent])  8.59 us
    ppermute x1, waiting for transfers between devices, per_device(): to_early = lax.ppermute(to_far, 'lon', sent)  8.43 us
    ppermute x1, starting transfers between devices, per_device(): early = lax.ppermute(to_near, 'lon', pairs(n_lon, 0, 4))  6.09 us
    pallas_call x6, Pallas kernels, call(): pl.pallas_call(kernel, out_shape=[s if hasattr(s, 'dtype') else jax.Shape...  4.32 us
    ppermute x1, waiting for transfers between devices, per_device(): got = lax.ppermute(fluxes, 'comp', [(0, 1)])  3.52 us
    all_gather x1, blocking collectives, per_device(): row0 = lax.all_gather(to_near, 'lat', axis_index_groups=partners(n_lat))  2.31 us
    ppermute x1, waiting for transfers between devices, per_device(): row1 = lax.ppermute(to_far, 'lat', pairs(n_lat, 1, 2))  2.27 us
    ppermute x1, starting transfers between devices, per_device(): row1 = lax.ppermute(to_far, 'lat', pairs(n_lat, 1, 2))  1.92 us
  transfers between devices with their start and end apart: 6, of which 4 were waited for; matrix products, arithmetic and copies ran while one was open for 0% of the time, Pallas kernels for 3%

profile of v5, /device:TPU:96, one launch (start us, length us, event | category | flops | bytes accessed | tf_op | source)
XLA Modules:
  0.0 41.5 jit_solution(11401223732852606113)
XLA Ops:
  0.6 1.2 %shard_map.95 = (f32[32,128]{1,0:T(8,128)S(1)}, f32[32,128]{1,0:T(8,128)S(1)}, f32[16,128]{1,0:T(8,128)S(1)}, f32[16,128]{1,0:T(8,128)S(1)}, f32[12,16,128]{2,1,...) custom-call(f32[12,16,128]{2,1,0:T(8,128)} %bitcast.13, ...), custom_call_target="tpu_custom_call" | custom-call | tf_op jit(solution)/shard_map/pallas_call | solution.py:420
  1.9 0.7 %collective-permute-start.1 = (f32[32,128]{1,0:T(8,128)S(1)}, f32[32,128]{1,0:T(8,128)S(1)}, u32[]{:S(2)}, u32[]{:S(2)}) collective-permute-start(f32[32,128]{1,0:T(8,128)S(1)} %get-tuple-element.28), channel_id=1, source_target_pairs={{2,3},{3,2},{6,7},{7,6},{10,11},{11,10},{14,15},{15,14},{18,19},{1... | collective-permute-start | bytes 49160 | tf_op jit(solution)/shard_map/ppermute | solution.py:461
  2.5 6.1 %collective-permute-start = (f32[32,128]{1,0:T(8,128)S(1)}, f32[32,128]{1,0:T(8,128)S(1)}, u32[]{:S(2)}, u32[]{:S(2)}) collective-permute-start(f32[32,128]{1,0:T(8,128)S(1)} %get-tuple-element.28), channel_id=1, source_target_pairs={{0,1},{1,0},{4,5},{5,4},{8,9},{9,8},{12,13},{13,12},{16,17},{17,16... | collective-permute-start | bytes 49160 | tf_op jit(solution)/shard_map/ppermute | solution.py:459
  8.6 8.6 %collective-permute-start.3 = (f32[32,128]{1,0:T(8,128)S(1)}, f32[32,128]{1,0:T(8,128)S(1)}, u32[]{:S(2)}, u32[]{:S(2)}) collective-permute-start(f32[32,128]{1,0:T(8,128)S(1)} %get-tuple-element.29), channel_id=1, source_target_pairs={{1,2},{4,3},{5,6},{8,7},{9,10},{12,11},{13,14},{0,15},{17,18},{20,... | collective-permute-start | bytes 49160 | tf_op jit(solution)/shard_map/ppermute | solution.py:460
  17.2 1.3 %collective-permute-start.2 = (f32[32,128]{1,0:T(8,128)S(1)}, f32[32,128]{1,0:T(8,128)S(1)}, u32[]{:S(2)}, u32[]{:S(2)}) collective-permute-start(f32[32,128]{1,0:T(8,128)S(1)} %get-tuple-element.29), channel_id=1, source_target_pairs={{2,1},{3,4},{6,5},{7,8},{10,9},{11,12},{14,13},{15,0},{18,17},{19,... | collective-permute-start | bytes 49160 | tf_op jit(solution)/shard_map/ppermute | solution.py:458
  18.5 0.0 collective-permute-done.1.late
  18.6 0.0 collective-permute-done.early
  18.6 0.1 collective-permute-done.3.to_late
  18.7 8.4 %collective-permute-done.2.to_early = f32[32,128]{1,0:T(8,128)S(1)} collective-permute-done((f32[32,128]{1,0:T(8,128)S(1)}, f32[32,128]{1,0:T(8,128)S(1)}, u32[]{:S(2)}, u32[]{:S(2)}) %collective-permute-start.2) | collective-permute-done | bytes 16416 | tf_op jit(solution)/shard_map/ppermute | solution.py:458
  27.1 1.9 %collective-permute-start.4 = (f32[104,128]{1,0:T(8,128)S(1)}, f32[104,128]{1,0:T(8,128)S(1)}, u32[]{:S(2)}, u32[]{:S(2)}) collective-permute-start(f32[104,128]{1,0:T(8,128)S(1)} %get-tuple-element.33), channel_id=1, source_target_pairs={{16,32},{32,16},{48,64},{64,48},{80,96},{96,80},{112,128},{128,112... | collective-permute-start | bytes 159752 | tf_op jit(solution)/shard_map/ppermute | solution.py:468
  29.1 0.1 shard_map.98
  29.2 2.3 %all-gather = f32[208,128]{1,0:T(8,128)S(1)} all-gather(f32[104,128]{1,0:T(8,128)S(1)} %get-tuple-element.32), channel_id=2, replica_groups={{0,16},{32,48},{64,80},{96,112},{128,144},{160,176},{192,208},{224,240}..., dimensions={0}, use_global_device_ids=true | all-gather | bytes 159744 | tf_op jit(solution)/shard_map/all_gather | solution.py:469
  31.5 2.3 %collective-permute-done.4.row1 = f32[104,128]{1,0:T(8,128)S(1)} collective-permute-done((f32[104,128]{1,0:T(8,128)S(1)}, f32[104,128]{1,0:T(8,128)S(1)}, u32[]{:S(2)}, u32[]{:S(2)}) %collective-permute-start.4) | collective-permute-done | bytes 53280 | tf_op jit(solution)/shard_map/ppermute | solution.py:468
  33.8 1.3 %collective-permute-start.5 = (f32[96,128]{1,0:T(8,128)S(1)}, f32[96,128]{1,0:T(8,128)S(1)}, u32[]{:S(2)}, u32[]{:S(2)}) collective-permute-start(f32[96,128]{1,0:T(8,128)S(1)} %shard_map.99.sent), channel_id=1, source_target_pairs={{0,256},{1,257},{2,258},{3,259},{4,260},{5,261},{6,262},{7,263},{8... | collective-permute-start | bytes 147464 | tf_op jit(solution)/shard_map/ppermute | solution.py:476
  35.1 1.2 %shard_map.97 = (f32[12,24,128]{2,1,0:T(8,128)S(1)}, f32[12,16,128]{2,1,0:T(8,128)S(1)}, f32[12,24,128]{2,1,0:T(8,128)S(1)}, f32[12,16,128]{2,1,0:T(8,128)S(1)}) custom-call(f32[12,16,128]{2,1,0:T(8,128)S(1)} %get-tuple-element.30.state, f32[11,16,128]{2,1,0:T(8,128)S(1)} %get-tuple-element.23.mix, f32[2,16,128]{2,1,0:T(8,128)S(1)} %get-tuple-element.24.vel, ...), custom_call_target="tpu_custom_call" | custom-call | tf_op jit(solution)/shard_map/pallas_call | solution.py:420
  36.3 3.5 %collective-permute-done.5.got = f32[96,128]{1,0:T(8,128)S(1)} collective-permute-done((f32[96,128]{1,0:T(8,128)S(1)}, f32[96,128]{1,0:T(8,128)S(1)}, u32[]{:S(2)}, u32[]{:S(2)}) %collective-permute-start.5) | collective-permute-done | bytes 49184 | tf_op jit(solution)/shard_map/ppermute | solution.py:476
  39.8 1.7 %shard_map.100 = (f32[12,16,128]{2,1,0:T(8,128)}, f32[2,16,128]{2,1,0:T(8,128)}) custom-call(f32[11,16,128]{2,1,0:T(8,128)S(1)} %get-tuple-element.23.mix, f32[2,16,128]{2,1,0:T(8,128)S(1)} %get-tuple-element.24.vel, f32[16,128]{1,0:T(8,128)S(1)} %get-tuple-element.25.rate_in.rate, s32[4,16,128]{2,1,0:T(8,128)S(1)} %get-tuple-element.26.index, ...), custom_call_target="tpu_custom_call" | custom-call | tf_op jit(solution)/shard_map/pallas_call | solution.py:420
  (2 shorter events, 0.0 us)
Async XLA Ops:
  1.9 16.7 %collective-permute-start.1 = (f32[32,128]{1,0:T(8,128)S(1)}, f32[32,128]{1,0:T(8,128)S(1)}, u32[]{:S(2)}, u32[]{:S(2)}) collective-permute-start(f32[32,128]{1,0:T(8,128)S(1)} %get-tuple-element.28), channel_id=1, source_target_pairs={{2,3},{3,2},{6,7},{7,6},{10,11},{11,10},{14,15},{15,14},{18,19},{1... | collective-permute-start | bytes 49160 | tf_op jit(solution)/shard_map/ppermute | solution.py:461
  2.5 16.0 %collective-permute-start = (f32[32,128]{1,0:T(8,128)S(1)}, f32[32,128]{1,0:T(8,128)S(1)}, u32[]{:S(2)}, u32[]{:S(2)}) collective-permute-start(f32[32,128]{1,0:T(8,128)S(1)} %get-tuple-element.28), channel_id=1, source_target_pairs={{0,1},{1,0},{4,5},{5,4},{8,9},{9,8},{12,13},{13,12},{16,17},{17,16... | collective-permute-start | bytes 49160 | tf_op jit(solution)/shard_map/ppermute | solution.py:459
  8.6 10.0 %collective-permute-start.3 = (f32[32,128]{1,0:T(8,128)S(1)}, f32[32,128]{1,0:T(8,128)S(1)}, u32[]{:S(2)}, u32[]{:S(2)}) collective-permute-start(f32[32,128]{1,0:T(8,128)S(1)} %get-tuple-element.29), channel_id=1, source_target_pairs={{1,2},{4,3},{5,6},{8,7},{9,10},{12,11},{13,14},{0,15},{17,18},{20,... | collective-permute-start | bytes 49160 | tf_op jit(solution)/shard_map/ppermute | solution.py:460
  17.2 9.9 %collective-permute-start.2 = (f32[32,128]{1,0:T(8,128)S(1)}, f32[32,128]{1,0:T(8,128)S(1)}, u32[]{:S(2)}, u32[]{:S(2)}) collective-permute-start(f32[32,128]{1,0:T(8,128)S(1)} %get-tuple-element.29), channel_id=1, source_target_pairs={{2,1},{3,4},{6,5},{7,8},{10,9},{11,12},{14,13},{15,0},{18,17},{19,... | collective-permute-start | bytes 49160 | tf_op jit(solution)/shard_map/ppermute | solution.py:458
  27.1 6.7 %collective-permute-start.4 = (f32[104,128]{1,0:T(8,128)S(1)}, f32[104,128]{1,0:T(8,128)S(1)}, u32[]{:S(2)}, u32[]{:S(2)}) collective-permute-start(f32[104,128]{1,0:T(8,128)S(1)} %get-tuple-element.33), channel_id=1, source_target_pairs={{16,32},{32,16},{48,64},{64,48},{80,96},{96,80},{112,128},{128,112... | collective-permute-start | bytes 159752 | tf_op jit(solution)/shard_map/ppermute | solution.py:468
  33.8 6.0 %collective-permute-start.5 = (f32[96,128]{1,0:T(8,128)S(1)}, f32[96,128]{1,0:T(8,128)S(1)}, u32[]{:S(2)}, u32[]{:S(2)}) collective-permute-start(f32[96,128]{1,0:T(8,128)S(1)} %shard_map.99.sent), channel_id=1, source_target_pairs={{0,256},{1,257},{2,258},{3,259},{4,260},{5,261},{6,262},{7,263},{8... | collective-permute-start | bytes 147464 | tf_op jit(solution)/shard_map/ppermute | solution.py:476

commit v6 on v5

--- a/solution.py
+++ b/solution.py
@@ -19,8 +19,7 @@
 AT_WEIGHT = 80
 AT_INDEX = 88
 AT_FLUX = AT_WEIGHT
-AT_WEST = 96
-AT_EAST = 100
+AT_CORNER = 96
 ROW_MESSAGE = 104
 COL_MESSAGE = 2 * ROWS
 
@@ -130,20 +129,23 @@
         msg1[ROWS:] = nothing
 
 
+def starts_early():
+    return lax.rem(lax.axis_index("lon"), 4) < 2
+
+
+def sides(near, far):
+    odd = lax.rem(lax.axis_index("lon"), 2) == 1
+    return jnp.where(odd, near, far), jnp.where(odd, far, near)
+
+
 def column_messages(got):
-    at_lon = lax.axis_index("lon")
-    odd = lax.rem(at_lon, 2) == 1
-    starts_early = lax.rem(at_lon, 4) < 2
-    near = jnp.where(starts_early, got[0][...], got[1][...])
-    far = jnp.where(starts_early, got[2][...], got[3][...])
-    return jnp.where(odd, near, far), jnp.where(odd, far, near)
-
-
-def pack_rows_kernel(
-    state, mix, vel, rate_in, index, weight, flux, early, late, to_early, to_late, msg0, msg1
-):
+    early = starts_early()
+    near = jnp.where(early, got[0][...], got[1][...])
+    return sides(near, jnp.where(early, got[2][...], got[3][...]))
+
+
+def pack_rows(state, mix, vel, rate_in, index, weight, flux, near, msg0, msg1):
     odd = lax.rem(lax.axis_index("lat"), 2) == 1
-    west, east = column_messages((early, late, to_early, to_late))
     rate = rate_in[...]
 
     def put(x, at, width):
@@ -170,18 +172,38 @@
             put(weight[j], AT_WEIGHT + 2 * j, 2)
             put(index[j].astype(jnp.float32), AT_INDEX + 2 * j, 2)
 
-    put(west[0:ROWS], AT_WEST, 4)
-    put(east[0:ROWS], AT_EAST, 4)
-    for at in (AT_RATE + 2, AT_RATE + 4):
+    put(near[0:ROWS], AT_CORNER, 4)
+    for at in (AT_RATE + 2, AT_RATE + 4, AT_CORNER + 4, AT_CORNER + 6):
         msg0[at : at + 2] = jnp.zeros((2, COLS), jnp.float32)
         msg1[at : at + 2] = jnp.zeros((2, COLS), jnp.float32)
 
 
-def row_messages(got0, got1):
-    odd = lax.rem(lax.axis_index("lat"), 2)
-    near = got0[1 - odd]
-    far = got1[...]
-    return jnp.where(odd == 1, near, far), jnp.where(odd == 1, far, near)
+def pack_rows_early_kernel(*refs):
+    @pl.when(starts_early())
+    def _():
+        pack_rows(*refs)
+
+
+def pack_rows_late_kernel(*refs):
+    @pl.when(jnp.logical_not(starts_early()))
+    def _():
+        pack_rows(*refs)
+
+
+def pack_corners_kernel(to_early, to_late, msg):
+    early = starts_early()
+    sub = sublanes()
+    head = jnp.where(early, to_early[0:8], to_late[0:8])
+    tail = jnp.where(early, to_early[8:ROWS], to_late[8:ROWS])
+    msg[...] = jnp.where(sub < 4, head, tail)
+
+
+def row_messages(got):
+    early = starts_early()
+    odd = lax.rem(lax.axis_index("lat"), 2) == 1
+    near = jnp.where(early, got[0][...], got[1][...])
+    far = jnp.where(early, got[2][...], got[3][...])
+    return jnp.where(odd, near, far), jnp.where(odd, far, near)
 
 
 def transport_weights(east, north):
@@ -267,13 +289,13 @@
 
 
 def top_kernel(
-    state, mix, vel, rate, flux, early, late, to_early, to_late, row0, row1, inverse, unit_top, seen,
+    state, mix, vel, rate, flux, early, late, to_early, to_late, row0e, row0l, row1e, row1l, inverse, unit_top, seen,
     fluxes,
 ):
     @pl.when(lax.axis_index("comp") == 0)
     def _():
         west, east = column_messages((early, late, to_early, to_late))
-        north, south = row_messages(row0, row1)
+        north, south = row_messages((row0e, row0l, row1e, row1l))
         weights = transport_weights(vel[0], vel[1])
         moved = []
         for level in range(LEV):
@@ -293,10 +315,11 @@
 
 
 def first_step_kernel(
-    state, mix, vel, early, late, to_early, to_late, row0, row1, before, before_side, unit, unit_side,
+    state, mix, vel, early, late, to_early, to_late, row0e, row0l, row1e, row1l, corner0, corner1,
+    before, before_side, unit, unit_side,
 ):
     west, east = column_messages((early, late, to_early, to_late))
-    north, south = row_messages(row0, row1)
+    north, south = row_messages((row0e, row0l, row1e, row1l))
     at_lat = lax.axis_index("lat")
     sub = sublanes()
     valid = ((sub < 4) & (at_lat < lax.axis_size("lat") - 1)) | ((sub >= 4) & (at_lat > 0))
@@ -307,15 +330,13 @@
         a, b = roll(a, -offset, 0), roll(b, 6 - offset, 0)
         return jnp.where(sub < 2, a, jnp.where(sub >= 6, b, 0.0))
 
-    def cornered(packed, at):
-        a, b = south[AT_WEST : AT_WEST + 8], north[AT_WEST : AT_WEST + 8]
-        if at == AT_WEST:
-            rim = jnp.where(sub < 4, a, roll(b, 4, 0))
-        else:
-            rim = jnp.where(sub < 4, roll(a, 4, 0), b)
-        return jnp.concatenate([packed[0:ROWS], rim], axis=0)
-
-    west_tile, east_tile = cornered(west, AT_WEST), cornered(east, AT_EAST)
+    odd = lax.rem(at_lat, 2) == 1
+    near_rim = jnp.where(sub < 4, south[AT_CORNER:], roll(north[AT_CORNER:], 4, 0))
+    chip, other = corner0[1 - lax.rem(at_lat, 2)], corner1[...]
+    far_rim = jnp.where((sub < 4) == odd, other, chip)
+    west_rim, east_rim = sides(near_rim, far_rim)
+    west_tile = jnp.concatenate([west[0:ROWS], west_rim], axis=0)
+    east_tile = jnp.concatenate([east[0:ROWS], east_rim], axis=0)
 
     def side(at, width, rows):
         return side_of(west_tile, east_tile, at, width, rows)
@@ -351,7 +372,7 @@
 
 
 def second_step_kernel(
-    mix, vel, rate_in, index, weight, early, late, to_early, to_late, row0, row1,
+    mix, vel, rate_in, index, weight, early, late, to_early, to_late, row0e, row0l, row1e, row1l,
     before, before_side, unit, unit_side, inverse, sent, got, new_state, series, force, force_side, force1,
 ):
     is_atmosphere = lax.axis_index("comp") == 0
@@ -373,7 +394,7 @@
         force[0:ROWS] = rate * regrid_tile(tables[0], index, weight)
         force1[...] = rate * regrid_tile(tables[5], index, weight)
         west, east = column_messages((early, late, to_early, to_late))
-        north, south = row_messages(row0, row1)
+        north, south = row_messages((row0e, row0l, row1e, row1l))
 
         def of_rows(message, table, place):
             index8 = message[AT_INDEX : AT_INDEX + 8].astype(jnp.int32)
@@ -453,34 +474,46 @@
         *(pltpu.with_memory_space_constraint(x, pltpu.HBM) for x in given), place=pltpu.HBM,
         scratch=[pltpu.VMEM(tile, couple.dtype), pltpu.VMEM(tile, mask.dtype), pltpu.SemaphoreType.DMA((8,))],
     )
+    row_shape = (ROW_MESSAGE, COLS)
+    fields = (state, mix, vel, rate, index, weight, flux)
+
+    def exchange_rows(kernel, near, places):
+        to_near, to_far = call(kernel, [row_shape, row_shape], *fields, near)
+
+        def among(found):
+            return [(i * n_lon + k, j * n_lon + k) for i, j in found for k in range(n_lon) if k % 4 in places]
+
+        far = lax.ppermute(to_far, ("lat", "lon"), among(pairs(n_lat, 1, 2)))
+        near = lax.ppermute(to_near, ("lat", "lon"), among(pairs(n_lat, 0, 2)))
+        return near, far
+
     joints = range(1, n_lon, 2)
     sent = [((i, (i + 1) % n_lon) if i % 4 == 3 else (i + 1, i)) for i in joints]
     to_early = lax.ppermute(to_far, "lon", sent)
     early = lax.ppermute(to_near, "lon", pairs(n_lon, 0, 4))
+    row0e, row1e = exchange_rows(pack_rows_early_kernel, early, (0, 1))
     to_late = lax.ppermute(to_far, "lon", [(j, i) for i, j in sent])
     late = lax.ppermute(to_near, "lon", pairs(n_lon, 2, 4))
+    row0l, row1l = exchange_rows(pack_rows_late_kernel, late, (2, 3))
     columns = (early, late, to_early, to_late)
-    row_shape = (ROW_MESSAGE, COLS)
-    to_near, to_far = call(
-        pack_rows_kernel, [row_shape, row_shape],
-        state, mix, vel, rate, index, weight, flux, *columns,
-    )
-    row1 = lax.ppermute(to_far, "lat", pairs(n_lat, 1, 2))
-    row0 = lax.all_gather(to_near, "lat", axis_index_groups=partners(n_lat))
+    rows = (row0e, row0l, row1e, row1l)
     wide, narrow = (LEV, 24, COLS), (LEV, ROWS, COLS)
     inverse, unit_top, seen = call(prepare_kernel, [narrow, tile, tile], prev, mix, index, weight)
     (fluxes,) = call(
         top_kernel, [(6 * ROWS, COLS)],
-        state, mix, vel, rate, flux, *columns, row0, row1, inverse, unit_top, seen,
-    )
+        state, mix, vel, rate, flux, *columns, *rows, inverse, unit_top, seen,
+    )
+    (corner,) = call(pack_corners_kernel, [(8, COLS)], to_early, to_late)
     got = lax.ppermute(fluxes, "comp", [(0, 1)])
+    corner1 = lax.ppermute(corner, "lat", pairs(n_lat, 1, 2))
+    corner0 = lax.all_gather(corner, "lat", axis_index_groups=partners(n_lat))
     parts = call(
         first_step_kernel, [wide, narrow, wide, narrow],
-        state, mix, vel, *columns, row0, row1,
+        state, mix, vel, *columns, *rows, corner0, corner1,
     )
     new_state, series = call(
         second_step_kernel, [(LEV, ROWS, COLS), (NSTEP, ROWS, COLS)],
-        mix, vel, rate, index, weight, *columns, row0, row1, *parts, inverse, fluxes, got,
+        mix, vel, rate, index, weight, *columns, *rows, *parts, inverse, fluxes, got,
         scratch=[pltpu.VMEM(shape, jnp.float32) for shape in ((24, COLS), tile, tile)],
     )
     return new_state[None], series[None]

time: 41.8 us -> 50.7 us (1.21)
  the two profiles are of different devices: /device:TPU:96 before, /device:TPU:25 now
where the time goes in v6:
time: 50.7 us; the launch traced here: 50.3 us
  starting transfers between devices  34.7 us (68%)
  waiting for transfers between devices  8.34 us (16%)
  Pallas kernels  4.67 us (9%)
  blocking collectives  1.82 us (4%)
  between operations  0.79 us (2%)
    ppermute x1, starting transfers between devices, per_device(): to_late = lax.ppermute(to_far, 'lon', [(j, i) for i, j in sent])  10.9 us
    ppermute x1, waiting for transfers between devices, per_device(): to_early = lax.ppermute(to_far, 'lon', sent)  7.02 us
    ppermute x1, starting transfers between devices, per_device(): early = lax.ppermute(to_near, 'lon', pairs(n_lon, 0, 4))  5.81 us
    ppermute x2, starting transfers between devices, exchange_rows(): far = lax.ppermute(to_far, ('lat', 'lon'), among(pairs(n_lat, 1, 2)))  4.98 us
    ppermute x1, starting transfers between devices, per_device(): corner1 = lax.ppermute(corner, 'lat', pairs(n_lat, 1, 2))  4.74 us
    pallas_call x8, Pallas kernels, call(): pl.pallas_call(kernel, out_shape=[s if hasattr(s, 'dtype') else jax.Shape...  4.67 us
    ppermute x2, starting transfers between devices, exchange_rows(): near = lax.ppermute(to_near, ('lat', 'lon'), among(pairs(n_lat, 0, 2)))  4.12 us
    ppermute x1, starting transfers between devices, per_device(): got = lax.ppermute(fluxes, 'comp', [(0, 1)])  2.26 us
  transfers between devices with their start and end apart: 10, of which 3 were waited for; matrix products, arithmetic and copies ran while one was open for 0% of the time, Pallas kernels for 3%

profile of v6, /device:TPU:25, one launch (start us, length us, event | category | flops | bytes accessed | tf_op | source)
XLA Modules:
  0.0 50.3 jit_solution(7545105875463404993)
XLA Ops:
  0.6 1.5 %shard_map.95 = (f32[32,128]{1,0:T(8,128)S(1)}, f32[32,128]{1,0:T(8,128)S(1)}, f32[16,128]{1,0:T(8,128)S(1)}, f32[16,128]{1,0:T(8,128)S(1)}, f32[12,16,128]{2,1,...) custom-call(f32[12,16,128]{2,1,0:T(8,128)} %bitcast.11, ...), custom_call_target="tpu_custom_call" | custom-call | tf_op jit(solution)/shard_map/pallas_call | solution.py:441
  2.1 5.8 %collective-permute-start = (f32[32,128]{1,0:T(8,128)S(1)}, f32[32,128]{1,0:T(8,128)S(1)}, u32[]{:S(2)}, u32[]{:S(2)}) collective-permute-start(f32[32,128]{1,0:T(8,128)S(1)} %get-tuple-element.30), channel_id=1, source_target_pairs={{0,1},{1,0},{4,5},{5,4},{8,9},{9,8},{12,13},{13,12},{16,17},{17,16... | collective-permute-start | bytes 49160 | tf_op jit(solution)/shard_map/ppermute | solution.py:493
  7.9 0.7 %collective-permute-start.1 = (f32[32,128]{1,0:T(8,128)S(1)}, f32[32,128]{1,0:T(8,128)S(1)}, u32[]{:S(2)}, u32[]{:S(2)}) collective-permute-start(f32[32,128]{1,0:T(8,128)S(1)} %get-tuple-element.30), channel_id=1, source_target_pairs={{2,3},{3,2},{6,7},{7,6},{10,11},{11,10},{14,15},{15,14},{18,19},{1... | collective-permute-start | bytes 49160 | tf_op jit(solution)/shard_map/ppermute | solution.py:496
  8.6 0.4 collective-permute-done.refs_7_.early
  9.1 3.5 %collective-permute-start.4 = (f32[104,128]{1,0:T(8,128)S(1)}, f32[104,128]{1,0:T(8,128)S(1)}, u32[]{:S(2)}, u32[]{:S(2)}) collective-permute-start(f32[104,128]{1,0:T(8,128)S(1)} %get-tuple-element.34), channel_id=1, source_target_pairs={{0,16},{1,17},{4,20},{5,21},{8,24},{9,25},{12,28},{13,29},{16,0},{... | collective-permute-start | bytes 159752 | tf_op jit(solution)/shard_map/ppermute | solution.py:487
  12.5 4.3 %collective-permute-start.6 = (f32[104,128]{1,0:T(8,128)S(1)}, f32[104,128]{1,0:T(8,128)S(1)}, u32[]{:S(2)}, u32[]{:S(2)}) collective-permute-start(f32[104,128]{1,0:T(8,128)S(1)} %get-tuple-element.36), channel_id=1, source_target_pairs={{16,32},{17,33},{20,36},{21,37},{24,40},{25,41},{28,44},{29,45},{3... | collective-permute-start | bytes 159752 | tf_op jit(solution)/shard_map/ppermute | solution.py:486
  16.9 0.0 collective-permute-done.1.refs_7_.late
  16.9 0.7 %collective-permute-start.5 = (f32[104,128]{1,0:T(8,128)S(1)}, f32[104,128]{1,0:T(8,128)S(1)}, u32[]{:S(2)}, u32[]{:S(2)}) collective-permute-start(f32[104,128]{1,0:T(8,128)S(1)} %get-tuple-element.35), channel_id=1, source_target_pairs={{2,18},{3,19},{6,22},{7,23},{10,26},{11,27},{14,30},{15,31},{18,2}... | collective-permute-start | bytes 159752 | tf_op jit(solution)/shard_map/ppermute | solution.py:487
  17.6 0.7 %collective-permute-start.7 = (f32[104,128]{1,0:T(8,128)S(1)}, f32[104,128]{1,0:T(8,128)S(1)}, u32[]{:S(2)}, u32[]{:S(2)}) collective-permute-start(f32[104,128]{1,0:T(8,128)S(1)} %get-tuple-element.37), channel_id=1, source_target_pairs={{18,34},{19,35},{22,38},{23,39},{26,42},{27,43},{30,46},{31,47},{3... | collective-permute-start | bytes 159752 | tf_op jit(solution)/shard_map/ppermute | solution.py:486
  18.2 10.9 %collective-permute-start.3 = (f32[32,128]{1,0:T(8,128)S(1)}, f32[32,128]{1,0:T(8,128)S(1)}, u32[]{:S(2)}, u32[]{:S(2)}) collective-permute-start(f32[32,128]{1,0:T(8,128)S(1)} %get-tuple-element.31), channel_id=1, source_target_pairs={{1,2},{4,3},{5,6},{8,7},{9,10},{12,11},{13,14},{0,15},{17,18},{20,... | collective-permute-start | bytes 49160 | tf_op jit(solution)/shard_map/ppermute | solution.py:495
  29.1 0.9 %collective-permute-done.3.to_late = f32[32,128]{1,0:T(8,128)S(1)} collective-permute-done((f32[32,128]{1,0:T(8,128)S(1)}, f32[32,128]{1,0:T(8,128)S(1)}, u32[]{:S(2)}, u32[]{:S(2)}) %collective-permute-start.3) | collective-permute-done | bytes 16416 | tf_op jit(solution)/shard_map/ppermute | solution.py:495
  30.0 1.3 %collective-permute-start.2 = (f32[32,128]{1,0:T(8,128)S(1)}, f32[32,128]{1,0:T(8,128)S(1)}, u32[]{:S(2)}, u32[]{:S(2)}) collective-permute-start(f32[32,128]{1,0:T(8,128)S(1)} %get-tuple-element.31), channel_id=1, source_target_pairs={{2,1},{3,4},{6,5},{7,8},{10,9},{11,12},{14,13},{15,0},{18,17},{19,... | collective-permute-start | bytes 49160 | tf_op jit(solution)/shard_map/ppermute | solution.py:492
  31.3 0.4 shard_map.100
  31.6 7.0 %collective-permute-done.2.to_early = f32[32,128]{1,0:T(8,128)S(1)} collective-permute-done((f32[32,128]{1,0:T(8,128)S(1)}, f32[32,128]{1,0:T(8,128)S(1)}, u32[]{:S(2)}, u32[]{:S(2)}) %collective-permute-start.2) | collective-permute-done | bytes 16416 | tf_op jit(solution)/shard_map/ppermute | solution.py:492
  38.7 0.0 collective-permute-done.4.row0e
  38.7 0.0 collective-permute-done.6.row1e
  38.7 0.0 collective-permute-done.5.row0l
  38.7 0.0 collective-permute-done.7.row1l
  38.7 0.6 %shard_map.101.sent = f32[96,128]{1,0:T(8,128)S(1)} custom-call(f32[12,16,128]{2,1,0:T(8,128)S(1)} %get-tuple-element.32.refs_0_.state, f32[11,16,128]{2,1,0:T(8,128)S(1)} %get-tuple-element.25.refs_1_.mix, f32[2,16,128]{2,1,0:T(8,128)S(1)} %get-tuple-element.26.refs_2_.vel, f32[16,128]{1,0:T(8,128)S(1)} %get-tuple-element.27.refs_3_.rate.rate_in, ...), custom_call_target="tpu_custom_call" | custom-call | tf_op jit(solution)/shard_map/pallas_call | solution.py:441
  39.3 2.3 %collective-permute-start.9 = (f32[96,128]{1,0:T(8,128)S(1)}, f32[96,128]{1,0:T(8,128)S(1)}, u32[]{:S(2)}, u32[]{:S(2)}) collective-permute-start(f32[96,128]{1,0:T(8,128)S(1)} %shard_map.101.sent), channel_id=1, source_target_pairs={{0,256},{1,257},{2,258},{3,259},{4,260},{5,261},{6,262},{7,263},{8... | collective-permute-start | bytes 147464 | tf_op jit(solution)/shard_map/ppermute | solution.py:507
  41.6 4.7 %collective-permute-start.8 = (f32[8,128]{1,0:T(8,128)S(1)}, f32[8,128]{1,0:T(8,128)S(1)}, u32[]{:S(2)}, u32[]{:S(2)}) collective-permute-start(f32[8,128]{1,0:T(8,128)S(1)} %shard_map.98), channel_id=1, source_target_pairs={{16,32},{32,16},{48,64},{64,48},{80,96},{96,80},{112,128},{128,112... | collective-permute-start | bytes 12296 | tf_op jit(solution)/shard_map/ppermute | solution.py:508
  46.4 1.8 %all-gather = f32[16,128]{1,0:T(8,128)S(1)} all-gather(f32[8,128]{1,0:T(8,128)S(1)} %shard_map.98), channel_id=2, replica_groups={{0,16},{32,48},{64,80},{96,112},{128,144},{160,176},{192,208},{224,240}..., dimensions={0}, use_global_device_ids=true | all-gather | bytes 12288 | tf_op jit(solution)/shard_map/all_gather | solution.py:509
  48.2 0.0 collective-permute-done.8.corner1
  48.2 1.2 %shard_map.99 = (f32[12,24,128]{2,1,0:T(8,128)S(1)}, f32[12,16,128]{2,1,0:T(8,128)S(1)}, f32[12,24,128]{2,1,0:T(8,128)S(1)}, f32[12,16,128]{2,1,0:T(8,128)S(1)}) custom-call(f32[12,16,128]{2,1,0:T(8,128)S(1)} %get-tuple-element.32.refs_0_.state, f32[11,16,128]{2,1,0:T(8,128)S(1)} %get-tuple-element.25.refs_1_.mix, ...), custom_call_target="tpu_custom_call" | custom-call | tf_op jit(solution)/shard_map/pallas_call | solution.py:441
  49.4 0.0 collective-permute-done.9.got
  49.4 1.0 %shard_map.102 = (f32[12,16,128]{2,1,0:T(8,128)}, f32[2,16,128]{2,1,0:T(8,128)}) custom-call(f32[11,16,128]{2,1,0:T(8,128)S(1)} %get-tuple-element.25.refs_1_.mix, f32[2,16,128]{2,1,0:T(8,128)S(1)} %get-tuple-element.26.refs_2_.vel, f32[16,128]{1,0:T(8,128)S(1)} %get-tuple-element.27.refs_3_.rate.rate_in, s32[4,16,128]{2,1,0:T(8,128)S(1)} %get-tuple-element.28.refs_4_.index, ...), custom_call_target="tpu_custom_call" | custom-call | tf_op jit(solution)/shard_map/pallas_call | solution.py:441
  (3 shorter events, 0.1 us)
Async XLA Ops:
  2.1 6.9 %collective-permute-start = (f32[32,128]{1,0:T(8,128)S(1)}, f32[32,128]{1,0:T(8,128)S(1)}, u32[]{:S(2)}, u32[]{:S(2)}) collective-permute-start(f32[32,128]{1,0:T(8,128)S(1)} %get-tuple-element.30), channel_id=1, source_target_pairs={{0,1},{1,0},{4,5},{5,4},{8,9},{9,8},{12,13},{13,12},{16,17},{17,16... | collective-permute-start | bytes 49160 | tf_op jit(solution)/shard_map/ppermute | solution.py:493
  7.9 8.9 %collective-permute-start.1 = (f32[32,128]{1,0:T(8,128)S(1)}, f32[32,128]{1,0:T(8,128)S(1)}, u32[]{:S(2)}, u32[]{:S(2)}) collective-permute-start(f32[32,128]{1,0:T(8,128)S(1)} %get-tuple-element.30), channel_id=1, source_target_pairs={{2,3},{3,2},{6,7},{7,6},{10,11},{11,10},{14,15},{15,14},{18,19},{1... | collective-permute-start | bytes 49160 | tf_op jit(solution)/shard_map/ppermute | solution.py:496
  9.1 29.6 %collective-permute-start.4 = (f32[104,128]{1,0:T(8,128)S(1)}, f32[104,128]{1,0:T(8,128)S(1)}, u32[]{:S(2)}, u32[]{:S(2)}) collective-permute-start(f32[104,128]{1,0:T(8,128)S(1)} %get-tuple-element.34), channel_id=1, source_target_pairs={{0,16},{1,17},{4,20},{5,21},{8,24},{9,25},{12,28},{13,29},{16,0},{... | collective-permute-start | bytes 159752 | tf_op jit(solution)/shard_map/ppermute | solution.py:487
  12.5 26.1 %collective-permute-start.6 = (f32[104,128]{1,0:T(8,128)S(1)}, f32[104,128]{1,0:T(8,128)S(1)}, u32[]{:S(2)}, u32[]{:S(2)}) collective-permute-start(f32[104,128]{1,0:T(8,128)S(1)} %get-tuple-element.36), channel_id=1, source_target_pairs={{16,32},{17,33},{20,36},{21,37},{24,40},{25,41},{28,44},{29,45},{3... | collective-permute-start | bytes 159752 | tf_op jit(solution)/shard_map/ppermute | solution.py:486
  16.9 21.8 %collective-permute-start.5 = (f32[104,128]{1,0:T(8,128)S(1)}, f32[104,128]{1,0:T(8,128)S(1)}, u32[]{:S(2)}, u32[]{:S(2)}) collective-permute-start(f32[104,128]{1,0:T(8,128)S(1)} %get-tuple-element.35), channel_id=1, source_target_pairs={{2,18},{3,19},{6,22},{7,23},{10,26},{11,27},{14,30},{15,31},{18,2}... | collective-permute-start | bytes 159752 | tf_op jit(solution)/shard_map/ppermute | solution.py:487
  17.6 21.1 %collective-permute-start.7 = (f32[104,128]{1,0:T(8,128)S(1)}, f32[104,128]{1,0:T(8,128)S(1)}, u32[]{:S(2)}, u32[]{:S(2)}) collective-permute-start(f32[104,128]{1,0:T(8,128)S(1)} %get-tuple-element.37), channel_id=1, source_target_pairs={{18,34},{19,35},{22,38},{23,39},{26,42},{27,43},{30,46},{31,47},{3... | collective-permute-start | bytes 159752 | tf_op jit(solution)/shard_map/ppermute | solution.py:486
  18.2 11.7 %collective-permute-start.3 = (f32[32,128]{1,0:T(8,128)S(1)}, f32[32,128]{1,0:T(8,128)S(1)}, u32[]{:S(2)}, u32[]{:S(2)}) collective-permute-start(f32[32,128]{1,0:T(8,128)S(1)} %get-tuple-element.31), channel_id=1, source_target_pairs={{1,2},{4,3},{5,6},{8,7},{9,10},{12,11},{13,14},{0,15},{17,18},{20,... | collective-permute-start | bytes 49160 | tf_op jit(solution)/shard_map/ppermute | solution.py:495
  30.0 8.7 %collective-permute-start.2 = (f32[32,128]{1,0:T(8,128)S(1)}, f32[32,128]{1,0:T(8,128)S(1)}, u32[]{:S(2)}, u32[]{:S(2)}) collective-permute-start(f32[32,128]{1,0:T(8,128)S(1)} %get-tuple-element.31), channel_id=1, source_target_pairs={{2,1},{3,4},{6,5},{7,8},{10,9},{11,12},{14,13},{15,0},{18,17},{19,... | collective-permute-start | bytes 49160 | tf_op jit(solution)/shard_map/ppermute | solution.py:492
  39.3 10.0 %collective-permute-start.9 = (f32[96,128]{1,0:T(8,128)S(1)}, f32[96,128]{1,0:T(8,128)S(1)}, u32[]{:S(2)}, u32[]{:S(2)}) collective-permute-start(f32[96,128]{1,0:T(8,128)S(1)} %shard_map.101.sent), channel_id=1, source_target_pairs={{0,256},{1,257},{2,258},{3,259},{4,260},{5,261},{6,262},{7,263},{8... | collective-permute-start | bytes 147464 | tf_op jit(solution)/shard_map/ppermute | solution.py:507
  41.6 6.6 %collective-permute-start.8 = (f32[8,128]{1,0:T(8,128)S(1)}, f32[8,128]{1,0:T(8,128)S(1)}, u32[]{:S(2)}, u32[]{:S(2)}) collective-permute-start(f32[8,128]{1,0:T(8,128)S(1)} %shard_map.98), channel_id=1, source_target_pairs={{16,32},{32,16},{48,64},{64,48},{80,96},{96,80},{112,128},{128,112... | collective-permute-start | bytes 12296 | tf_op jit(solution)/shard_map/ppermute | solution.py:508

commit v7 on v5

--- a/solution.py
+++ b/solution.py
@@ -71,11 +71,11 @@
         pltpu.make_async_copy(source, target, arrived.at[k])
         for k, (source, target) in enumerate(
             (
+                (index_hbm, index),
+                (prev_hbm, prev),
+                (weight_hbm, weight),
                 (state_hbm, state),
                 (mix_hbm, mix),
-                (index_hbm, index),
-                (weight_hbm, weight),
-                (prev_hbm, prev),
                 (vel_hbm, vel),
                 (couple_hbm, couple),
                 (mask_hbm, mask),
@@ -87,7 +87,14 @@
     is_atmosphere = lax.axis_index("comp") == 0
     odd = lax.rem(lax.axis_index("lon"), 2) == 1
     lane = lanes(ROWS)
-    for move in moves:
+    for move in moves[:3]:
+        move.wait()
+
+    @pl.when(is_atmosphere)
+    def _():
+        flux_out[...] = regrid_tile(prev[0], index, weight)
+
+    for move in moves[3:]:
         move.wait()
     rate = couple[...] * mask[...].astype(jnp.float32)
     rate_out[...] = rate
@@ -117,7 +124,7 @@
 
     @pl.when(is_atmosphere)
     def _():
-        flux = rate * (regrid_tile(prev[0], index, weight) - state[0])
+        flux = rate * (flux_out[...] - state[0])
         flux_out[...] = flux
         msg0[ROWS:] = flux
         msg1[ROWS:] = flux
@@ -204,12 +211,13 @@
         for shift, factor in zip(shifts, side_weights[1]):
             side_result = side_result + factor * roll(side, shift, 0)[:ROWS]
     for k, shift in enumerate(shifts):
-        moved, moved_side = roll(own[:own_rows], shift, 1), roll(side[:own_rows], shift, 1)
-        cut = lane < shift if shift > 0 else lane >= COLS + shift
-        result = result + own_weights[0][k] * jnp.where(cut, moved_side, moved)
+        cut = lane >= COLS - shift if shift > 0 else lane < -shift
+        own_part, side_part = own[:own_rows], side[:own_rows]
+        moved = roll(jnp.where(cut, side_part, own_part), shift, 1)
+        result = result + own_weights[0][k] * moved
         if side_weights is not None:
-            there = jnp.where(cut[:ROWS], moved[:ROWS], moved_side[:ROWS])
-            side_result = side_result + side_weights[0][k] * there
+            there = jnp.where(cut[:ROWS], own_part[:ROWS], side_part[:ROWS])
+            side_result = side_result + side_weights[0][k] * roll(there, shift, 1)
     return result, side_result
 
 

time: 41.8 us -> 41.9 us (level)
  no operation moved by 1% of the time
where the time goes in v7:
time: 41.9 us; the launch traced here: 41.6 us
  starting transfers between devices  19.8 us (47%)
  waiting for transfers between devices  14.6 us (35%)
  Pallas kernels  4.12 us (10%)
  blocking collectives  2.31 us (6%)
  between operations  0.73 us (2%)
    ppermute x1, waiting for transfers between devices, per_device(): to_early = lax.ppermute(to_far, 'lon', sent)  8.6 us
    ppermute x1, starting transfers between devices, per_device(): to_late = lax.ppermute(to_far, 'lon', [(j, i) for i, j in sent])  8.59 us
    ppermute x1, starting transfers between devices, per_device(): early = lax.ppermute(to_near, 'lon', pairs(n_lon, 0, 4))  6.09 us
    pallas_call x6, Pallas kernels, call(): pl.pallas_call(kernel, out_shape=[s if hasattr(s, 'dtype') else jax.Shape...  4.12 us
    ppermute x1, waiting for transfers between devices, per_device(): got = lax.ppermute(fluxes, 'comp', [(0, 1)])  3.67 us
    all_gather x1, blocking collectives, per_device(): row0 = lax.all_gather(to_near, 'lat', axis_index_groups=partners(n_lat))  2.31 us
    ppermute x1, waiting for transfers between devices, per_device(): row1 = lax.ppermute(to_far, 'lat', pairs(n_lat, 1, 2))  2.27 us
    ppermute x1, starting transfers between devices, per_device(): row1 = lax.ppermute(to_far, 'lat', pairs(n_lat, 1, 2))  1.92 us
  transfers between devices with their start and end apart: 6, of which 4 were waited for; matrix products, arithmetic and copies ran while one was open for 0% of the time, Pallas kernels for 3%

profile of v7, /device:TPU:96, one launch (start us, length us, event | category | flops | bytes accessed | tf_op | source)
XLA Modules:
  0.0 41.6 jit_solution(15666713204288518000)
XLA Ops:
  0.6 1.3 %shard_map.95 = (f32[32,128]{1,0:T(8,128)S(1)}, f32[32,128]{1,0:T(8,128)S(1)}, f32[16,128]{1,0:T(8,128)S(1)}, f32[16,128]{1,0:T(8,128)S(1)}, f32[12,16,128]{2,1,...) custom-call(f32[12,16,128]{2,1,0:T(8,128)} %bitcast.13, ...), custom_call_target="tpu_custom_call" | custom-call | tf_op jit(solution)/shard_map/pallas_call | solution.py:428
  1.9 0.7 %collective-permute-start.1 = (f32[32,128]{1,0:T(8,128)S(1)}, f32[32,128]{1,0:T(8,128)S(1)}, u32[]{:S(2)}, u32[]{:S(2)}) collective-permute-start(f32[32,128]{1,0:T(8,128)S(1)} %get-tuple-element.28), channel_id=1, source_target_pairs={{2,3},{3,2},{6,7},{7,6},{10,11},{11,10},{14,15},{15,14},{18,19},{1... | collective-permute-start | bytes 49160 | tf_op jit(solution)/shard_map/ppermute | solution.py:469
  2.6 6.1 %collective-permute-start = (f32[32,128]{1,0:T(8,128)S(1)}, f32[32,128]{1,0:T(8,128)S(1)}, u32[]{:S(2)}, u32[]{:S(2)}) collective-permute-start(f32[32,128]{1,0:T(8,128)S(1)} %get-tuple-element.28), channel_id=1, source_target_pairs={{0,1},{1,0},{4,5},{5,4},{8,9},{9,8},{12,13},{13,12},{16,17},{17,16... | collective-permute-start | bytes 49160 | tf_op jit(solution)/shard_map/ppermute | solution.py:467
  8.7 8.6 %collective-permute-start.3 = (f32[32,128]{1,0:T(8,128)S(1)}, f32[32,128]{1,0:T(8,128)S(1)}, u32[]{:S(2)}, u32[]{:S(2)}) collective-permute-start(f32[32,128]{1,0:T(8,128)S(1)} %get-tuple-element.29), channel_id=1, source_target_pairs={{1,2},{4,3},{5,6},{8,7},{9,10},{12,11},{13,14},{0,15},{17,18},{20,... | collective-permute-start | bytes 49160 | tf_op jit(solution)/shard_map/ppermute | solution.py:468
  17.3 1.3 %collective-permute-start.2 = (f32[32,128]{1,0:T(8,128)S(1)}, f32[32,128]{1,0:T(8,128)S(1)}, u32[]{:S(2)}, u32[]{:S(2)}) collective-permute-start(f32[32,128]{1,0:T(8,128)S(1)} %get-tuple-element.29), channel_id=1, source_target_pairs={{2,1},{3,4},{6,5},{7,8},{10,9},{11,12},{14,13},{15,0},{18,17},{19,... | collective-permute-start | bytes 49160 | tf_op jit(solution)/shard_map/ppermute | solution.py:466
  18.6 0.0 collective-permute-done.1.late
  18.6 0.0 collective-permute-done.early
  18.6 0.1 collective-permute-done.3.to_late
  18.7 8.6 %collective-permute-done.2.to_early = f32[32,128]{1,0:T(8,128)S(1)} collective-permute-done((f32[32,128]{1,0:T(8,128)S(1)}, f32[32,128]{1,0:T(8,128)S(1)}, u32[]{:S(2)}, u32[]{:S(2)}) %collective-permute-start.2) | collective-permute-done | bytes 16416 | tf_op jit(solution)/shard_map/ppermute | solution.py:466
  27.4 1.9 %collective-permute-start.4 = (f32[104,128]{1,0:T(8,128)S(1)}, f32[104,128]{1,0:T(8,128)S(1)}, u32[]{:S(2)}, u32[]{:S(2)}) collective-permute-start(f32[104,128]{1,0:T(8,128)S(1)} %get-tuple-element.33), channel_id=1, source_target_pairs={{16,32},{32,16},{48,64},{64,48},{80,96},{96,80},{112,128},{128,112... | collective-permute-start | bytes 159752 | tf_op jit(solution)/shard_map/ppermute | solution.py:476
  29.3 0.1 shard_map.98
  29.5 2.3 %all-gather = f32[208,128]{1,0:T(8,128)S(1)} all-gather(f32[104,128]{1,0:T(8,128)S(1)} %get-tuple-element.32), channel_id=2, replica_groups={{0,16},{32,48},{64,80},{96,112},{128,144},{160,176},{192,208},{224,240}..., dimensions={0}, use_global_device_ids=true | all-gather | bytes 159744 | tf_op jit(solution)/shard_map/all_gather | solution.py:477
  31.8 2.3 %collective-permute-done.4.row1 = f32[104,128]{1,0:T(8,128)S(1)} collective-permute-done((f32[104,128]{1,0:T(8,128)S(1)}, f32[104,128]{1,0:T(8,128)S(1)}, u32[]{:S(2)}, u32[]{:S(2)}) %collective-permute-start.4) | collective-permute-done | bytes 53280 | tf_op jit(solution)/shard_map/ppermute | solution.py:476
  34.0 1.3 %collective-permute-start.5 = (f32[96,128]{1,0:T(8,128)S(1)}, f32[96,128]{1,0:T(8,128)S(1)}, u32[]{:S(2)}, u32[]{:S(2)}) collective-permute-start(f32[96,128]{1,0:T(8,128)S(1)} %shard_map.99.sent), channel_id=1, source_target_pairs={{0,256},{1,257},{2,258},{3,259},{4,260},{5,261},{6,262},{7,263},{8... | collective-permute-start | bytes 147464 | tf_op jit(solution)/shard_map/ppermute | solution.py:484
  35.3 1.0 %shard_map.97 = (f32[12,24,128]{2,1,0:T(8,128)S(1)}, f32[12,16,128]{2,1,0:T(8,128)S(1)}, f32[12,24,128]{2,1,0:T(8,128)S(1)}, f32[12,16,128]{2,1,0:T(8,128)S(1)}) custom-call(f32[12,16,128]{2,1,0:T(8,128)S(1)} %get-tuple-element.30.state, f32[11,16,128]{2,1,0:T(8,128)S(1)} %get-tuple-element.23.mix, f32[2,16,128]{2,1,0:T(8,128)S(1)} %get-tuple-element.24.vel, ...), custom_call_target="tpu_custom_call" | custom-call | tf_op jit(solution)/shard_map/pallas_call | solution.py:428
  36.3 3.7 %collective-permute-done.5.got = f32[96,128]{1,0:T(8,128)S(1)} collective-permute-done((f32[96,128]{1,0:T(8,128)S(1)}, f32[96,128]{1,0:T(8,128)S(1)}, u32[]{:S(2)}, u32[]{:S(2)}) %collective-permute-start.5) | collective-permute-done | bytes 49184 | tf_op jit(solution)/shard_map/ppermute | solution.py:484
  40.0 1.6 %shard_map.100 = (f32[12,16,128]{2,1,0:T(8,128)}, f32[2,16,128]{2,1,0:T(8,128)}) custom-call(f32[11,16,128]{2,1,0:T(8,128)S(1)} %get-tuple-element.23.mix, f32[2,16,128]{2,1,0:T(8,128)S(1)} %get-tuple-element.24.vel, f32[16,128]{1,0:T(8,128)S(1)} %get-tuple-element.25.rate_in.rate, s32[4,16,128]{2,1,0:T(8,128)S(1)} %get-tuple-element.26.index, ...), custom_call_target="tpu_custom_call" | custom-call | tf_op jit(solution)/shard_map/pallas_call | solution.py:428
  (2 shorter events, 0.0 us)
Async XLA Ops:
  1.9 16.7 %collective-permute-start.1 = (f32[32,128]{1,0:T(8,128)S(1)}, f32[32,128]{1,0:T(8,128)S(1)}, u32[]{:S(2)}, u32[]{:S(2)}) collective-permute-start(f32[32,128]{1,0:T(8,128)S(1)} %get-tuple-element.28), channel_id=1, source_target_pairs={{2,3},{3,2},{6,7},{7,6},{10,11},{11,10},{14,15},{15,14},{18,19},{1... | collective-permute-start | bytes 49160 | tf_op jit(solution)/shard_map/ppermute | solution.py:469
  2.6 16.0 %collective-permute-start = (f32[32,128]{1,0:T(8,128)S(1)}, f32[32,128]{1,0:T(8,128)S(1)}, u32[]{:S(2)}, u32[]{:S(2)}) collective-permute-start(f32[32,128]{1,0:T(8,128)S(1)} %get-tuple-element.28), channel_id=1, source_target_pairs={{0,1},{1,0},{4,5},{5,4},{8,9},{9,8},{12,13},{13,12},{16,17},{17,16... | collective-permute-start | bytes 49160 | tf_op jit(solution)/shard_map/ppermute | solution.py:467
  8.7 10.0 %collective-permute-start.3 = (f32[32,128]{1,0:T(8,128)S(1)}, f32[32,128]{1,0:T(8,128)S(1)}, u32[]{:S(2)}, u32[]{:S(2)}) collective-permute-start(f32[32,128]{1,0:T(8,128)S(1)} %get-tuple-element.29), channel_id=1, source_target_pairs={{1,2},{4,3},{5,6},{8,7},{9,10},{12,11},{13,14},{0,15},{17,18},{20,... | collective-permute-start | bytes 49160 | tf_op jit(solution)/shard_map/ppermute | solution.py:468
  17.3 10.0 %collective-permute-start.2 = (f32[32,128]{1,0:T(8,128)S(1)}, f32[32,128]{1,0:T(8,128)S(1)}, u32[]{:S(2)}, u32[]{:S(2)}) collective-permute-start(f32[32,128]{1,0:T(8,128)S(1)} %get-tuple-element.29), channel_id=1, source_target_pairs={{2,1},{3,4},{6,5},{7,8},{10,9},{11,12},{14,13},{15,0},{18,17},{19,... | collective-permute-start | bytes 49160 | tf_op jit(solution)/shard_map/ppermute | solution.py:466
  27.4 6.7 %collective-permute-start.4 = (f32[104,128]{1,0:T(8,128)S(1)}, f32[104,128]{1,0:T(8,128)S(1)}, u32[]{:S(2)}, u32[]{:S(2)}) collective-permute-start(f32[104,128]{1,0:T(8,128)S(1)} %get-tuple-element.33), channel_id=1, source_target_pairs={{16,32},{32,16},{48,64},{64,48},{80,96},{96,80},{112,128},{128,112... | collective-permute-start | bytes 159752 | tf_op jit(solution)/shard_map/ppermute | solution.py:476
  34.0 6.0 %collective-permute-start.5 = (f32[96,128]{1,0:T(8,128)S(1)}, f32[96,128]{1,0:T(8,128)S(1)}, u32[]{:S(2)}, u32[]{:S(2)}) collective-permute-start(f32[96,128]{1,0:T(8,128)S(1)} %shard_map.99.sent), channel_id=1, source_target_pairs={{0,256},{1,257},{2,258},{3,259},{4,260},{5,261},{6,262},{7,263},{8... | collective-permute-start | bytes 147464 | tf_op jit(solution)/shard_map/ppermute | solution.py:484

commit v8 on v7

--- a/solution.py
+++ b/solution.py
@@ -262,49 +262,56 @@
     return jnp.where(lane < width, a, jnp.where(lane >= COLS - width, b, 0.0))
 
 
-def prepare_kernel(prev, mix, index, weight, inverse_out, unit_top, seen):
-    inverses, ratios = factors([mix[level] for level in range(LEV - 1)])
-    for level in range(LEV):
-        inverse_out[level] = inverses[level]
-    own_mix = [mix[level] for level in range(LEV - 1)]
-    unit_top[...] = solve([1.0] + [None] * (LEV - 1), own_mix, inverses, ratios)[0]
-
-    @pl.when(lax.axis_index("comp") == 0)
-    def _():
-        seen[...] = regrid_tile(prev[1], index, weight)
-
-
-def top_kernel(
-    state, mix, vel, rate, flux, early, late, to_early, to_late, row0, row1, inverse, unit_top, seen,
-    fluxes,
-):
-    @pl.when(lax.axis_index("comp") == 0)
-    def _():
-        west, east = column_messages((early, late, to_early, to_late))
-        north, south = row_messages(row0, row1)
-        weights = transport_weights(vel[0], vel[1])
-        moved = []
-        for level in range(LEV):
-            own = jnp.concatenate([state[level], rim_of_levels(north, south, level)], axis=0)
-            there = side_of(west[0:ROWS], east[0:ROWS], 4 * level, 4, ROWS)
-            moved.append(horizontal(own, there, weights, None, ROWS)[0])
-        own_mix = [mix[level] for level in range(LEV - 1)]
-        inverses = [inverse[level] for level in range(LEV)]
-        ratios = [own_mix[level] * inverses[level] for level in range(LEV - 1)]
-        top = solve(moved, own_mix, inverses, ratios)[0] + flux[...] * unit_top[...]
-        fluxes[0:ROWS] = flux[...]
-        fluxes[ROWS : 2 * ROWS] = west[ROWS:]
-        fluxes[2 * ROWS : 3 * ROWS] = east[ROWS:]
-        fluxes[3 * ROWS : 4 * ROWS] = north[AT_FLUX : AT_FLUX + ROWS]
-        fluxes[4 * ROWS : 5 * ROWS] = south[AT_FLUX : AT_FLUX + ROWS]
-        fluxes[5 * ROWS :] = rate[...] * (seen[...] - top)
-
-
-def first_step_kernel(
-    state, mix, vel, early, late, to_early, to_late, row0, row1, before, before_side, unit, unit_side,
+IMPULSE = [1.0] + [None] * (LEV - 1)
+
+
+def prepare_kernel(
+    prev, mix, index, weight, early, late, to_early, to_late, inverse, inverse_side, unit, unit_side, seen
 ):
     west, east = column_messages((early, late, to_early, to_late))
-    north, south = row_messages(row0, row1)
+    own_mix = [mix[level] for level in range(LEV - 1)]
+    side_mix = [side_of(west, east, AT_MIX + 2 * level, 2, ROWS) for level in range(LEV - 1)]
+    found = [(factors(m), m) for m in (own_mix, side_mix)]
+    for ((inverses, ratios), m), inverse_out, out in zip(
+        found, (inverse, inverse_side), (unit, unit_side)
+    ):
+        impulse = solve(IMPULSE, m, inverses, ratios)
+        for level in range(LEV):
+            inverse_out[level] = inverses[level]
+            out[level] = impulse[level]
+
+    @pl.when(lax.axis_index("comp") == 0)
+    def _():
+        seen[...] = regrid_tile(prev[1], index, weight)
+
+
+def stored(inverse, mixes):
+    inverses = [inverse[level] for level in range(LEV)]
+    return inverses, [mixes[level] * inverses[level] for level in range(LEV - 1)]
+
+
+def top_step(state, mix, vel, rate, flux, columns, rows, inverse, unit, seen, fluxes):
+    west, east = column_messages(columns)
+    north, south = row_messages(*rows)
+    weights = transport_weights(vel[0], vel[1])
+    moved = []
+    for level in range(LEV):
+        own = jnp.concatenate([state[level], rim_of_levels(north, south, level)], axis=0)
+        there = side_of(west[0:ROWS], east[0:ROWS], 4 * level, 4, ROWS)
+        moved.append(horizontal(own, there, weights, None, ROWS)[0])
+    own_mix = [mix[level] for level in range(LEV - 1)]
+    top = solve(moved, own_mix, *stored(inverse, own_mix))[0] + flux[...] * unit[0]
+    fluxes[0:ROWS] = flux[...]
+    fluxes[ROWS : 2 * ROWS] = west[ROWS:]
+    fluxes[2 * ROWS : 3 * ROWS] = east[ROWS:]
+    fluxes[3 * ROWS : 4 * ROWS] = north[AT_FLUX : AT_FLUX + ROWS]
+    fluxes[4 * ROWS : 5 * ROWS] = south[AT_FLUX : AT_FLUX + ROWS]
+    fluxes[5 * ROWS :] = rate[...] * (seen[...] - top)
+
+
+def halo_step(state, mix, vel, columns, rows, inverse, inverse_side, before, before_side, unit_rim):
+    west, east = column_messages(columns)
+    north, south = row_messages(*rows)
     at_lat = lax.axis_index("lat")
     sub = sublanes()
     valid = ((sub < 4) & (at_lat < lax.axis_size("lat") - 1)) | ((sub >= 4) & (at_lat > 0))
@@ -328,60 +335,89 @@
     def side(at, width, rows):
         return side_of(west_tile, east_tile, at, width, rows)
 
-    def extended(x, rim):
-        return jnp.concatenate([x, rim], axis=0)
-
-    own_mix = [extended(mix[level], rim2(AT_MIX + 2 * level)) for level in range(LEV - 1)]
+    own_mix = [mix[level] for level in range(LEV - 1)]
+    rim_mix = [rim2(AT_MIX + 2 * level) for level in range(LEV - 1)]
     side_mix = [side(AT_MIX + 2 * level, 2, ROWS) for level in range(LEV - 1)]
-    own_vel = [extended(vel[part], rim2(AT_VEL + 2 * part)) for part in range(2)]
+    own_vel = [
+        jnp.concatenate([vel[part], rim2(AT_VEL + 2 * part)], axis=0) for part in range(2)
+    ]
     side_vel = [side(AT_VEL + 2 * part, 2, ROWS) for part in range(2)]
     own_weights, side_weights = transport_weights(*own_vel), transport_weights(*side_vel)
-
+    rim_factors = factors(rim_mix)
     moved, moved_side = [], []
     for level in range(LEV):
-        own = extended(state[level], rim_of_levels(north, south, level))
+        own = jnp.concatenate([state[level], rim_of_levels(north, south, level)], axis=0)
         a, b = horizontal(own, side(4 * level, 4, 24), own_weights, side_weights, 24)
         moved.append(a)
         moved_side.append(b)
-    inverses, ratios = factors(own_mix)
-    solved = solve(moved, own_mix, inverses, ratios)
-    impulse = solve([1.0] + [None] * (LEV - 1), own_mix, inverses, ratios)
+    rim = solve([x[ROWS:] for x in moved], rim_mix, *rim_factors)
+    impulse = solve(IMPULSE, rim_mix, *rim_factors)
+    own = solve([x[:ROWS] for x in moved], own_mix, *stored(inverse, own_mix))
+    there = solve(moved_side, side_mix, *stored(inverse_side, side_mix))
     for level in range(LEV):
-        for out, values in ((before, solved), (unit, impulse)):
-            out[level, 0:ROWS] = values[level][:ROWS]
-            out[level, ROWS:] = jnp.where(valid, values[level][ROWS:], 0.0)
-    inverses, ratios = factors(side_mix)
-    solved = solve(moved_side, side_mix, inverses, ratios)
-    impulse = solve([1.0] + [None] * (LEV - 1), side_mix, inverses, ratios)
-    for level in range(LEV):
-        before_side[level] = solved[level]
-        unit_side[level] = impulse[level]
+        before[level, 0:ROWS] = own[level]
+        before[level, ROWS:] = jnp.where(valid, rim[level], 0.0)
+        before_side[level] = there[level]
+        unit_rim[level] = jnp.where(valid, impulse[level], 0.0)
+
+
+def middle_kernel(
+    state, mix, vel, rate, flux, early, late, to_early, to_late, row0, row1,
+    inverse, inverse_side, unit, seen, fluxes, before, before_side, unit_rim,
+):
+    columns, rows = (early, late, to_early, to_late), (row0, row1)
+
+    @pl.when(lax.axis_index("comp") == 0)
+    def _():
+        top_step(state, mix, vel, rate, flux, columns, rows, inverse, unit, seen, fluxes)
+
+    @pl.when(lax.axis_index("comp") != 0)
+    def _():
+        halo_step(state, mix, vel, columns, rows, inverse, inverse_side, before, before_side, unit_rim)
 
 
 def second_step_kernel(
-    mix, vel, rate_in, index, weight, early, late, to_early, to_late, row0, row1,
-    before, before_side, unit, unit_side, inverse, sent, got, new_state, series, force, force_side, force1,
+    state, mix, vel, rate_in, index, weight, early, late, to_early, to_late, row0, row1,
+    inverse, inverse_side, unit, unit_side, given_before, given_side, given_rim, got,
+    new_state, series, own_before, own_side, own_rim,
 ):
-    is_atmosphere = lax.axis_index("comp") == 0
+    columns, rows = (early, late, to_early, to_late), (row0, row1)
     sub = sublanes()
     lane = lanes(ROWS)
-
-    @pl.when(is_atmosphere)
-    def _():
-        tables = [sent[k * ROWS : (k + 1) * ROWS] for k in range(6)]
-        force[0:ROWS] = tables[0]
-        force[ROWS:] = jnp.where(sub < 4, tables[4][0:8], tables[3][8:16])
-        force_side[...] = jnp.where(lane < 64, tables[2], tables[1])
-        force1[...] = tables[5]
-
-    @pl.when(jnp.logical_not(is_atmosphere))
-    def _():
-        tables = [got[k * ROWS : (k + 1) * ROWS] for k in range(6)]
+    tables = [got[0, k * ROWS : (k + 1) * ROWS] for k in range(6)]
+    own_mix = [mix[level] for level in range(LEV - 1)]
+
+    def advance(force, force_rim, force_side, force1, before, before_side, unit_rim):
+        weights = transport_weights(vel[0], vel[1])
+        moved = []
+        for level in range(LEV):
+            tile = before[level, 0:ROWS] + force * unit[level]
+            rim = before[level, ROWS:] + force_rim * unit_rim[level]
+            there = before_side[level] + force_side * unit_side[level]
+            if level == 0:
+                top = tile
+            own = jnp.concatenate([tile, rim], axis=0)
+            moved.append(horizontal(own, there, weights, None, ROWS)[0])
+        moved[0] = moved[0] + force1
+        solved = solve(moved, own_mix, *stored(inverse, own_mix))
+        for level in range(LEV):
+            new_state[level] = solved[level]
+        return top, solved[0]
+
+    @pl.when(lax.axis_index("comp") == 0)
+    def _():
+        halo_step(state, mix, vel, columns, rows, inverse, inverse_side, own_before, own_side, own_rim)
+        rim = jnp.where(sub < 4, tables[4][0:8], tables[3][8:16])
+        side = jnp.where(lane < 64, tables[2], tables[1])
+        advance(tables[0], rim, side, tables[5], own_before, own_side, own_rim)
+        series[0] = tables[0]
+        series[1] = tables[5]
+
+    @pl.when(lax.axis_index("comp") != 0)
+    def _():
         rate = rate_in[...]
-        force[0:ROWS] = rate * regrid_tile(tables[0], index, weight)
-        force1[...] = rate * regrid_tile(tables[5], index, weight)
-        west, east = column_messages((early, late, to_early, to_late))
-        north, south = row_messages(row0, row1)
+        west, east = column_messages(columns)
+        north, south = row_messages(*rows)
 
         def of_rows(message, table, place):
             index8 = message[AT_INDEX : AT_INDEX + 8].astype(jnp.int32)
@@ -391,8 +427,6 @@
             block, offset = 8 * (AT_RATE // 8), AT_RATE % 8
             return roll(message[block : block + 8], place - offset, 0) * roll(total, place, 0)
 
-        force[ROWS:] = jnp.where(sub < 4, of_rows(south, tables[4], 0), of_rows(north, tables[3], 6))
-
         def of_columns(message, table, place):
             tile = message[0:ROWS]
             total = roll(gather_cells(table, tile.astype(jnp.int32)), AT_WEIGHT - AT_INDEX, 1) * tile
@@ -400,28 +434,15 @@
             total = total + roll(total, -2, 1)
             return roll(tile, place - AT_RATE, 1) * roll(total, place - AT_WEIGHT, 1)
 
-        force_side[...] = jnp.where(
+        rim = jnp.where(sub < 4, of_rows(south, tables[4], 0), of_rows(north, tables[3], 6))
+        side = jnp.where(
             lane < 64, of_columns(east, tables[2], 0), of_columns(west, tables[1], COLS - 2)
         )
-
-    own_weights = transport_weights(vel[0], vel[1])
-    f, f_side = force[...], force_side[...]
-    moved = []
-    for level in range(LEV):
-        own = before[level] + f * unit[level]
-        there = before_side[level] + f_side * unit_side[level]
-        if level == 0:
-            top = own[:ROWS]
-        moved.append(horizontal(own, there, own_weights, None, ROWS)[0])
-    moved[0] = moved[0] + force1[...]
-    own_mix = [mix[level] for level in range(LEV - 1)]
-    inverses = [inverse[level] for level in range(LEV)]
-    ratios = [own_mix[level] * inverses[level] for level in range(LEV - 1)]
-    solved = solve(moved, own_mix, inverses, ratios)
-    for level in range(LEV):
-        new_state[level] = solved[level]
-    series[0] = jnp.where(is_atmosphere, f[:ROWS], top)
-    series[1] = jnp.where(is_atmosphere, force1[...], solved[0])
+        force = rate * regrid_tile(tables[0], index, weight)
+        force1 = rate * regrid_tile(tables[5], index, weight)
+        top, last = advance(force, rim, side, force1, given_before, given_side, given_rim)
+        series[0] = top
+        series[1] = last
 
 
 def call(kernel, shapes, *args, scratch=(), place=pltpu.VMEM):
@@ -475,21 +496,22 @@
     )
     row1 = lax.ppermute(to_far, "lat", pairs(n_lat, 1, 2))
     row0 = lax.all_gather(to_near, "lat", axis_index_groups=partners(n_lat))
-    wide, narrow = (LEV, 24, COLS), (LEV, ROWS, COLS)
-    inverse, unit_top, seen = call(prepare_kernel, [narrow, tile, tile], prev, mix, index, weight)
-    (fluxes,) = call(
-        top_kernel, [(6 * ROWS, COLS)],
-        state, mix, vel, rate, flux, *columns, row0, row1, inverse, unit_top, seen,
-    )
-    got = lax.ppermute(fluxes, "comp", [(0, 1)])
-    parts = call(
-        first_step_kernel, [wide, narrow, wide, narrow],
-        state, mix, vel, *columns, row0, row1,
-    )
+    rows = (row0, row1)
+    narrow = (LEV, ROWS, COLS)
+    parts = [(LEV, 24, COLS), narrow, (LEV, 8, COLS)]
+    inverse, inverse_side, unit, unit_side, seen = call(
+        prepare_kernel, [narrow] * 4 + [tile], prev, mix, index, weight, *columns
+    )
+    fluxes, *before = call(
+        middle_kernel, [(6 * ROWS, COLS)] + parts,
+        state, mix, vel, rate, flux, *columns, *rows, inverse, inverse_side, unit, seen,
+    )
+    got = lax.all_gather(fluxes, "comp")
     new_state, series = call(
-        second_step_kernel, [(LEV, ROWS, COLS), (NSTEP, ROWS, COLS)],
-        mix, vel, rate, index, weight, *columns, row0, row1, *parts, inverse, fluxes, got,
-        scratch=[pltpu.VMEM(shape, jnp.float32) for shape in ((24, COLS), tile, tile)],
+        second_step_kernel, [narrow, (NSTEP, ROWS, COLS)],
+        state, mix, vel, rate, index, weight, *columns, *rows,
+        inverse, inverse_side, unit, unit_side, *before, got,
+        scratch=[pltpu.VMEM(shape, jnp.float32) for shape in parts],
     )
     return new_state[None], series[None]
 

time: 41.9 us -> 42.5 us (1.014)
  the two profiles are of different devices: /device:TPU:96 before, /device:TPU:24 now
where the time goes in v8:
time: 42.5 us; the launch traced here: 42.2 us
  starting transfers between devices  19.5 us (46%)
  blocking collectives  9.41 us (22%)
  waiting for transfers between devices  8.64 us (20%)
  Pallas kernels  4.03 us (9%)
  between operations  0.72 us (2%)
    ppermute x1, starting transfers between devices, per_device(): to_late = lax.ppermute(to_far, 'lon', [(j, i) for i, j in sent])  9.49 us
    ppermute x1, waiting for transfers between devices, per_device(): to_early = lax.ppermute(to_far, 'lon', sent)  8.53 us
    ppermute x1, starting transfers between devices, per_device(): early = lax.ppermute(to_near, 'lon', pairs(n_lon, 0, 4))  6.09 us
    all_gather x1, blocking collectives, per_device(): got = lax.all_gather(fluxes, 'comp')  4.98 us
    all_gather x1, blocking collectives, per_device(): row0 = lax.all_gather(to_near, 'lat', axis_index_groups=partners(n_lat))  4.42 us
    pallas_call x5, Pallas kernels, call(): pl.pallas_call(kernel, out_shape=[s if hasattr(s, 'dtype') else jax.Shape...  4.03 us
    ppermute x1, starting transfers between devices, per_device(): row1 = lax.ppermute(to_far, 'lat', pairs(n_lat, 1, 2))  1.92 us
    ppermute x1, starting transfers between devices, per_device(): to_early = lax.ppermute(to_far, 'lon', sent)  1.29 us
  transfers between devices with their start and end apart: 5, of which 2 were waited for; matrix products, arithmetic and copies ran while one was open for 0% of the time, Pallas kernels for 1%

profile of v8, /device:TPU:24, one launch (start us, length us, event | category | flops | bytes accessed | tf_op | source)
XLA Modules:
  0.0 42.2 jit_solution(3355656888159860312)
XLA Ops:
  0.6 1.3 %shard_map.95 = (f32[32,128]{1,0:T(8,128)S(1)}, f32[32,128]{1,0:T(8,128)S(1)}, f32[16,128]{1,0:T(8,128)S(1)}, f32[16,128]{1,0:T(8,128)S(1)}, f32[12,16,128]{2,1,...) custom-call(f32[12,16,128]{2,1,0:T(8,128)} %bitcast.14, ...), custom_call_target="tpu_custom_call" | custom-call | tf_op jit(solution)/shard_map/pallas_call | solution.py:449
  2.0 0.7 %collective-permute-start.1 = (f32[32,128]{1,0:T(8,128)S(1)}, f32[32,128]{1,0:T(8,128)S(1)}, u32[]{:S(2)}, u32[]{:S(2)}) collective-permute-start(f32[32,128]{1,0:T(8,128)S(1)} %get-tuple-element.31), channel_id=1, source_target_pairs={{2,3},{3,2},{6,7},{7,6},{10,11},{11,10},{14,15},{15,14},{18,19},{1... | collective-permute-start | bytes 49160 | tf_op jit(solution)/shard_map/ppermute | solution.py:490
  2.6 6.1 %collective-permute-start = (f32[32,128]{1,0:T(8,128)S(1)}, f32[32,128]{1,0:T(8,128)S(1)}, u32[]{:S(2)}, u32[]{:S(2)}) collective-permute-start(f32[32,128]{1,0:T(8,128)S(1)} %get-tuple-element.31), channel_id=1, source_target_pairs={{0,1},{1,0},{4,5},{5,4},{8,9},{9,8},{12,13},{13,12},{16,17},{17,16... | collective-permute-start | bytes 49160 | tf_op jit(solution)/shard_map/ppermute | solution.py:488
  8.7 9.5 %collective-permute-start.3 = (f32[32,128]{1,0:T(8,128)S(1)}, f32[32,128]{1,0:T(8,128)S(1)}, u32[]{:S(2)}, u32[]{:S(2)}) collective-permute-start(f32[32,128]{1,0:T(8,128)S(1)} %get-tuple-element.32), channel_id=1, source_target_pairs={{1,2},{4,3},{5,6},{8,7},{9,10},{12,11},{13,14},{0,15},{17,18},{20,... | collective-permute-start | bytes 49160 | tf_op jit(solution)/shard_map/ppermute | solution.py:489
  18.2 1.3 %collective-permute-start.2 = (f32[32,128]{1,0:T(8,128)S(1)}, f32[32,128]{1,0:T(8,128)S(1)}, u32[]{:S(2)}, u32[]{:S(2)}) collective-permute-start(f32[32,128]{1,0:T(8,128)S(1)} %get-tuple-element.32), channel_id=1, source_target_pairs={{2,1},{3,4},{6,5},{7,8},{10,9},{11,12},{14,13},{15,0},{18,17},{19,... | collective-permute-start | bytes 49160 | tf_op jit(solution)/shard_map/ppermute | solution.py:487
  19.5 0.0 collective-permute-done.1.late
  19.5 0.0 collective-permute-done.early
  19.5 0.1 collective-permute-done.3.to_late
  19.6 8.5 %collective-permute-done.2.to_early = f32[32,128]{1,0:T(8,128)S(1)} collective-permute-done((f32[32,128]{1,0:T(8,128)S(1)}, f32[32,128]{1,0:T(8,128)S(1)}, u32[]{:S(2)}, u32[]{:S(2)}) %collective-permute-start.2) | collective-permute-done | bytes 16416 | tf_op jit(solution)/shard_map/ppermute | solution.py:487
  28.2 1.9 %collective-permute-start.4 = (f32[104,128]{1,0:T(8,128)S(1)}, f32[104,128]{1,0:T(8,128)S(1)}, u32[]{:S(2)}, u32[]{:S(2)}) collective-permute-start(f32[104,128]{1,0:T(8,128)S(1)} %get-tuple-element.35), channel_id=1, source_target_pairs={{16,32},{32,16},{48,64},{64,48},{80,96},{96,80},{112,128},{128,112... | collective-permute-start | bytes 159752 | tf_op jit(solution)/shard_map/ppermute | solution.py:497
  30.2 0.5 %shard_map.97 = (f32[12,16,128]{2,1,0:T(8,128)S(1)}, f32[12,16,128]{2,1,0:T(8,128)S(1)}, f32[12,16,128]{2,1,0:T(8,128)S(1)}, f32[12,16,128]{2,1,0:T(8,128)S(1)}, f32[16,128]{1,0:T(8,128)S(1)}) custom-call(f32[2,16,128]{2,1,0:T(8,128)S(1)} %get-tuple-element.36.prev, f32[11,16,128]{2,1,0:T(8,128)S(1)} %get-tuple-element.26.mix, ...), custom_call_target="tpu_custom_call" | custom-call | tf_op jit(solution)/shard_map/pallas_call | solution.py:449
  30.6 4.4 %all-gather = f32[208,128]{1,0:T(8,128)S(1)} all-gather(f32[104,128]{1,0:T(8,128)S(1)} %get-tuple-element.34), channel_id=2, replica_groups={{0,16},{32,48},{64,80},{96,112},{128,144},{160,176},{192,208},{224,240}..., dimensions={0}, use_global_device_ids=true | all-gather | bytes 159744 | tf_op jit(solution)/shard_map/all_gather | solution.py:498
  35.0 0.0 collective-permute-done.4.row1
  35.0 0.3 shard_map.98
  35.3 5.0 %all-gather.1 = f32[192,128]{1,0:T(8,128)S(1)} all-gather(f32[96,128]{1,0:T(8,128)S(1)} %get-tuple-element.45), channel_id=3, replica_groups=mesh['comp'=2,'lat'=16,'lon'=16] {'comp'}, dimensions={0}, use_global_device_ids=true | all-gather | bytes 147456 | tf_op jit(solution)/shard_map/all_gather | solution.py:509
  40.3 1.9 %shard_map.99 = (f32[12,16,128]{2,1,0:T(8,128)}, f32[2,16,128]{2,1,0:T(8,128)}) custom-call(f32[12,16,128]{2,1,0:T(8,128)S(1)} %get-tuple-element.25.state, f32[11,16,128]{2,1,0:T(8,128)S(1)} %get-tuple-element.26.mix, f32[2,16,128]{2,1,0:T(8,128)S(1)} %get-tuple-element.27.vel, f32[16,128]{1,0:T(8,128)S(1)} %get-tuple-element.28.rate_in.rate, ...), custom_call_target="tpu_custom_call" | custom-call | tf_op jit(solution)/shard_map/pallas_call | solution.py:449
  (1 shorter events, 0.0 us)
Async XLA Ops:
  2.0 17.6 %collective-permute-start.1 = (f32[32,128]{1,0:T(8,128)S(1)}, f32[32,128]{1,0:T(8,128)S(1)}, u32[]{:S(2)}, u32[]{:S(2)}) collective-permute-start(f32[32,128]{1,0:T(8,128)S(1)} %get-tuple-element.31), channel_id=1, source_target_pairs={{2,3},{3,2},{6,7},{7,6},{10,11},{11,10},{14,15},{15,14},{18,19},{1... | collective-permute-start | bytes 49160 | tf_op jit(solution)/shard_map/ppermute | solution.py:490
  2.6 16.9 %collective-permute-start = (f32[32,128]{1,0:T(8,128)S(1)}, f32[32,128]{1,0:T(8,128)S(1)}, u32[]{:S(2)}, u32[]{:S(2)}) collective-permute-start(f32[32,128]{1,0:T(8,128)S(1)} %get-tuple-element.31), channel_id=1, source_target_pairs={{0,1},{1,0},{4,5},{5,4},{8,9},{9,8},{12,13},{13,12},{16,17},{17,16... | collective-permute-start | bytes 49160 | tf_op jit(solution)/shard_map/ppermute | solution.py:488
  8.7 10.9 %collective-permute-start.3 = (f32[32,128]{1,0:T(8,128)S(1)}, f32[32,128]{1,0:T(8,128)S(1)}, u32[]{:S(2)}, u32[]{:S(2)}) collective-permute-start(f32[32,128]{1,0:T(8,128)S(1)} %get-tuple-element.32), channel_id=1, source_target_pairs={{1,2},{4,3},{5,6},{8,7},{9,10},{12,11},{13,14},{0,15},{17,18},{20,... | collective-permute-start | bytes 49160 | tf_op jit(solution)/shard_map/ppermute | solution.py:489
  18.2 10.0 %collective-permute-start.2 = (f32[32,128]{1,0:T(8,128)S(1)}, f32[32,128]{1,0:T(8,128)S(1)}, u32[]{:S(2)}, u32[]{:S(2)}) collective-permute-start(f32[32,128]{1,0:T(8,128)S(1)} %get-tuple-element.32), channel_id=1, source_target_pairs={{2,1},{3,4},{6,5},{7,8},{10,9},{11,12},{14,13},{15,0},{18,17},{19,... | collective-permute-start | bytes 49160 | tf_op jit(solution)/shard_map/ppermute | solution.py:487
  28.2 6.8 %collective-permute-start.4 = (f32[104,128]{1,0:T(8,128)S(1)}, f32[104,128]{1,0:T(8,128)S(1)}, u32[]{:S(2)}, u32[]{:S(2)}) collective-permute-start(f32[104,128]{1,0:T(8,128)S(1)} %get-tuple-element.35), channel_id=1, source_target_pairs={{16,32},{32,16},{48,64},{64,48},{80,96},{96,80},{112,128},{128,112... | collective-permute-start | bytes 159752 | tf_op jit(solution)/shard_map/ppermute | solution.py:497

commit v9 on v8

--- a/solution.py
+++ b/solution.py
@@ -199,26 +199,24 @@
     return weights(east), weights(north)
 
 
-def horizontal(own, side, own_weights, side_weights, own_rows):
-    shifts = (2, 1, -1, -2)
-    result = own[:own_rows] * (1.0 - 4.0 * smoothing)
-    for shift, factor in zip(shifts, own_weights[1]):
-        result = result + factor * roll(own, shift, 0)[:own_rows]
-    lane = lanes(own_rows)
-    side_result = None
-    if side_weights is not None:
-        side_result = side[:ROWS] * (1.0 - 4.0 * smoothing)
-        for shift, factor in zip(shifts, side_weights[1]):
-            side_result = side_result + factor * roll(side, shift, 0)[:ROWS]
-    for k, shift in enumerate(shifts):
+SHIFTS = (2, 1, -1, -2)
+
+
+def along_longitude(own, side, weights):
+    lane = lanes(own.shape[0])
+    result = own * (1.0 - 4.0 * smoothing)
+    for shift, factor in zip(SHIFTS, weights[0]):
         cut = lane >= COLS - shift if shift > 0 else lane < -shift
-        own_part, side_part = own[:own_rows], side[:own_rows]
-        moved = roll(jnp.where(cut, side_part, own_part), shift, 1)
-        result = result + own_weights[0][k] * moved
-        if side_weights is not None:
-            there = jnp.where(cut[:ROWS], own_part[:ROWS], side_part[:ROWS])
-            side_result = side_result + side_weights[0][k] * roll(there, shift, 1)
-    return result, side_result
+        result = result + factor * roll(jnp.where(cut, side, own), shift, 1)
+    return result
+
+
+def along_latitude(own, weights, rows):
+    result = None
+    for shift, factor in zip(SHIFTS, weights[1]):
+        tap = factor * roll(own, shift, 0)[:rows]
+        result = tap if result is None else result + tap
+    return result
 
 
 def factors(mix):
@@ -265,24 +263,41 @@
 IMPULSE = [1.0] + [None] * (LEV - 1)
 
 
-def prepare_kernel(
-    prev, mix, index, weight, early, late, to_early, to_late, inverse, inverse_side, unit, unit_side, seen
+def prepare_own_kernel(prev, mix, index, weight, inverse, unit, seen):
+    own_mix = [mix[level] for level in range(LEV - 1)]
+    inverses, ratios = factors(own_mix)
+    impulse = solve(IMPULSE, own_mix, inverses, ratios)
+    for level in range(LEV):
+        inverse[level] = inverses[level]
+        unit[level] = impulse[level]
+
+    @pl.when(lax.axis_index("comp") == 0)
+    def _():
+        seen[...] = regrid_tile(prev[1], index, weight)
+
+
+def prepare_side_kernel(
+    state, vel, early, late, to_early, to_late,
+    inverse, unit, side_mix, side_state, lon_own, lon_side,
 ):
     west, east = column_messages((early, late, to_early, to_late))
-    own_mix = [mix[level] for level in range(LEV - 1)]
-    side_mix = [side_of(west, east, AT_MIX + 2 * level, 2, ROWS) for level in range(LEV - 1)]
-    found = [(factors(m), m) for m in (own_mix, side_mix)]
-    for ((inverses, ratios), m), inverse_out, out in zip(
-        found, (inverse, inverse_side), (unit, unit_side)
-    ):
-        impulse = solve(IMPULSE, m, inverses, ratios)
-        for level in range(LEV):
-            inverse_out[level] = inverses[level]
-            out[level] = impulse[level]
-
-    @pl.when(lax.axis_index("comp") == 0)
-    def _():
-        seen[...] = regrid_tile(prev[1], index, weight)
+    own_weights = transport_weights(vel[0], vel[1])
+    side_weights = transport_weights(
+        *(side_of(west, east, AT_VEL + 2 * part, 2, ROWS) for part in range(2))
+    )
+    for level in range(LEV):
+        there = side_of(west, east, 4 * level, 4, ROWS)
+        side_state[level] = there
+        lon_own[level] = along_longitude(state[level], there, own_weights)
+        lon_side[level] = along_longitude(there, state[level], side_weights)
+    mixes = [side_of(west, east, AT_MIX + 2 * level, 2, ROWS) for level in range(LEV - 1)]
+    inverses, ratios = factors(mixes)
+    impulse = solve(IMPULSE, mixes, inverses, ratios)
+    for level in range(LEV):
+        inverse[level] = inverses[level]
+        unit[level] = impulse[level]
+        if level < LEV - 1:
+            side_mix[level] = mixes[level]
 
 
 def stored(inverse, mixes):
@@ -290,15 +305,14 @@
     return inverses, [mixes[level] * inverses[level] for level in range(LEV - 1)]
 
 
-def top_step(state, mix, vel, rate, flux, columns, rows, inverse, unit, seen, fluxes):
+def top_step(state, mix, vel, rate, flux, columns, rows, inverse, unit, seen, lon_own, fluxes):
     west, east = column_messages(columns)
     north, south = row_messages(*rows)
     weights = transport_weights(vel[0], vel[1])
     moved = []
     for level in range(LEV):
         own = jnp.concatenate([state[level], rim_of_levels(north, south, level)], axis=0)
-        there = side_of(west[0:ROWS], east[0:ROWS], 4 * level, 4, ROWS)
-        moved.append(horizontal(own, there, weights, None, ROWS)[0])
+        moved.append(lon_own[level] + along_latitude(own, weights, ROWS))
     own_mix = [mix[level] for level in range(LEV - 1)]
     top = solve(moved, own_mix, *stored(inverse, own_mix))[0] + flux[...] * unit[0]
     fluxes[0:ROWS] = flux[...]
@@ -309,7 +323,7 @@
     fluxes[5 * ROWS :] = rate[...] * (seen[...] - top)
 
 
-def halo_step(state, mix, vel, columns, rows, inverse, inverse_side, before, before_side, unit_rim):
+def halo_step(state, mix, vel, columns, rows, inverse, side, before, before_side, unit_rim):
     west, east = column_messages(columns)
     north, south = row_messages(*rows)
     at_lat = lax.axis_index("lat")
@@ -322,37 +336,34 @@
         a, b = roll(a, -offset, 0), roll(b, 6 - offset, 0)
         return jnp.where(sub < 2, a, jnp.where(sub >= 6, b, 0.0))
 
-    def cornered(packed, at):
-        a, b = south[AT_WEST : AT_WEST + 8], north[AT_WEST : AT_WEST + 8]
-        if at == AT_WEST:
-            rim = jnp.where(sub < 4, a, roll(b, 4, 0))
-        else:
-            rim = jnp.where(sub < 4, roll(a, 4, 0), b)
-        return jnp.concatenate([packed[0:ROWS], rim], axis=0)
-
-    west_tile, east_tile = cornered(west, AT_WEST), cornered(east, AT_EAST)
-
-    def side(at, width, rows):
-        return side_of(west_tile, east_tile, at, width, rows)
-
+    inverse_side, side_mix_ref, side_state, lon_own, lon_side = side
+    a, b = south[AT_WEST : AT_WEST + 8], north[AT_WEST : AT_WEST + 8]
+    west_rim = jnp.where(sub < 4, a, roll(b, 4, 0))
+    east_rim = jnp.where(sub < 4, roll(a, 4, 0), b)
     own_mix = [mix[level] for level in range(LEV - 1)]
+    side_mix = [side_mix_ref[level] for level in range(LEV - 1)]
     rim_mix = [rim2(AT_MIX + 2 * level) for level in range(LEV - 1)]
-    side_mix = [side(AT_MIX + 2 * level, 2, ROWS) for level in range(LEV - 1)]
-    own_vel = [
-        jnp.concatenate([vel[part], rim2(AT_VEL + 2 * part)], axis=0) for part in range(2)
-    ]
-    side_vel = [side(AT_VEL + 2 * part, 2, ROWS) for part in range(2)]
-    own_weights, side_weights = transport_weights(*own_vel), transport_weights(*side_vel)
+    rim_vel = [rim2(AT_VEL + 2 * part) for part in range(2)]
+    own_weights = transport_weights(
+        *(jnp.concatenate([vel[part], rim_vel[part]], axis=0) for part in range(2))
+    )
+    rim_weights = transport_weights(*rim_vel)
+    side_weights = transport_weights(
+        *(side_of(west, east, AT_VEL + 2 * part, 2, ROWS) for part in range(2))
+    )
     rim_factors = factors(rim_mix)
-    moved, moved_side = [], []
-    for level in range(LEV):
-        own = jnp.concatenate([state[level], rim_of_levels(north, south, level)], axis=0)
-        a, b = horizontal(own, side(4 * level, 4, 24), own_weights, side_weights, 24)
-        moved.append(a)
-        moved_side.append(b)
-    rim = solve([x[ROWS:] for x in moved], rim_mix, *rim_factors)
+    moved, moved_rim, moved_side = [], [], []
+    for level in range(LEV):
+        rim = rim_of_levels(north, south, level)
+        side_rim = side_of(west_rim, east_rim, 4 * level, 4, 8)
+        taps = along_latitude(jnp.concatenate([state[level], rim], axis=0), own_weights, 24)
+        moved.append(lon_own[level] + taps[:ROWS])
+        moved_rim.append(along_longitude(rim, side_rim, rim_weights) + taps[ROWS:])
+        there = jnp.concatenate([side_state[level], side_rim], axis=0)
+        moved_side.append(lon_side[level] + along_latitude(there, side_weights, ROWS))
+    rim = solve(moved_rim, rim_mix, *rim_factors)
     impulse = solve(IMPULSE, rim_mix, *rim_factors)
-    own = solve([x[:ROWS] for x in moved], own_mix, *stored(inverse, own_mix))
+    own = solve(moved, own_mix, *stored(inverse, own_mix))
     there = solve(moved_side, side_mix, *stored(inverse_side, side_mix))
     for level in range(LEV):
         before[level, 0:ROWS] = own[level]
@@ -363,22 +374,25 @@
 
 def middle_kernel(
     state, mix, vel, rate, flux, early, late, to_early, to_late, row0, row1,
-    inverse, inverse_side, unit, seen, fluxes, before, before_side, unit_rim,
+    inverse, unit, seen, inverse_side, side_mix, side_state, lon_own, lon_side,
+    fluxes, before, before_side, unit_rim,
 ):
     columns, rows = (early, late, to_early, to_late), (row0, row1)
+    side = (inverse_side, side_mix, side_state, lon_own, lon_side)
 
     @pl.when(lax.axis_index("comp") == 0)
     def _():
-        top_step(state, mix, vel, rate, flux, columns, rows, inverse, unit, seen, fluxes)
+        top_step(state, mix, vel, rate, flux, columns, rows, inverse, unit, seen, lon_own, fluxes)
 
     @pl.when(lax.axis_index("comp") != 0)
     def _():
-        halo_step(state, mix, vel, columns, rows, inverse, inverse_side, before, before_side, unit_rim)
+        halo_step(state, mix, vel, columns, rows, inverse, side, before, before_side, unit_rim)
 
 
 def second_step_kernel(
     state, mix, vel, rate_in, index, weight, early, late, to_early, to_late, row0, row1,
-    inverse, inverse_side, unit, unit_side, given_before, given_side, given_rim, got,
+    inverse, unit, inverse_side, side_mix, side_state, lon_own, lon_side, unit_side,
+    given_before, given_side, given_rim, got,
     new_state, series, own_before, own_side, own_rim,
 ):
     columns, rows = (early, late, to_early, to_late), (row0, row1)
@@ -397,7 +411,8 @@
             if level == 0:
                 top = tile
             own = jnp.concatenate([tile, rim], axis=0)
-            moved.append(horizontal(own, there, weights, None, ROWS)[0])
+            taps = along_latitude(own, weights, ROWS)
+            moved.append(along_longitude(tile, there, weights) + taps)
         moved[0] = moved[0] + force1
         solved = solve(moved, own_mix, *stored(inverse, own_mix))
         for level in range(LEV):
@@ -406,7 +421,8 @@
 
     @pl.when(lax.axis_index("comp") == 0)
     def _():
-        halo_step(state, mix, vel, columns, rows, inverse, inverse_side, own_before, own_side, own_rim)
+        side = (inverse_side, side_mix, side_state, lon_own, lon_side)
+        halo_step(state, mix, vel, columns, rows, inverse, side, own_before, own_side, own_rim)
         rim = jnp.where(sub < 4, tables[4][0:8], tables[3][8:16])
         side = jnp.where(lane < 64, tables[2], tables[1])
         advance(tables[0], rim, side, tables[5], own_before, own_side, own_rim)
@@ -499,18 +515,21 @@
     rows = (row0, row1)
     narrow = (LEV, ROWS, COLS)
     parts = [(LEV, 24, COLS), narrow, (LEV, 8, COLS)]
-    inverse, inverse_side, unit, unit_side, seen = call(
-        prepare_kernel, [narrow] * 4 + [tile], prev, mix, index, weight, *columns
-    )
+    inverse, unit, seen = call(prepare_own_kernel, [narrow, narrow, tile], prev, mix, index, weight)
+    inverse_side, unit_side, *side = call(
+        prepare_side_kernel,
+        [narrow, narrow, (LEV - 1, ROWS, COLS), narrow, narrow, narrow], state, vel, *columns,
+    )
+    known = (inverse_side, *side)
     fluxes, *before = call(
         middle_kernel, [(6 * ROWS, COLS)] + parts,
-        state, mix, vel, rate, flux, *columns, *rows, inverse, inverse_side, unit, seen,
+        state, mix, vel, rate, flux, *columns, *rows, inverse, unit, seen, *known,
     )
     got = lax.all_gather(fluxes, "comp")
     new_state, series = call(
         second_step_kernel, [narrow, (NSTEP, ROWS, COLS)],
         state, mix, vel, rate, index, weight, *columns, *rows,
-        inverse, inverse_side, unit, unit_side, *before, got,
+        inverse, unit, *known, unit_side, *before, got,
         scratch=[pltpu.VMEM(shape, jnp.float32) for shape in parts],
     )
     return new_state[None], series[None]

time: 42.5 us -> 42 us (0.988)
    pallas_call x5 -> x6, Pallas kernels: 4.03 us -> 3.8 us  [call(): pl.pallas_call(kernel, out_shape=[s if hasattr(s, 'dtype') else jax.Shape...]
  transfers between devices with their start and end apart: 5 -> 5, of which waited for: 2 -> 2; matrix products, arithmetic and copies ran while one was open for 0% -> 0% of each run, Pallas kernels for 1% -> 3%
where the time goes in v9:
time: 42 us; the launch traced here: 41.8 us
  starting transfers between devices  19.5 us (46%)
  blocking collectives  9.18 us (22%)
  waiting for transfers between devices  8.64 us (21%)
  Pallas kernels  3.8 us (9%)
  between operations  0.72 us (2%)
    ppermute x1, starting transfers between devices, per_device(): to_late = lax.ppermute(to_far, 'lon', [(j, i) for i, j in sent])  9.49 us
    ppermute x1, waiting for transfers between devices, per_device(): to_early = lax.ppermute(to_far, 'lon', sent)  8.53 us
    ppermute x1, starting transfers between devices, per_device(): early = lax.ppermute(to_near, 'lon', pairs(n_lon, 0, 4))  6.09 us
    all_gather x1, blocking collectives, per_device(): got = lax.all_gather(fluxes, 'comp')  4.76 us
    all_gather x1, blocking collectives, per_device(): row0 = lax.all_gather(to_near, 'lat', axis_index_groups=partners(n_lat))  4.42 us
    pallas_call x6, Pallas kernels, call(): pl.pallas_call(kernel, out_shape=[s if hasattr(s, 'dtype') else jax.Shape...  3.8 us
    ppermute x1, starting transfers between devices, per_device(): row1 = lax.ppermute(to_far, 'lat', pairs(n_lat, 1, 2))  1.92 us
    ppermute x1, starting transfers between devices, per_device(): to_early = lax.ppermute(to_far, 'lon', sent)  1.29 us
  transfers between devices with their start and end apart: 5, of which 2 were waited for; matrix products, arithmetic and copies ran while one was open for 0% of the time, Pallas kernels for 3%

profile of v9, /device:TPU:24, one launch (start us, length us, event | category | flops | bytes accessed | tf_op | source)
XLA Modules:
  0.0 41.8 jit_solution(6202212443195062733)
XLA Ops:
  0.6 1.3 %shard_map.95 = (f32[32,128]{1,0:T(8,128)S(1)}, f32[32,128]{1,0:T(8,128)S(1)}, f32[16,128]{1,0:T(8,128)S(1)}, f32[16,128]{1,0:T(8,128)S(1)}, f32[12,16,128]{2,1,...) custom-call(f32[12,16,128]{2,1,0:T(8,128)} %bitcast.14, ...), custom_call_target="tpu_custom_call" | custom-call | tf_op jit(solution)/shard_map/pallas_call | solution.py:465
  2.0 0.7 %collective-permute-start.1 = (f32[32,128]{1,0:T(8,128)S(1)}, f32[32,128]{1,0:T(8,128)S(1)}, u32[]{:S(2)}, u32[]{:S(2)}) collective-permute-start(f32[32,128]{1,0:T(8,128)S(1)} %get-tuple-element.35), channel_id=1, source_target_pairs={{2,3},{3,2},{6,7},{7,6},{10,11},{11,10},{14,15},{15,14},{18,19},{1... | collective-permute-start | bytes 49160 | tf_op jit(solution)/shard_map/ppermute | solution.py:506
  2.6 6.1 %collective-permute-start = (f32[32,128]{1,0:T(8,128)S(1)}, f32[32,128]{1,0:T(8,128)S(1)}, u32[]{:S(2)}, u32[]{:S(2)}) collective-permute-start(f32[32,128]{1,0:T(8,128)S(1)} %get-tuple-element.35), channel_id=1, source_target_pairs={{0,1},{1,0},{4,5},{5,4},{8,9},{9,8},{12,13},{13,12},{16,17},{17,16... | collective-permute-start | bytes 49160 | tf_op jit(solution)/shard_map/ppermute | solution.py:504
  8.7 9.5 %collective-permute-start.3 = (f32[32,128]{1,0:T(8,128)S(1)}, f32[32,128]{1,0:T(8,128)S(1)}, u32[]{:S(2)}, u32[]{:S(2)}) collective-permute-start(f32[32,128]{1,0:T(8,128)S(1)} %get-tuple-element.36), channel_id=1, source_target_pairs={{1,2},{4,3},{5,6},{8,7},{9,10},{12,11},{13,14},{0,15},{17,18},{20,... | collective-permute-start | bytes 49160 | tf_op jit(solution)/shard_map/ppermute | solution.py:505
  18.2 1.3 %collective-permute-start.2 = (f32[32,128]{1,0:T(8,128)S(1)}, f32[32,128]{1,0:T(8,128)S(1)}, u32[]{:S(2)}, u32[]{:S(2)}) collective-permute-start(f32[32,128]{1,0:T(8,128)S(1)} %get-tuple-element.36), channel_id=1, source_target_pairs={{2,1},{3,4},{6,5},{7,8},{10,9},{11,12},{14,13},{15,0},{18,17},{19,... | collective-permute-start | bytes 49160 | tf_op jit(solution)/shard_map/ppermute | solution.py:503
  19.5 0.0 collective-permute-done.1.late
  19.5 0.0 collective-permute-done.early
  19.5 0.1 collective-permute-done.3.to_late
  19.6 8.5 %collective-permute-done.2.to_early = f32[32,128]{1,0:T(8,128)S(1)} collective-permute-done((f32[32,128]{1,0:T(8,128)S(1)}, f32[32,128]{1,0:T(8,128)S(1)}, u32[]{:S(2)}, u32[]{:S(2)}) %collective-permute-start.2) | collective-permute-done | bytes 16416 | tf_op jit(solution)/shard_map/ppermute | solution.py:503
  28.2 1.9 %collective-permute-start.4 = (f32[104,128]{1,0:T(8,128)S(1)}, f32[104,128]{1,0:T(8,128)S(1)}, u32[]{:S(2)}, u32[]{:S(2)}) collective-permute-start(f32[104,128]{1,0:T(8,128)S(1)} %get-tuple-element.39), channel_id=1, source_target_pairs={{16,32},{32,16},{48,64},{64,48},{80,96},{96,80},{112,128},{128,112... | collective-permute-start | bytes 159752 | tf_op jit(solution)/shard_map/ppermute | solution.py:513
  30.2 0.4 shard_map.97
  30.5 0.8 %shard_map.98 = (f32[12,16,128]{2,1,0:T(8,128)S(1)}, f32[12,16,128]{2,1,0:T(8,128)S(1)}, f32[11,16,128]{2,1,0:T(8,128)S(1)}, f32[12,16,128]{2,1,0:T(8,128)S(1)},...) custom-call(f32[12,16,128]{2,1,0:T(8,128)S(1)} %get-tuple-element.29.state, ...), custom_call_target="tpu_custom_call" | custom-call | tf_op jit(solution)/shard_map/pallas_call | solution.py:465
  31.4 4.4 %all-gather = f32[208,128]{1,0:T(8,128)S(1)} all-gather(f32[104,128]{1,0:T(8,128)S(1)} %get-tuple-element.38), channel_id=2, replica_groups={{0,16},{32,48},{64,80},{96,112},{128,144},{160,176},{192,208},{224,240}..., dimensions={0}, use_global_device_ids=true | all-gather | bytes 159744 | tf_op jit(solution)/shard_map/all_gather | solution.py:514
  35.8 0.0 collective-permute-done.4.row1
  35.8 0.1 shard_map.99
  35.9 4.8 %all-gather.1 = f32[192,128]{1,0:T(8,128)S(1)} all-gather(f32[96,128]{1,0:T(8,128)S(1)} %get-tuple-element.53), channel_id=3, replica_groups=mesh['comp'=2,'lat'=16,'lon'=16] {'comp'}, dimensions={0}, use_global_device_ids=true | all-gather | bytes 147456 | tf_op jit(solution)/shard_map/all_gather | solution.py:528
  40.7 1.1 %shard_map.100 = (f32[12,16,128]{2,1,0:T(8,128)}, f32[2,16,128]{2,1,0:T(8,128)}) custom-call(f32[12,16,128]{2,1,0:T(8,128)S(1)} %get-tuple-element.29.state, f32[11,16,128]{2,1,0:T(8,128)S(1)} %get-tuple-element.30.mix, f32[2,16,128]{2,1,0:T(8,128)S(1)} %get-tuple-element.31.vel, f32[16,128]{1,0:T(8,128)S(1)} %get-tuple-element.32.rate_in.rate, ...), custom_call_target="tpu_custom_call" | custom-call | tf_op jit(solution)/shard_map/pallas_call | solution.py:465
  (1 shorter events, 0.0 us)
Async XLA Ops:
  2.0 17.6 %collective-permute-start.1 = (f32[32,128]{1,0:T(8,128)S(1)}, f32[32,128]{1,0:T(8,128)S(1)}, u32[]{:S(2)}, u32[]{:S(2)}) collective-permute-start(f32[32,128]{1,0:T(8,128)S(1)} %get-tuple-element.35), channel_id=1, source_target_pairs={{2,3},{3,2},{6,7},{7,6},{10,11},{11,10},{14,15},{15,14},{18,19},{1... | collective-permute-start | bytes 49160 | tf_op jit(solution)/shard_map/ppermute | solution.py:506
  2.6 16.9 %collective-permute-start = (f32[32,128]{1,0:T(8,128)S(1)}, f32[32,128]{1,0:T(8,128)S(1)}, u32[]{:S(2)}, u32[]{:S(2)}) collective-permute-start(f32[32,128]{1,0:T(8,128)S(1)} %get-tuple-element.35), channel_id=1, source_target_pairs={{0,1},{1,0},{4,5},{5,4},{8,9},{9,8},{12,13},{13,12},{16,17},{17,16... | collective-permute-start | bytes 49160 | tf_op jit(solution)/shard_map/ppermute | solution.py:504
  8.7 10.9 %collective-permute-start.3 = (f32[32,128]{1,0:T(8,128)S(1)}, f32[32,128]{1,0:T(8,128)S(1)}, u32[]{:S(2)}, u32[]{:S(2)}) collective-permute-start(f32[32,128]{1,0:T(8,128)S(1)} %get-tuple-element.36), channel_id=1, source_target_pairs={{1,2},{4,3},{5,6},{8,7},{9,10},{12,11},{13,14},{0,15},{17,18},{20,... | collective-permute-start | bytes 49160 | tf_op jit(solution)/shard_map/ppermute | solution.py:505
  18.2 10.0 %collective-permute-start.2 = (f32[32,128]{1,0:T(8,128)S(1)}, f32[32,128]{1,0:T(8,128)S(1)}, u32[]{:S(2)}, u32[]{:S(2)}) collective-permute-start(f32[32,128]{1,0:T(8,128)S(1)} %get-tuple-element.36), channel_id=1, source_target_pairs={{2,1},{3,4},{6,5},{7,8},{10,9},{11,12},{14,13},{15,0},{18,17},{19,... | collective-permute-start | bytes 49160 | tf_op jit(solution)/shard_map/ppermute | solution.py:503
  28.2 7.6 %collective-permute-start.4 = (f32[104,128]{1,0:T(8,128)S(1)}, f32[104,128]{1,0:T(8,128)S(1)}, u32[]{:S(2)}, u32[]{:S(2)}) collective-permute-start(f32[104,128]{1,0:T(8,128)S(1)} %get-tuple-element.39), channel_id=1, source_target_pairs={{16,32},{32,16},{48,64},{64,48},{80,96},{96,80},{112,128},{128,112... | collective-permute-start | bytes 159752 | tf_op jit(solution)/shard_map/ppermute | solution.py:513

commit v10 on v9

--- a/solution.py
+++ b/solution.py
@@ -137,13 +137,19 @@
         msg1[ROWS:] = nothing
 
 
+def starts_early():
+    return lax.rem(lax.axis_index("lon"), 4) < 2
+
+
+def sides(near, far):
+    odd = lax.rem(lax.axis_index("lon"), 2) == 1
+    return jnp.where(odd, near, far), jnp.where(odd, far, near)
+
+
 def column_messages(got):
-    at_lon = lax.axis_index("lon")
-    odd = lax.rem(at_lon, 2) == 1
-    starts_early = lax.rem(at_lon, 4) < 2
-    near = jnp.where(starts_early, got[0][...], got[1][...])
-    far = jnp.where(starts_early, got[2][...], got[3][...])
-    return jnp.where(odd, near, far), jnp.where(odd, far, near)
+    early = starts_early()
+    near = jnp.where(early, got[0][...], got[1][...])
+    return sides(near, jnp.where(early, got[2][...], got[3][...]))
 
 
 def pack_rows_kernel(
@@ -276,11 +282,10 @@
         seen[...] = regrid_tile(prev[1], index, weight)
 
 
-def prepare_side_kernel(
-    state, vel, early, late, to_early, to_late,
-    inverse, unit, side_mix, side_state, lon_own, lon_side,
+def prepare_side(
+    state, vel, near, far, inverse, unit, side_mix, side_state, lon_own, lon_side
 ):
-    west, east = column_messages((early, late, to_early, to_late))
+    west, east = sides(near[0:ROWS], far[0:ROWS])
     own_weights = transport_weights(vel[0], vel[1])
     side_weights = transport_weights(
         *(side_of(west, east, AT_VEL + 2 * part, 2, ROWS) for part in range(2))
@@ -298,6 +303,18 @@
         unit[level] = impulse[level]
         if level < LEV - 1:
             side_mix[level] = mixes[level]
+
+
+def side_early_kernel(state, vel, near, far, *out):
+    @pl.when(starts_early())
+    def _():
+        prepare_side(state, vel, near, far, *out)
+
+
+def side_late_kernel(state, vel, near, far, *both):
+    @pl.when(jnp.logical_not(starts_early()))
+    def _():
+        prepare_side(state, vel, near, far, *both[len(both) // 2 :])
 
 
 def stored(inverse, mixes):
@@ -461,7 +478,7 @@
         series[1] = last
 
 
-def call(kernel, shapes, *args, scratch=(), place=pltpu.VMEM):
+def call(kernel, shapes, *args, scratch=(), place=pltpu.VMEM, aliases=None):
     return pl.pallas_call(
         kernel,
         out_shape=[s if hasattr(s, "dtype") else jax.ShapeDtypeStruct(s, jnp.float32) for s in shapes],
@@ -469,6 +486,7 @@
         out_specs=[pl.BlockSpec(memory_space=pltpu.VMEM)] * len(shapes),
         scratch_shapes=list(scratch),
         compiler_params=pltpu.CompilerParams(vmem_limit_bytes=16 * 1024 * 1024),
+        input_output_aliases=aliases or {},
         interpret=INTERPRET,
     )(*args)
 
@@ -516,9 +534,11 @@
     narrow = (LEV, ROWS, COLS)
     parts = [(LEV, 24, COLS), narrow, (LEV, 8, COLS)]
     inverse, unit, seen = call(prepare_own_kernel, [narrow, narrow, tile], prev, mix, index, weight)
+    shapes = [narrow, narrow, (LEV - 1, ROWS, COLS), narrow, narrow, narrow]
+    side = call(side_early_kernel, shapes, state, vel, early, to_early)
     inverse_side, unit_side, *side = call(
-        prepare_side_kernel,
-        [narrow, narrow, (LEV - 1, ROWS, COLS), narrow, narrow, narrow], state, vel, *columns,
+        side_late_kernel, shapes, state, vel, late, to_late, *side,
+        aliases={4 + k: k for k in range(len(shapes))},
     )
     known = (inverse_side, *side)
     fluxes, *before = call(

time: 42 us -> 35.9 us (0.85)
  waiting for transfers between devices: 8.64 us -> 1.4 us
  starting transfers between devices: 19.5 us -> 20.1 us
  blocking collectives: 9.18 us -> 9.64 us
    ppermute x1, waiting for transfers between devices: 8.53 us -> 0.01 us  [per_device(): to_early = lax.ppermute(to_far, 'lon', sent)]
    ppermute x1, waiting for transfers between devices: 0.1 us -> 1.39 us  [per_device(): to_late = lax.ppermute(to_far, 'lon', [(j, i) for i, j in sent])]
    ppermute x1, starting transfers between devices: 9.49 us -> 10.1 us  [per_device(): to_late = lax.ppermute(to_far, 'lon', [(j, i) for i, j in sent])]
    all_gather x1, blocking collectives: 4.76 us -> 5.22 us  [per_device(): got = lax.all_gather(fluxes, 'comp')]
    pallas_call x6 -> x7, Pallas kernels: 3.8 us -> 3.83 us  [call(): pl.pallas_call(kernel, out_shape=[s if hasattr(s, 'dtype') else jax.Shape...]
  transfers between devices with their start and end apart: 5 -> 5, of which waited for: 2 -> 1; matrix products, arithmetic and copies ran while one was open for 0% -> 0% of each run, Pallas kernels for 3% -> 3%
where the time goes in v10:
time: 35.9 us; the launch traced here: 35.7 us
  starting transfers between devices  20.1 us (56%)
  blocking collectives  9.64 us (27%)
  Pallas kernels  3.83 us (11%)
  waiting for transfers between devices  1.4 us (4%)
  between operations  0.74 us (2%)
    ppermute x1, starting transfers between devices, per_device(): to_late = lax.ppermute(to_far, 'lon', [(j, i) for i, j in sent])  10.1 us
    ppermute x1, starting transfers between devices, per_device(): early = lax.ppermute(to_near, 'lon', pairs(n_lon, 0, 4))  6.09 us
    all_gather x1, blocking collectives, per_device(): got = lax.all_gather(fluxes, 'comp')  5.22 us
    all_gather x1, blocking collectives, per_device(): row0 = lax.all_gather(to_near, 'lat', axis_index_groups=partners(n_lat))  4.42 us
    pallas_call x7, Pallas kernels, call(): pl.pallas_call(kernel, out_shape=[s if hasattr(s, 'dtype') else jax.Shape...  3.83 us
    ppermute x1, starting transfers between devices, per_device(): row1 = lax.ppermute(to_far, 'lat', pairs(n_lat, 1, 2))  1.92 us
    ppermute x1, waiting for transfers between devices, per_device(): to_late = lax.ppermute(to_far, 'lon', [(j, i) for i, j in sent])  1.39 us
    ppermute x1, starting transfers between devices, per_device(): to_early = lax.ppermute(to_far, 'lon', sent)  1.29 us
  transfers between devices with their start and end apart: 5, of which 1 were waited for; matrix products, arithmetic and copies ran while one was open for 0% of the time, Pallas kernels for 3%

profile of v10, /device:TPU:24, one launch (start us, length us, event | category | flops | bytes accessed | tf_op | source)
XLA Modules:
  0.0 35.7 jit_solution(16624574064425624917)
XLA Ops:
  0.6 1.3 %shard_map.95 = (f32[32,128]{1,0:T(8,128)S(1)}, f32[32,128]{1,0:T(8,128)S(1)}, f32[16,128]{1,0:T(8,128)S(1)}, f32[16,128]{1,0:T(8,128)S(1)}, f32[12,16,128]{2,1,...) custom-call(f32[12,16,128]{2,1,0:T(8,128)} %bitcast.14, ...), custom_call_target="tpu_custom_call" | custom-call | tf_op jit(solution)/shard_map/pallas_call | solution.py:482
  2.0 6.1 %collective-permute-start = (f32[32,128]{1,0:T(8,128)S(1)}, f32[32,128]{1,0:T(8,128)S(1)}, u32[]{:S(2)}, u32[]{:S(2)}) collective-permute-start(f32[32,128]{1,0:T(8,128)S(1)} %get-tuple-element.41), channel_id=1, source_target_pairs={{0,1},{1,0},{4,5},{5,4},{8,9},{9,8},{12,13},{13,12},{16,17},{17,16... | collective-permute-start | bytes 49160 | tf_op jit(solution)/shard_map/ppermute | solution.py:522
  8.1 1.3 %collective-permute-start.2 = (f32[32,128]{1,0:T(8,128)S(1)}, f32[32,128]{1,0:T(8,128)S(1)}, u32[]{:S(2)}, u32[]{:S(2)}) collective-permute-start(f32[32,128]{1,0:T(8,128)S(1)} %get-tuple-element.42), channel_id=1, source_target_pairs={{2,1},{3,4},{6,5},{7,8},{10,9},{11,12},{14,13},{15,0},{18,17},{19,... | collective-permute-start | bytes 49160 | tf_op jit(solution)/shard_map/ppermute | solution.py:521
  9.4 0.7 %collective-permute-start.1 = (f32[32,128]{1,0:T(8,128)S(1)}, f32[32,128]{1,0:T(8,128)S(1)}, u32[]{:S(2)}, u32[]{:S(2)}) collective-permute-start(f32[32,128]{1,0:T(8,128)S(1)} %get-tuple-element.41), channel_id=1, source_target_pairs={{2,3},{3,2},{6,7},{7,6},{10,11},{11,10},{14,15},{15,14},{18,19},{1... | collective-permute-start | bytes 49160 | tf_op jit(solution)/shard_map/ppermute | solution.py:524
  10.0 10.1 %collective-permute-start.3 = (f32[32,128]{1,0:T(8,128)S(1)}, f32[32,128]{1,0:T(8,128)S(1)}, u32[]{:S(2)}, u32[]{:S(2)}) collective-permute-start(f32[32,128]{1,0:T(8,128)S(1)} %get-tuple-element.42), channel_id=1, source_target_pairs={{1,2},{4,3},{5,6},{8,7},{9,10},{12,11},{13,14},{0,15},{17,18},{20,... | collective-permute-start | bytes 49160 | tf_op jit(solution)/shard_map/ppermute | solution.py:523
  20.1 0.0 collective-permute-done.early.near
  20.1 0.0 collective-permute-done.2.to_early.far
  20.2 0.0 collective-permute-done.1.late.near
  20.2 1.4 %collective-permute-done.3.to_late.far = f32[32,128]{1,0:T(8,128)S(1)} collective-permute-done((f32[32,128]{1,0:T(8,128)S(1)}, f32[32,128]{1,0:T(8,128)S(1)}, u32[]{:S(2)}, u32[]{:S(2)}) %collective-permute-start.3) | collective-permute-done | bytes 16416 | tf_op jit(solution)/shard_map/ppermute | solution.py:523
  21.6 1.9 %collective-permute-start.4 = (f32[104,128]{1,0:T(8,128)S(1)}, f32[104,128]{1,0:T(8,128)S(1)}, u32[]{:S(2)}, u32[]{:S(2)}) collective-permute-start(f32[104,128]{1,0:T(8,128)S(1)} %get-tuple-element.45), channel_id=1, source_target_pairs={{16,32},{32,16},{48,64},{64,48},{80,96},{96,80},{112,128},{128,112... | collective-permute-start | bytes 159752 | tf_op jit(solution)/shard_map/ppermute | solution.py:531
  23.5 0.4 %shard_map.97 = (f32[12,16,128]{2,1,0:T(8,128)S(1)}, f32[12,16,128]{2,1,0:T(8,128)S(1)}, f32[16,128]{1,0:T(8,128)S(1)}) custom-call(f32[2,16,128]{2,1,0:T(8,128)S(1)} %get-tuple-element.46.prev, f32[11,16,128]{2,1,0:T(8,128)S(1)} %get-tuple-element.36.mix, s32[4,16,128]{2,1,0:T(8,128)S(1)} %get-tuple-element.39.index, f32[4,16,128]{2,1,0:T(8,128)S(1)} %get-tuple-element.40.weight), custom_call_target="tpu_custom_call" | custom-call | tf_op jit(solution)/shard_map/pallas_call | solution.py:482
  23.9 0.8 %shard_map.98 = (f32[12,16,128]{2,1,0:T(8,128)S(1)}, f32[12,16,128]{2,1,0:T(8,128)S(1)}, f32[11,16,128]{2,1,0:T(8,128)S(1)}, f32[12,16,128]{2,1,0:T(8,128)S(1)},...) custom-call(f32[12,16,128]{2,1,0:T(8,128)S(1)} %get-tuple-element.35.state, ...), custom_call_target="tpu_custom_call" | custom-call | tf_op jit(solution)/shard_map/pallas_call | solution.py:482
  24.8 4.4 %all-gather = f32[208,128]{1,0:T(8,128)S(1)} all-gather(f32[104,128]{1,0:T(8,128)S(1)} %get-tuple-element.44), channel_id=2, replica_groups={{0,16},{32,48},{64,80},{96,112},{128,144},{160,176},{192,208},{224,240}..., dimensions={0}, use_global_device_ids=true | all-gather | bytes 159744 | tf_op jit(solution)/shard_map/all_gather | solution.py:532
  29.2 0.0 collective-permute-done.4.row1
  29.2 0.1 shard_map.100
  29.3 5.2 %all-gather.1 = f32[192,128]{1,0:T(8,128)S(1)} all-gather(f32[96,128]{1,0:T(8,128)S(1)} %get-tuple-element.65), channel_id=3, replica_groups=mesh['comp'=2,'lat'=16,'lon'=16] {'comp'}, dimensions={0}, use_global_device_ids=true | all-gather | bytes 147456 | tf_op jit(solution)/shard_map/all_gather | solution.py:548
  34.6 1.1 %shard_map.101 = (f32[12,16,128]{2,1,0:T(8,128)}, f32[2,16,128]{2,1,0:T(8,128)}) custom-call(f32[12,16,128]{2,1,0:T(8,128)S(1)} %get-tuple-element.35.state, f32[11,16,128]{2,1,0:T(8,128)S(1)} %get-tuple-element.36.mix, f32[2,16,128]{2,1,0:T(8,128)S(1)} %get-tuple-element.37.vel, f32[16,128]{1,0:T(8,128)S(1)} %get-tuple-element.38.rate_in.rate, ...), custom_call_target="tpu_custom_call" | custom-call | tf_op jit(solution)/shard_map/pallas_call | solution.py:482
  (2 shorter events, 0.1 us)
Async XLA Ops:
  2.0 18.2 %collective-permute-start = (f32[32,128]{1,0:T(8,128)S(1)}, f32[32,128]{1,0:T(8,128)S(1)}, u32[]{:S(2)}, u32[]{:S(2)}) collective-permute-start(f32[32,128]{1,0:T(8,128)S(1)} %get-tuple-element.41), channel_id=1, source_target_pairs={{0,1},{1,0},{4,5},{5,4},{8,9},{9,8},{12,13},{13,12},{16,17},{17,16... | collective-permute-start | bytes 49160 | tf_op jit(solution)/shard_map/ppermute | solution.py:522
  8.1 12.1 %collective-permute-start.2 = (f32[32,128]{1,0:T(8,128)S(1)}, f32[32,128]{1,0:T(8,128)S(1)}, u32[]{:S(2)}, u32[]{:S(2)}) collective-permute-start(f32[32,128]{1,0:T(8,128)S(1)} %get-tuple-element.42), channel_id=1, source_target_pairs={{2,1},{3,4},{6,5},{7,8},{10,9},{11,12},{14,13},{15,0},{18,17},{19,... | collective-permute-start | bytes 49160 | tf_op jit(solution)/shard_map/ppermute | solution.py:521
  9.4 10.8 %collective-permute-start.1 = (f32[32,128]{1,0:T(8,128)S(1)}, f32[32,128]{1,0:T(8,128)S(1)}, u32[]{:S(2)}, u32[]{:S(2)}) collective-permute-start(f32[32,128]{1,0:T(8,128)S(1)} %get-tuple-element.41), channel_id=1, source_target_pairs={{2,3},{3,2},{6,7},{7,6},{10,11},{11,10},{14,15},{15,14},{18,19},{1... | collective-permute-start | bytes 49160 | tf_op jit(solution)/shard_map/ppermute | solution.py:524
  10.0 11.5 %collective-permute-start.3 = (f32[32,128]{1,0:T(8,128)S(1)}, f32[32,128]{1,0:T(8,128)S(1)}, u32[]{:S(2)}, u32[]{:S(2)}) collective-permute-start(f32[32,128]{1,0:T(8,128)S(1)} %get-tuple-element.42), channel_id=1, source_target_pairs={{1,2},{4,3},{5,6},{8,7},{9,10},{12,11},{13,14},{0,15},{17,18},{20,... | collective-permute-start | bytes 49160 | tf_op jit(solution)/shard_map/ppermute | solution.py:523
  21.6 7.6 %collective-permute-start.4 = (f32[104,128]{1,0:T(8,128)S(1)}, f32[104,128]{1,0:T(8,128)S(1)}, u32[]{:S(2)}, u32[]{:S(2)}) collective-permute-start(f32[104,128]{1,0:T(8,128)S(1)} %get-tuple-element.45), channel_id=1, source_target_pairs={{16,32},{32,16},{48,64},{64,48},{80,96},{96,80},{112,128},{128,112... | collective-permute-start | bytes 159752 | tf_op jit(solution)/shard_map/ppermute | solution.py:531

commit v11 on v10

--- a/solution.py
+++ b/solution.py
@@ -269,7 +269,7 @@
 IMPULSE = [1.0] + [None] * (LEV - 1)
 
 
-def prepare_own_kernel(prev, mix, index, weight, inverse, unit, seen):
+def prepare_own(prev, mix, index, weight, inverse, unit, seen):
     own_mix = [mix[level] for level in range(LEV - 1)]
     inverses, ratios = factors(own_mix)
     impulse = solve(IMPULSE, own_mix, inverses, ratios)
@@ -280,6 +280,18 @@
     @pl.when(lax.axis_index("comp") == 0)
     def _():
         seen[...] = regrid_tile(prev[1], index, weight)
+
+
+def own_early_kernel(*refs):
+    @pl.when(starts_early())
+    def _():
+        prepare_own(*refs)
+
+
+def own_late_kernel(prev, mix, index, weight, *both):
+    @pl.when(jnp.logical_not(starts_early()))
+    def _():
+        prepare_own(prev, mix, index, weight, *both[len(both) // 2 :])
 
 
 def prepare_side(
@@ -401,16 +413,12 @@
     def _():
         top_step(state, mix, vel, rate, flux, columns, rows, inverse, unit, seen, lon_own, fluxes)
 
-    @pl.when(lax.axis_index("comp") != 0)
-    def _():
-        halo_step(state, mix, vel, columns, rows, inverse, side, before, before_side, unit_rim)
+    halo_step(state, mix, vel, columns, rows, inverse, side, before, before_side, unit_rim)
 
 
 def second_step_kernel(
-    state, mix, vel, rate_in, index, weight, early, late, to_early, to_late, row0, row1,
-    inverse, unit, inverse_side, side_mix, side_state, lon_own, lon_side, unit_side,
-    given_before, given_side, given_rim, got,
-    new_state, series, own_before, own_side, own_rim,
+    mix, vel, rate_in, index, weight, early, late, to_early, to_late, row0, row1,
+    inverse, unit, unit_side, before, before_side, unit_rim, got, new_state, series,
 ):
     columns, rows = (early, late, to_early, to_late), (row0, row1)
     sub = sublanes()
@@ -418,7 +426,7 @@
     tables = [got[0, k * ROWS : (k + 1) * ROWS] for k in range(6)]
     own_mix = [mix[level] for level in range(LEV - 1)]
 
-    def advance(force, force_rim, force_side, force1, before, before_side, unit_rim):
+    def advance(force, force_rim, force_side, force1):
         weights = transport_weights(vel[0], vel[1])
         moved = []
         for level in range(LEV):
@@ -438,11 +446,9 @@
 
     @pl.when(lax.axis_index("comp") == 0)
     def _():
-        side = (inverse_side, side_mix, side_state, lon_own, lon_side)
-        halo_step(state, mix, vel, columns, rows, inverse, side, own_before, own_side, own_rim)
         rim = jnp.where(sub < 4, tables[4][0:8], tables[3][8:16])
         side = jnp.where(lane < 64, tables[2], tables[1])
-        advance(tables[0], rim, side, tables[5], own_before, own_side, own_rim)
+        advance(tables[0], rim, side, tables[5])
         series[0] = tables[0]
         series[1] = tables[5]
 
@@ -473,7 +479,7 @@
         )
         force = rate * regrid_tile(tables[0], index, weight)
         force1 = rate * regrid_tile(tables[5], index, weight)
-        top, last = advance(force, rim, side, force1, given_before, given_side, given_rim)
+        top, last = advance(force, rim, side, force1)
         series[0] = top
         series[1] = last
 
@@ -520,6 +526,9 @@
     sent = [((i, (i + 1) % n_lon) if i % 4 == 3 else (i + 1, i)) for i in joints]
     to_early = lax.ppermute(to_far, "lon", sent)
     early = lax.ppermute(to_near, "lon", pairs(n_lon, 0, 4))
+    narrow = (LEV, ROWS, COLS)
+    own_shapes = [narrow, narrow, tile]
+    own = call(own_early_kernel, own_shapes, prev, mix, index, weight)
     to_late = lax.ppermute(to_far, "lon", [(j, i) for i, j in sent])
     late = lax.ppermute(to_near, "lon", pairs(n_lon, 2, 4))
     columns = (early, late, to_early, to_late)
@@ -531,9 +540,11 @@
     row1 = lax.ppermute(to_far, "lat", pairs(n_lat, 1, 2))
     row0 = lax.all_gather(to_near, "lat", axis_index_groups=partners(n_lat))
     rows = (row0, row1)
-    narrow = (LEV, ROWS, COLS)
     parts = [(LEV, 24, COLS), narrow, (LEV, 8, COLS)]
-    inverse, unit, seen = call(prepare_own_kernel, [narrow, narrow, tile], prev, mix, index, weight)
+    inverse, unit, seen = call(
+        own_late_kernel, own_shapes, prev, mix, index, weight, *own,
+        aliases={4 + k: k for k in range(len(own_shapes))},
+    )
     shapes = [narrow, narrow, (LEV - 1, ROWS, COLS), narrow, narrow, narrow]
     side = call(side_early_kernel, shapes, state, vel, early, to_early)
     inverse_side, unit_side, *side = call(
@@ -548,9 +559,7 @@
     got = lax.all_gather(fluxes, "comp")
     new_state, series = call(
         second_step_kernel, [narrow, (NSTEP, ROWS, COLS)],
-        state, mix, vel, rate, index, weight, *columns, *rows,
-        inverse, unit, *known, unit_side, *before, got,
-        scratch=[pltpu.VMEM(shape, jnp.float32) for shape in parts],
+        mix, vel, rate, index, weight, *columns, *rows, inverse, unit, unit_side, *before, got,
     )
     return new_state[None], series[None]
 

time: 35.9 us -> 35.9 us (level)
  the two profiles are of different devices: /device:TPU:24 before, /device:TPU:88 now
where the time goes in v11:
time: 35.9 us; the launch traced here: 35.6 us
  starting transfers between devices  20.1 us (56%)
  blocking collectives  9.18 us (26%)
  Pallas kernels  4.24 us (12%)
  waiting for transfers between devices  1.4 us (4%)
  between operations  0.75 us (2%)
    ppermute x1, starting transfers between devices, per_device(): to_late = lax.ppermute(to_far, 'lon', [(j, i) for i, j in sent])  10.1 us
    ppermute x1, starting transfers between devices, per_device(): early = lax.ppermute(to_near, 'lon', pairs(n_lon, 0, 4))  6.09 us
    all_gather x1, blocking collectives, per_device(): got = lax.all_gather(fluxes, 'comp')  4.76 us
    all_gather x1, blocking collectives, per_device(): row0 = lax.all_gather(to_near, 'lat', axis_index_groups=partners(n_lat))  4.42 us
    pallas_call x8, Pallas kernels, call(): pl.pallas_call(kernel, out_shape=[s if hasattr(s, 'dtype') else jax.Shape...  4.24 us
    ppermute x1, starting transfers between devices, per_device(): row1 = lax.ppermute(to_far, 'lat', pairs(n_lat, 1, 2))  1.92 us
    ppermute x1, waiting for transfers between devices, per_device(): to_late = lax.ppermute(to_far, 'lon', [(j, i) for i, j in sent])  1.39 us
    ppermute x1, starting transfers between devices, per_device(): to_early = lax.ppermute(to_far, 'lon', sent)  1.29 us
  transfers between devices with their start and end apart: 5, of which 1 were waited for; matrix products, arithmetic and copies ran while one was open for 0% of the time, Pallas kernels for 3%

profile of v11, /device:TPU:88, one launch (start us, length us, event | category | flops | bytes accessed | tf_op | source)
XLA Modules:
  0.0 35.6 jit_solution(4593027556301551432)
XLA Ops:
  0.6 1.3 %shard_map.95 = (f32[32,128]{1,0:T(8,128)S(1)}, f32[32,128]{1,0:T(8,128)S(1)}, f32[16,128]{1,0:T(8,128)S(1)}, f32[16,128]{1,0:T(8,128)S(1)}, f32[12,16,128]{2,1,...) custom-call(f32[12,16,128]{2,1,0:T(8,128)} %bitcast.14, ...), custom_call_target="tpu_custom_call" | custom-call | tf_op jit(solution)/shard_map/pallas_call | solution.py:488
  1.9 6.1 %collective-permute-start = (f32[32,128]{1,0:T(8,128)S(1)}, f32[32,128]{1,0:T(8,128)S(1)}, u32[]{:S(2)}, u32[]{:S(2)}) collective-permute-start(f32[32,128]{1,0:T(8,128)S(1)} %get-tuple-element.43), channel_id=1, source_target_pairs={{0,1},{1,0},{4,5},{5,4},{8,9},{9,8},{12,13},{13,12},{16,17},{17,16... | collective-permute-start | bytes 49160 | tf_op jit(solution)/shard_map/ppermute | solution.py:528
  8.0 1.3 %collective-permute-start.2 = (f32[32,128]{1,0:T(8,128)S(1)}, f32[32,128]{1,0:T(8,128)S(1)}, u32[]{:S(2)}, u32[]{:S(2)}) collective-permute-start(f32[32,128]{1,0:T(8,128)S(1)} %get-tuple-element.44), channel_id=1, source_target_pairs={{2,1},{3,4},{6,5},{7,8},{10,9},{11,12},{14,13},{15,0},{18,17},{19,... | collective-permute-start | bytes 49160 | tf_op jit(solution)/shard_map/ppermute | solution.py:527
  9.3 0.7 %collective-permute-start.1 = (f32[32,128]{1,0:T(8,128)S(1)}, f32[32,128]{1,0:T(8,128)S(1)}, u32[]{:S(2)}, u32[]{:S(2)}) collective-permute-start(f32[32,128]{1,0:T(8,128)S(1)} %get-tuple-element.43), channel_id=1, source_target_pairs={{2,3},{3,2},{6,7},{7,6},{10,11},{11,10},{14,15},{15,14},{18,19},{1... | collective-permute-start | bytes 49160 | tf_op jit(solution)/shard_map/ppermute | solution.py:533
  10.0 10.1 %collective-permute-start.3 = (f32[32,128]{1,0:T(8,128)S(1)}, f32[32,128]{1,0:T(8,128)S(1)}, u32[]{:S(2)}, u32[]{:S(2)}) collective-permute-start(f32[32,128]{1,0:T(8,128)S(1)} %get-tuple-element.44), channel_id=1, source_target_pairs={{1,2},{4,3},{5,6},{8,7},{9,10},{12,11},{13,14},{0,15},{17,18},{20,... | collective-permute-start | bytes 49160 | tf_op jit(solution)/shard_map/ppermute | solution.py:532
  20.1 0.0 collective-permute-done.early.near
  20.1 0.0 collective-permute-done.2.to_early.far
  20.1 0.0 collective-permute-done.1.late.near
  20.1 1.4 %collective-permute-done.3.to_late.far = f32[32,128]{1,0:T(8,128)S(1)} collective-permute-done((f32[32,128]{1,0:T(8,128)S(1)}, f32[32,128]{1,0:T(8,128)S(1)}, u32[]{:S(2)}, u32[]{:S(2)}) %collective-permute-start.3) | collective-permute-done | bytes 16416 | tf_op jit(solution)/shard_map/ppermute | solution.py:532
  21.6 1.9 %collective-permute-start.4 = (f32[104,128]{1,0:T(8,128)S(1)}, f32[104,128]{1,0:T(8,128)S(1)}, u32[]{:S(2)}, u32[]{:S(2)}) collective-permute-start(f32[104,128]{1,0:T(8,128)S(1)} %get-tuple-element.48), channel_id=1, source_target_pairs={{16,32},{32,16},{48,64},{64,48},{80,96},{96,80},{112,128},{128,112... | collective-permute-start | bytes 159752 | tf_op jit(solution)/shard_map/ppermute | solution.py:540
  23.5 0.2 shard_map.97
  23.7 0.8 %shard_map.99 = (f32[12,16,128]{2,1,0:T(8,128)S(1)}, f32[12,16,128]{2,1,0:T(8,128)S(1)}, f32[11,16,128]{2,1,0:T(8,128)S(1)}, f32[12,16,128]{2,1,0:T(8,128)S(1)},...) custom-call(f32[12,16,128]{2,1,0:T(8,128)S(1)} %get-tuple-element.45.state, ...), custom_call_target="tpu_custom_call" | custom-call | tf_op jit(solution)/shard_map/pallas_call | solution.py:488
  24.6 4.4 %all-gather = f32[208,128]{1,0:T(8,128)S(1)} all-gather(f32[104,128]{1,0:T(8,128)S(1)} %get-tuple-element.47), channel_id=2, replica_groups={{0,16},{32,48},{64,80},{96,112},{128,144},{160,176},{192,208},{224,240}..., dimensions={0}, use_global_device_ids=true | all-gather | bytes 159744 | tf_op jit(solution)/shard_map/all_gather | solution.py:541
  29.0 0.0 collective-permute-done.4.row1
  29.0 0.3 shard_map.101
  29.3 4.8 %all-gather.1 = f32[192,128]{1,0:T(8,128)S(1)} all-gather(f32[96,128]{1,0:T(8,128)S(1)} %get-tuple-element.71), channel_id=3, replica_groups=mesh['comp'=2,'lat'=16,'lon'=16] {'comp'}, dimensions={0}, use_global_device_ids=true | all-gather | bytes 147456 | tf_op jit(solution)/shard_map/all_gather | solution.py:559
  34.1 1.6 %shard_map.102 = (f32[12,16,128]{2,1,0:T(8,128)}, f32[2,16,128]{2,1,0:T(8,128)}) custom-call(f32[11,16,128]{2,1,0:T(8,128)S(1)} %get-tuple-element.38.mix.refs_1_, f32[2,16,128]{2,1,0:T(8,128)S(1)} %get-tuple-element.39.vel, f32[16,128]{1,0:T(8,128)S(1)} %get-tuple-element.40.rate_in.rate, s32[4,16,128]{2,1,0:T(8,128)S(1)} %get-tuple-element.41.index.refs_2_, ...), custom_call_target="tpu_custom_call" | custom-call | tf_op jit(solution)/shard_map/pallas_call | solution.py:488
  (3 shorter events, 0.1 us)
Async XLA Ops:
  1.9 18.2 %collective-permute-start = (f32[32,128]{1,0:T(8,128)S(1)}, f32[32,128]{1,0:T(8,128)S(1)}, u32[]{:S(2)}, u32[]{:S(2)}) collective-permute-start(f32[32,128]{1,0:T(8,128)S(1)} %get-tuple-element.43), channel_id=1, source_target_pairs={{0,1},{1,0},{4,5},{5,4},{8,9},{9,8},{12,13},{13,12},{16,17},{17,16... | collective-permute-start | bytes 49160 | tf_op jit(solution)/shard_map/ppermute | solution.py:528
  8.0 12.1 %collective-permute-start.2 = (f32[32,128]{1,0:T(8,128)S(1)}, f32[32,128]{1,0:T(8,128)S(1)}, u32[]{:S(2)}, u32[]{:S(2)}) collective-permute-start(f32[32,128]{1,0:T(8,128)S(1)} %get-tuple-element.44), channel_id=1, source_target_pairs={{2,1},{3,4},{6,5},{7,8},{10,9},{11,12},{14,13},{15,0},{18,17},{19,... | collective-permute-start | bytes 49160 | tf_op jit(solution)/shard_map/ppermute | solution.py:527
  9.3 10.8 %collective-permute-start.1 = (f32[32,128]{1,0:T(8,128)S(1)}, f32[32,128]{1,0:T(8,128)S(1)}, u32[]{:S(2)}, u32[]{:S(2)}) collective-permute-start(f32[32,128]{1,0:T(8,128)S(1)} %get-tuple-element.43), channel_id=1, source_target_pairs={{2,3},{3,2},{6,7},{7,6},{10,11},{11,10},{14,15},{15,14},{18,19},{1... | collective-permute-start | bytes 49160 | tf_op jit(solution)/shard_map/ppermute | solution.py:533
  10.0 11.5 %collective-permute-start.3 = (f32[32,128]{1,0:T(8,128)S(1)}, f32[32,128]{1,0:T(8,128)S(1)}, u32[]{:S(2)}, u32[]{:S(2)}) collective-permute-start(f32[32,128]{1,0:T(8,128)S(1)} %get-tuple-element.44), channel_id=1, source_target_pairs={{1,2},{4,3},{5,6},{8,7},{9,10},{12,11},{13,14},{0,15},{17,18},{20,... | collective-permute-start | bytes 49160 | tf_op jit(solution)/shard_map/ppermute | solution.py:532
  21.6 7.4 %collective-permute-start.4 = (f32[104,128]{1,0:T(8,128)S(1)}, f32[104,128]{1,0:T(8,128)S(1)}, u32[]{:S(2)}, u32[]{:S(2)}) collective-permute-start(f32[104,128]{1,0:T(8,128)S(1)} %get-tuple-element.48), channel_id=1, source_target_pairs={{16,32},{32,16},{48,64},{64,48},{80,96},{96,80},{112,128},{128,112... | collective-permute-start | bytes 159752 | tf_op jit(solution)/shard_map/ppermute | solution.py:540
